TPU v7x, 32 devices: a whole 2x2x4 slice. The times are simulated.
32 devices in a mesh: rep: 4 (over x, core), fsdp: 8 (over z, y).
Axes of the slice: x: 2, y: 2, z: 4, core: 2. Of those that a mesh axis runs over, the one named last changes fastest.
Arguments:
- inputs: bfloat16 [32, 512, 1536], P(('rep', 'fsdp')), may hold values from -6 to 6
- cotangent: bfloat16 [32, 512, 1536], P(('rep', 'fsdp')), may hold values from -6 to 6
- lengths: int32 [32], P(('rep', 'fsdp')), may hold values from 128 to 512, as said below
- choices: int32 [32, 512, 8], P(('rep', 'fsdp')), may hold values from 0 to 15, all different within a row
- gain_attn: bfloat16 [1536], P('fsdp'), may hold values from 0.099609375 to 1.8984375
- gain_moe: bfloat16 [1536], P('fsdp'), may hold values from 0.099609375 to 1.8984375
- query_weight: bfloat16 [1536, 1536], P('fsdp'), may hold values from -0.15625 to 0.15625
- key_weight: bfloat16 [1536, 512], P('fsdp'), may hold values from -0.15625 to 0.15625
- value_weight: bfloat16 [1536, 512], P('fsdp'), may hold values from -0.15625 to 0.15625
- w_out: bfloat16 [1536, 1536], P('fsdp'), may hold values from -0.625 to 0.625
- w_router: bfloat16 [1536, 16], P('fsdp'), may hold values from -0.078125 to 0.078125
- w_gate: bfloat16 [16, 1536, 512], P('fsdp'), may hold values from -0.15625 to 0.15625
- w_up: bfloat16 [16, 1536, 512], P('fsdp'), may hold values from -0.15625 to 0.15625
- w_down: bfloat16 [16, 512, 1536], P('fsdp'), may hold values from -0.75 to 0.75
Outputs:
- output: bfloat16 [32, 512, 1536], P(('rep', 'fsdp'))
- grad_input: bfloat16 [32, 512, 1536], P(('rep', 'fsdp'))
- grad_gain_attn: float32 [1536], P('fsdp')
- grad_gain_moe: float32 [1536], P('fsdp')
- grad_query: float32 [1536, 1536], P('fsdp')
- grad_key: float32 [1536, 512], P('fsdp')
- grad_value: float32 [1536, 512], P('fsdp')
- grad_out: float32 [1536, 1536], P('fsdp')
- grad_router: float32 [1536, 16], P('fsdp')
- grad_gate: float32 [16, 1536, 512], P('fsdp')
- grad_up: float32 [16, 1536, 512], P('fsdp')
- grad_down: float32 [16, 512, 1536], P('fsdp')
Inputs may be any that keep to these rules, and one draw needn't show every extreme that they name: `lengths`: valid tokens of each sequence of 512 slots, from its start; some sequence is full. `choices`: a token's 8 experts are distinct; those of padding tokens are ignored.
All inputs are finite; a program needn't handle non-finite values.
Results may differ from a plain program's by a relative error of at most 0.023.
Values may be sent and summed in bfloat16 or wider, within the bound.
No kernel may reach another device: no remote copies, remote signals or barrier semaphores. Data moves between devices by JAX's collectives and lax.ppermute only.
A program may use at most 320 MiB of HBM per device.

v0:
```python
import math

import jax
import jax.numpy as jnp
from jax import lax
from jax.sharding import PartitionSpec as P

QUERY_HEADS = 24
KEY_VALUE_HEADS = 8
HEAD_SIZE = 64


def rms_scale(value_rows, gain_vec):
    inverse = lax.rsqrt(jnp.mean(value_rows * value_rows, axis=-1, keepdims=True) + 1e-05)
    return value_rows * inverse * gain_vec


def swiglu(gate_part, up_part):
    return jax.nn.silu(gate_part) * up_part


def rotation(expert_slot_count, head_dim):
    half_dim = head_dim // 2
    frequency = jnp.exp(
        -jnp.log(10000.0) * 2.0 * jnp.arange(half_dim, dtype=jnp.float32) / head_dim
    )
    angles = jnp.arange(expert_slot_count, dtype=jnp.float32)[:, None] * frequency[None, :]
    return (jnp.cos(angles), jnp.sin(angles))


def rotary_apply(value_rows, cosine_table, sine_table):
    half_dim = value_rows.shape[-1] // 2
    extra_dims = (1,) * (value_rows.ndim - 2)
    cosine_table = cosine_table.reshape(
        cosine_table.shape[:1] + extra_dims + cosine_table.shape[1:]
    )
    sine_table = sine_table.reshape(sine_table.shape[:1] + extra_dims + sine_table.shape[1:])
    first_half = value_rows[..., :half_dim]
    second = value_rows[..., half_dim:]
    return jnp.concatenate(
        [
            first_half * cosine_table - second * sine_table,
            second * cosine_table + first_half * sine_table,
        ],
        axis=-1,
    )


def route_pairs(choices_row, length, experts, capacity):
    expert_slot_count, top_count = choices_row.shape
    valid_rows = jnp.arange(expert_slot_count, dtype=jnp.int32) < length
    marks_hit = (
        choices_row[:, :, None] == jnp.arange(experts, dtype=jnp.int32)[None, None, :]
    ) & valid_rows[:, None, None]
    marks_hit = marks_hit.astype(jnp.int32).reshape(expert_slot_count * top_count, experts)
    before = jnp.cumsum(marks_hit, axis=0) - marks_hit
    position = jnp.sum(before * marks_hit, axis=1).reshape(expert_slot_count, top_count)
    kept_pairs = valid_rows[:, None] & (position < capacity)
    slot_index = jnp.where(kept_pairs, choices_row * capacity + position, experts * capacity)
    token_ids = jnp.repeat(jnp.arange(expert_slot_count, dtype=jnp.int32), top_count)
    source_token = (
        jnp.full((experts * capacity,), expert_slot_count, jnp.int32)
        .at[slot_index.reshape(-1)]
        .set(token_ids, mode="drop")
    )
    return (kept_pairs, slot_index, source_token)


def expert_front(received, w_gate, w_up, w_down):
    gate_part = jnp.einsum("necd,edf->necf", received, w_gate, preferred_element_type=jnp.float32)
    up_part = jnp.einsum("necd,edf->necf", received, w_up, preferred_element_type=jnp.float32)
    inner = swiglu(gate_part, up_part).astype(jnp.bfloat16)
    expert_out = jnp.einsum(
        "necf,efd->necd", inner, w_down, preferred_element_type=jnp.float32
    ).astype(jnp.bfloat16)
    return (gate_part, up_part, inner, expert_out)


def expert_rear(received, gate_part, up_part, inner, grad_recv, w_gate, w_up, w_down):
    grad_down = jnp.einsum("necf,necd->efd", inner, grad_recv, preferred_element_type=jnp.float32)
    grad_inner = jnp.einsum("necd,efd->necf", grad_recv, w_down, preferred_element_type=jnp.float32)
    unused_value, swiglu_pull = jax.vjp(swiglu, gate_part, up_part)
    grad_gate_float, grad_up_float = swiglu_pull(grad_inner)
    grad_gate_part = grad_gate_float.astype(jnp.bfloat16)
    grad_up_part = grad_up_float.astype(jnp.bfloat16)
    grad_gate = jnp.einsum(
        "necd,necf->edf", received, grad_gate_part, preferred_element_type=jnp.float32
    )
    grad_up = jnp.einsum(
        "necd,necf->edf", received, grad_up_part, preferred_element_type=jnp.float32
    )
    grad_rows = jnp.einsum(
        "necf,edf->necd", grad_gate_part, w_gate, preferred_element_type=jnp.float32
    )
    grad_rows = grad_rows + jnp.einsum(
        "necf,edf->necd", grad_up_part, w_up, preferred_element_type=jnp.float32
    )
    return (grad_gate, grad_up, grad_down, grad_rows.astype(jnp.bfloat16))


def body(
    inputs,
    cotangent,
    lengths,
    choices,
    gain_attn,
    gain_moe,
    query_weight,
    key_weight,
    value_weight,
    w_out,
    w_router,
    w_gate,
    w_up,
    w_down,
):
    groups = lax.axis_size("fsdp")
    tokens = inputs[0].astype(jnp.float32)
    expert_slot_count, width = tokens.shape
    length = lengths[0]
    choices_row = choices[0]
    top_count = choices_row.shape[1]
    local_experts = w_gate.shape[0]
    experts = local_experts * groups
    capacity = 25 * expert_slot_count * top_count // (32 * experts)
    query_group_width = QUERY_HEADS // KEY_VALUE_HEADS
    scale_factor = 1.0 / math.sqrt(HEAD_SIZE)
    cosine_table, sine_table = rotation(expert_slot_count, HEAD_SIZE)
    full_set = (
        lax.all_gather(gain_attn, "fsdp", axis=0, tiled=True),
        lax.all_gather(gain_moe, "fsdp", axis=0, tiled=True),
        lax.all_gather(query_weight, "fsdp", axis=0, tiled=True),
        lax.all_gather(key_weight, "fsdp", axis=0, tiled=True),
        lax.all_gather(value_weight, "fsdp", axis=0, tiled=True),
        lax.all_gather(w_out, "fsdp", axis=0, tiled=True),
        lax.all_gather(w_router, "fsdp", axis=0, tiled=True),
    )
    full_gain_attn, full_gain_moe, full_query, full_key, full_value, full_out, full_router = (
        full_set
    )
    normed_float, norm_one_pull = jax.vjp(rms_scale, tokens, full_gain_attn.astype(jnp.float32))
    attention_normed = normed_float.astype(jnp.bfloat16)
    query_rows = jnp.dot(attention_normed, full_query, preferred_element_type=jnp.float32).reshape(
        expert_slot_count, KEY_VALUE_HEADS, query_group_width, HEAD_SIZE
    )
    unrotated_keys = jnp.dot(
        attention_normed, full_key, preferred_element_type=jnp.float32
    ).reshape(expert_slot_count, KEY_VALUE_HEADS, HEAD_SIZE)
    value_rows = (
        jnp.dot(attention_normed, full_value, preferred_element_type=jnp.float32)
        .astype(jnp.bfloat16)
        .reshape(expert_slot_count, KEY_VALUE_HEADS, HEAD_SIZE)
    )
    rot_queries = rotary_apply(query_rows, cosine_table, sine_table).astype(jnp.bfloat16)
    rot_keys = rotary_apply(unrotated_keys, cosine_table, sine_table).astype(jnp.bfloat16)
    rows_index = jnp.arange(expert_slot_count, dtype=jnp.int32)
    allowed = (rows_index[None, :] <= rows_index[:, None]) & (rows_index[None, :] < length)

    def masked_scores():
        raw_scores = (
            jnp.einsum("qhgd,khd->hgqk", rot_queries, rot_keys, preferred_element_type=jnp.float32)
            * scale_factor
        )
        return jnp.where(allowed, raw_scores, -1e30)

    scores = masked_scores()
    log_total = jax.nn.logsumexp(scores, axis=-1, keepdims=True)
    probs_low = jnp.exp(scores - log_total).astype(jnp.bfloat16)
    mixed = jnp.einsum("hgqk,khd->qhgd", probs_low, value_rows, preferred_element_type=jnp.float32)
    mixed = mixed.astype(jnp.bfloat16).reshape(expert_slot_count, QUERY_HEADS * HEAD_SIZE)
    hidden = tokens + jnp.dot(mixed, full_out, preferred_element_type=jnp.float32)
    normed_float_two, norm_two_pull = jax.vjp(rms_scale, hidden, full_gain_moe.astype(jnp.float32))
    normed_two = normed_float_two.astype(jnp.bfloat16)
    logits = jnp.dot(normed_two, full_router, preferred_element_type=jnp.float32)
    gates = jax.nn.softmax(jnp.take_along_axis(logits, choices_row, axis=1), axis=-1)
    kept_pairs, slot_index, source_token = route_pairs(choices_row, length, experts, capacity)
    pair_weight = gates * kept_pairs
    valid_rows = (rows_index < length)[:, None]
    grad_y = jnp.where(valid_rows, cotangent[0].astype(jnp.float32), 0.0)
    send_rows = jnp.take(normed_two, source_token, axis=0, mode="fill", fill_value=0).reshape(
        groups, local_experts * capacity, width
    )
    slot_gate = (
        jnp.zeros((experts * capacity,), jnp.float32)
        .at[slot_index.reshape(-1)]
        .set(pair_weight.reshape(-1), mode="drop")
    )
    grad_send = (
        jnp.take(grad_y, source_token, axis=0, mode="fill", fill_value=0.0) * slot_gate[:, None]
    )
    grad_send = grad_send.astype(jnp.bfloat16).reshape(groups, local_experts * capacity, width)
    block_shape = (groups, local_experts, capacity, width)
    flat_shape = (groups, local_experts * capacity, width)
    received = lax.all_to_all(send_rows, "fsdp", split_axis=0, concat_axis=0, tiled=True).reshape(
        block_shape
    )
    gate_part, up_part, inner, expert_out = expert_front(received, w_gate, w_up, w_down)
    returned = lax.all_to_all(
        expert_out.reshape(flat_shape), "fsdp", split_axis=0, concat_axis=0, tiled=True
    )
    grad_recv = lax.all_to_all(grad_send, "fsdp", split_axis=0, concat_axis=0, tiled=True).reshape(
        block_shape
    )
    grad_gate, grad_up, grad_down, grad_rows = expert_rear(
        received, gate_part, up_part, inner, grad_recv, w_gate, w_up, w_down
    )
    grad_back = lax.all_to_all(
        grad_rows.reshape(flat_shape), "fsdp", split_axis=0, concat_axis=0, tiled=True
    )
    returned = returned.reshape(experts * capacity, width)
    grad_back = grad_back.reshape(experts * capacity, width)
    picked = jnp.take(returned, slot_index, axis=0, mode="fill", fill_value=0)
    mixture = jnp.sum(pair_weight[:, :, None] * picked, axis=1)
    output = jnp.where(valid_rows, hidden + mixture, 0.0).astype(jnp.bfloat16)
    grad_gates = kept_pairs * jnp.sum(grad_y[:, None, :] * picked, axis=-1)
    grad_chosen = gates * (grad_gates - jnp.sum(gates * grad_gates, axis=-1, keepdims=True))
    hit_table = (
        choices_row[:, :, None] == jnp.arange(experts, dtype=jnp.int32)[None, None, :]
    ).astype(jnp.float32)
    grad_logits = jnp.sum(hit_table * grad_chosen[:, :, None], axis=1).astype(jnp.bfloat16)
    full_set = (
        lax.all_gather(gain_attn, "fsdp", axis=0, tiled=True),
        lax.all_gather(gain_moe, "fsdp", axis=0, tiled=True),
        lax.all_gather(query_weight, "fsdp", axis=0, tiled=True),
        lax.all_gather(key_weight, "fsdp", axis=0, tiled=True),
        lax.all_gather(value_weight, "fsdp", axis=0, tiled=True),
        lax.all_gather(w_out, "fsdp", axis=0, tiled=True),
        lax.all_gather(w_router, "fsdp", axis=0, tiled=True),
    )
    full_gain_attn, full_gain_moe, full_query, full_key, full_value, full_out, full_router = (
        full_set
    )
    pair_grads = jnp.take(grad_back, slot_index, axis=0, mode="fill", fill_value=0)
    grad_normed_two = jnp.sum(pair_grads, axis=1, dtype=jnp.float32)
    grad_normed_two = grad_normed_two + jnp.einsum(
        "se,de->sd", grad_logits, full_router, preferred_element_type=jnp.float32
    )
    grad_router = jnp.einsum(
        "sd,se->de", normed_two, grad_logits, preferred_element_type=jnp.float32
    )
    grad_hidden_norm, grad_gain_moe = norm_two_pull(grad_normed_two)
    grad_hidden = grad_y + grad_hidden_norm
    grad_attn = grad_hidden.astype(jnp.bfloat16)
    grad_out = jnp.einsum("sa,sd->ad", mixed, grad_attn, preferred_element_type=jnp.float32)
    gradient_mixed_rows = jnp.einsum(
        "sd,ad->sa", grad_attn, full_out, preferred_element_type=jnp.float32
    )
    gradient_mixed_rows = gradient_mixed_rows.astype(jnp.bfloat16).reshape(
        expert_slot_count, KEY_VALUE_HEADS, query_group_width, HEAD_SIZE
    )
    scores = masked_scores()
    probs = jnp.exp(scores - log_total)
    probs_low = probs.astype(jnp.bfloat16)
    gradient_value_rows = jnp.einsum(
        "hgqk,qhgd->khd", probs_low, gradient_mixed_rows, preferred_element_type=jnp.float32
    )
    gradient_value_rows = gradient_value_rows.astype(jnp.bfloat16).reshape(
        expert_slot_count, KEY_VALUE_HEADS * HEAD_SIZE
    )
    grad_probs = jnp.einsum(
        "qhgd,khd->hgqk", gradient_mixed_rows, value_rows, preferred_element_type=jnp.float32
    )
    grad_scores = probs * (grad_probs - jnp.sum(probs * grad_probs, axis=-1, keepdims=True))
    grad_scores = grad_scores.astype(jnp.bfloat16)
    grad_rot_queries = (
        jnp.einsum("hgqk,khd->qhgd", grad_scores, rot_keys, preferred_element_type=jnp.float32)
        * scale_factor
    )
    gradient_rotated_keys = (
        jnp.einsum("hgqk,qhgd->khd", grad_scores, rot_queries, preferred_element_type=jnp.float32)
        * scale_factor
    )
    grad_queries = (
        rotary_apply(grad_rot_queries, cosine_table, -sine_table)
        .astype(jnp.bfloat16)
        .reshape(expert_slot_count, QUERY_HEADS * HEAD_SIZE)
    )
    grad_keys = (
        rotary_apply(gradient_rotated_keys, cosine_table, -sine_table)
        .astype(jnp.bfloat16)
        .reshape(expert_slot_count, KEY_VALUE_HEADS * HEAD_SIZE)
    )
    grad_query = jnp.einsum(
        "sd,sa->da", attention_normed, grad_queries, preferred_element_type=jnp.float32
    )
    grad_key = jnp.einsum(
        "sd,sa->da", attention_normed, grad_keys, preferred_element_type=jnp.float32
    )
    grad_value = jnp.einsum(
        "sd,sa->da", attention_normed, gradient_value_rows, preferred_element_type=jnp.float32
    )
    grad_normed_one = jnp.einsum(
        "sa,da->sd", grad_queries, full_query, preferred_element_type=jnp.float32
    )
    grad_normed_one = grad_normed_one + jnp.einsum(
        "sa,da->sd", grad_keys, full_key, preferred_element_type=jnp.float32
    )
    grad_normed_one = grad_normed_one + jnp.einsum(
        "sa,da->sd", gradient_value_rows, full_value, preferred_element_type=jnp.float32
    )
    grad_tokens_norm, grad_gain_attn = norm_one_pull(grad_normed_one)
    grad_input = (grad_hidden + grad_tokens_norm).astype(jnp.bfloat16)
    owned = (
        lax.psum_scatter(
            grad_gain_attn.astype(jnp.bfloat16), "fsdp", scatter_dimension=0, tiled=True
        ).astype(jnp.float32),
        lax.psum_scatter(
            grad_gain_moe.astype(jnp.bfloat16), "fsdp", scatter_dimension=0, tiled=True
        ).astype(jnp.float32),
        lax.psum_scatter(
            grad_query.astype(jnp.bfloat16), "fsdp", scatter_dimension=0, tiled=True
        ).astype(jnp.float32),
        lax.psum_scatter(
            grad_key.astype(jnp.bfloat16), "fsdp", scatter_dimension=0, tiled=True
        ).astype(jnp.float32),
        lax.psum_scatter(
            grad_value.astype(jnp.bfloat16), "fsdp", scatter_dimension=0, tiled=True
        ).astype(jnp.float32),
        lax.psum_scatter(
            grad_out.astype(jnp.bfloat16), "fsdp", scatter_dimension=0, tiled=True
        ).astype(jnp.float32),
        lax.psum_scatter(
            grad_router.astype(jnp.bfloat16), "fsdp", scatter_dimension=0, tiled=True
        ).astype(jnp.float32),
    )
    totals = (
        lax.psum(owned[0].astype(jnp.bfloat16), "rep").astype(jnp.float32),
        lax.psum(owned[1].astype(jnp.bfloat16), "rep").astype(jnp.float32),
        lax.psum(owned[2].astype(jnp.bfloat16), "rep").astype(jnp.float32),
        lax.psum(owned[3].astype(jnp.bfloat16), "rep").astype(jnp.float32),
        lax.psum(owned[4].astype(jnp.bfloat16), "rep").astype(jnp.float32),
        lax.psum(owned[5].astype(jnp.bfloat16), "rep").astype(jnp.float32),
        lax.psum(owned[6].astype(jnp.bfloat16), "rep").astype(jnp.float32),
        lax.psum(grad_gate.astype(jnp.bfloat16), "rep").astype(jnp.float32),
        lax.psum(grad_up.astype(jnp.bfloat16), "rep").astype(jnp.float32),
        lax.psum(grad_down.astype(jnp.bfloat16), "rep").astype(jnp.float32),
    )
    return (
        output[None],
        grad_input[None],
        totals[0],
        totals[1],
        totals[2],
        totals[3],
        totals[4],
        totals[5],
        totals[6],
        totals[7],
        totals[8],
        totals[9],
    )


def solution(mesh):
    in_specs = (
        P(("rep", "fsdp"), None, None),
        P(("rep", "fsdp"), None, None),
        P(("rep", "fsdp")),
        P(("rep", "fsdp"), None, None),
        P("fsdp"),
        P("fsdp"),
        P("fsdp", None),
        P("fsdp", None),
        P("fsdp", None),
        P("fsdp", None),
        P("fsdp", None),
        P("fsdp", None, None),
        P("fsdp", None, None),
        P("fsdp", None, None),
    )
    out_specs = (
        P(("rep", "fsdp"), None, None),
        P(("rep", "fsdp"), None, None),
        P("fsdp"),
        P("fsdp"),
        P("fsdp", None),
        P("fsdp", None),
        P("fsdp", None),
        P("fsdp", None),
        P("fsdp", None),
        P("fsdp", None, None),
        P("fsdp", None, None),
        P("fsdp", None, None),
    )
    return jax.shard_map(body, mesh=mesh, in_specs=in_specs, out_specs=out_specs, check_vma=False)
```

profile of v0, /device:TPU:0, one launch (start us, length us, event | category | flops | bytes accessed | tf_op | source)
XLA Modules:
  0.0 2052.4 jit_solution(10280987167617916473)
XLA Ops:
  16.5 9.6 reduce-window.6
  31.4 23.9 %all-reduce.5 = (bf16[1536]{0:T(1024)(128)(2,1)S(1)}, bf16[1536]{0:T(1024)(128)(2,1)S(1)}) all-reduce(bf16[1536]{0:T(1024)(128)(2,1)S(1)} %dynamic-update-slice, bf16[1536]{0:T(1024)(128)(2,1)S(1)} %dynamic-update-slice.1), channel_id=1, replica_groups=mesh['rep'=4,'fsdp'=8] {'fsdp'}, use_global_device_ids=true, to_apply=%add | all-reduce | flops 3072 | bytes 12288
  58.4 15.7 scatter_custom_fusion
  86.7 16.4 all-gather.6.cloned.1.call-done
  107.0 77.1 %all-gather.10.cloned.1.call-done = bf16[1536,1536]{1,0:T(8,128)(2,1)} async-done(((bf16[192,1536]{1,0:T(8,128)(2,1)}), bf16[1536,1536]{1,0:T(8,128)(2,1)}) %all-gather.10.cloned.1.call-update) | async-done | bytes 4718608 | tf_op jit(solution)/shard_map/all_gather | solution.py:132
  184.1 6.6 copy.84
  197.2 10.4 fusion.6
  207.6 11.2 exponential_reduce_fusion
  219.5 13.6 convolution_convert_fusion.6
  233.1 31.0 %all-gather.12.cloned.1.call-done = bf16[1536,1536]{1,0:T(8,128)(2,1)} async-done(((bf16[192,1536]{1,0:T(8,128)(2,1)}), bf16[1536,1536]{1,0:T(8,128)(2,1)}) %all-gather.12.cloned.1.call-update) | async-done | bytes 4718608 | tf_op jit(solution)/shard_map/all_gather | solution.py:135
  264.2 6.3 multiply_reduce_fusion.2
  273.7 22.4 %gather_fusion = bf16[3200,1536]{1,0:T(8,128)(2,1)} fusion(bf16[512,1536]{1,0:T(8,128)(2,1)} %multiply_convert_fusion.1, s32[4096]{0:T(1024)S(1)} %pad_clamp_fusion), kind=kCustom, calls=%fused_computation.2 | custom fusion | bytes 19673600 | tf_op jit(solution)/shard_map/jit(_take)/gather | solution.py:180
  296.1 8.3 broadcast_select_fusion
  309.6 233.2 %all-gather = bf16[8,192,16]{1,2,0:T(8,128)(2,1)S(1)} all-gather(bf16[1,192,16]{1,2,0:T(8,128)(2,1)S(1)} %bitcast.326), channel_id=1, replica_groups=mesh['rep'=4,'fsdp'=8] {'fsdp'}, dimensions={0}, use_global_device_ids=true | all-gather | bytes 55296 | tf_op jit(solution)/shard_map/all_gather | solution.py:136
  546.6 22.2 %gather_fusion.1 = f32[3200,1536]{1,0:T(8,128)} fusion(f32[512,1536]{1,0:T(8,128)} %convert_select_fusion, s32[4096]{0:T(1024)S(1)} %pad_clamp_fusion), kind=kCustom, calls=%fused_computation.3 | custom fusion | bytes 39334400 | tf_op jit(solution)/shard_map/jit(_take)/gather | solution.py:189
  570.7 33.0 %gather_fusion.2 = f32[4096]{0:T(1024)S(1)} fusion(f32[512,16]{0,1:T(8,128)S(1)} %fusion.115, s32[4096]{0:T(1024)S(1)} %reshape.685), kind=kCustom, calls=%fused_computation.4 | custom fusion | bytes 65536 | tf_op jit(solution)/shard_map/jit(take_along_axis)/gather | solution.py:175
  610.8 15.7 scatter_custom_fusion.1
  626.6 12.1 multiply_convert_fusion
  644.0 10.7 fusion.11
  654.7 9.6 fusion.13
  664.2 188.6 %all-to-all-done.2 = bf16[8,400,1536]{2,1,0:T(8,128)(2,1)} async-done(((bf16[8,400,1536]{2,1,0:T(8,128)(2,1)}), bf16[8,400,1536]{2,1,0:T(8,128)(2,1)}, u32[]{:S(2)}, u32[]{:S(2)}) %all-to-all-start.2) | async-done | bytes 9830432 | tf_op jit(solution)/shard_map/all_to_all | solution.py:201
  852.9 16.5 fusion.19
  869.4 9.9 convert_bitcast_fusion
  879.3 8.5 copy.95
  893.4 11.4 fusion.46
  904.8 13.4 fusion.15
  918.2 8.6 copy.97
  926.8 179.3 %all-to-all-done.1 = bf16[8,400,1536]{2,1,0:T(8,128)(2,1)} async-done(((bf16[8,400,1536]{2,1,0:T(8,128)(2,1)}), bf16[8,400,1536]{2,1,0:T(8,128)(2,1)}, u32[]{:S(2)}, u32[]{:S(2)}) %all-to-all-start.1) | async-done | bytes 9830432 | tf_op jit(solution)/shard_map/all_to_all | solution.py:198
  1113.5 30.8 %gather_fusion.3 = bf16[4096,1536]{1,0:T(8,128)(2,1)} fusion(bf16[3200,1536]{1,0:T(8,128)(2,1)} %bitcast.38, s32[4096]{0:T(1024)S(1)} %broadcast_clamp_fusion), kind=kCustom, calls=%fused_computation.clone | custom fusion | bytes 25182208 | tf_op jit(solution)/shard_map/jit(_take)/gather | solution.py:212
  1144.3 180.2 %all-to-all-done.3 = bf16[8,400,1536]{2,1,0:T(8,128)(2,1)} async-done(((bf16[8,400,1536]{2,1,0:T(8,128)(2,1)}), bf16[8,400,1536]{2,1,0:T(8,128)(2,1)}, u32[]{:S(2)}, u32[]{:S(2)}) %all-to-all-start.3) | async-done | bytes 9830432 | tf_op jit(solution)/shard_map/all_to_all | solution.py:207
  1324.5 30.6 %gather_fusion.4 = bf16[4096,1536]{1,0:T(8,128)(2,1)} fusion(bf16[3200,1536]{1,0:T(8,128)(2,1)} %bitcast.50, s32[4096]{0:T(1024)S(1)} %broadcast_clamp_fusion), kind=kCustom, calls=%fused_computation.1.clone | custom fusion | bytes 25182208 | tf_op jit(solution)/shard_map/jit(_take)/gather | solution.py:233
  1355.1 25.9 %fusion.1 = (f32[512,8]{1,0:T(8,128)S(1)}, f32[512,1536]{1,0:T(8,128)}, f32[512,1536]{1,0:T(8,128)}) fusion(f32[512,1536]{1,0:T(8,128)S(1)} %copy-done.2, bf16[4096,1536]{1,0:T(8,128)(2,1)} %gather_fusion.3, pred[512,8]{1,0:T(8,128)(4,1)} %get-tuple-element.37, f32[512,8]{1,0:T(8,128)S(1)} %copy-done.33, bf16[4096,1536]{1,0:T(8,128)(2,1)} %gather_fusion.4), kind=kLoop, calls=%fused_computation.10 | loop fusion | flops 55046144 | bytes 34639872 | tf_op jit(solution)/shard_map/reduce_sum | solution.py:215
  1394.2 12.2 fusion.66
  1406.4 21.4 %fusion.2 = (f32[8,3,512]{2,1,0:T(4,128)S(1)}, f32[8,512,512,3]{2,1,3,0:T(8,128)}) fusion(f32[8,512,512,3]{2,1,3,0:T(8,128)} %get-tuple-element.58, f32[8,3,512]{2,1,0:T(4,128)S(1)} %copy-done.39, pred[512,512]{0,1:T(8,128)(4,1)S(1)} %copy-done.16, bf16[512,8,64,1]{0,2,3,1:T(8,128)(2,1)} %bitcast.317, bf16[512,8,3,64]{0,3,2,1:T(8,128)(2,1)S(1)} %bitcast.307), kind=kOutput, calls=%fused_computation.13 | convolution fusion | flops 836751360 | bytes 52789248 | tf_op jit(solution)/shard_map/qhgd,khd->hgqk/dot_general | solution.py:260
  1431.4 22.7 %fusion.4 = bf16[8,3,512,512]{2,3,1,0:T(8,128)(2,1)} fusion(f32[8,512,512,3]{2,1,3,0:T(8,128)} %get-tuple-element.63, f32[8,512,512,3]{2,1,3,0:T(8,128)} %get-tuple-element.58, f32[8,3,512]{2,1,0:T(4,128)S(1)} %get-tuple-element.62, f32[8,3,512]{2,1,0:T(4,128)S(1)} %copy-done.39, pred[512,512]{0,1:T(8,128)(4,1)S(1)} %copy-done.16), kind=kLoop, calls=%fused_computation.15 | loop fusion | flops 37748736 | bytes 63275008 | tf_op jit(solution)/shard_map/convert_element_type | solution.py:264
  1454.1 8.6 fusion.65
  1465.7 7.2 convolution_convert_fusion
  1473.8 6.9 multiply_bitcast_fusion
  1486.9 11.8 bitcast_convert_fusion
  1498.7 9.8 bitcast_convert_fusion.1
  1510.1 10.7 bitcast_convert_fusion.2
  1520.9 42.5 %reduce-scatter.10.cloned.1.call-done = bf16[192,512]{1,0:T(8,128)(2,1)} async-done(((bf16[1536,512]{1,0:T(8,128)(2,1)}), bf16[192,512]{1,0:T(8,128)(2,1)}) %reduce-scatter.10.cloned.1.call-update) | async-done | bytes 196624 | tf_op jit(solution)/shard_map/reduce_scatter | solution.py:313
  1563.4 98.6 %reduce-scatter.14.cloned.1.call-done = bf16[192,1536]{1,0:T(8,128)(2,1)} async-done(((bf16[1536,1536]{1,0:T(8,128)(2,1)}), bf16[192,1536]{1,0:T(8,128)(2,1)}) %reduce-scatter.14.cloned.1.call-update) | async-done | bytes 589840 | tf_op jit(solution)/shard_map/reduce_scatter | solution.py:319
  1662.0 99.3 %reduce-scatter.8.cloned.1.call-done = bf16[192,1536]{1,0:T(8,128)(2,1)} async-done(((bf16[1536,1536]{1,0:T(8,128)(2,1)}), bf16[192,1536]{1,0:T(8,128)(2,1)}) %reduce-scatter.8.cloned.1.call-update) | async-done | bytes 589840 | tf_op jit(solution)/shard_map/reduce_scatter | solution.py:310
  1772.8 20.5 all-reduce.4
  1798.4 27.9 %reduce-scatter.16.cloned.1.call-done = bf16[192,16]{1,0:T(8,128)(2,1)} async-done(((bf16[1536,16]{1,0:T(8,128)(2,1)}), bf16[192,16]{1,0:T(8,128)(2,1)}) %reduce-scatter.16.cloned.1.call-update) | async-done | bytes 6160
  1827.1 5.9 all-reduce.6
  1834.7 191.6 %all-reduce.10.cloned.1.call-done = (bf16[192,1536]{1,0:T(8,128)(2,1)}, bf16[192,512]{1,0:T(8,128)(2,1)}, bf16[192,512]{1,0:T(8,128)(2,1)}, bf16[192,1536]{1,0:T...) async-done(((bf16[192,1536]{1,0:T(8,128)(2,1)}, bf16[192,512]{1,0:T(8,128)(2,1)}, ...) | async-done | bytes 11010064 | tf_op jit(solution)/shard_map/psum | solution.py:329
  (288 shorter events, 144.4 us)
Async XLA Ops:
  7.2 845.7 %copy-start = (bf16[2,512,1536]{2,1,0:T(8,128)(2,1)S(1)}, bf16[2,512,1536]{2,1,0:T(8,128)(2,1)}, u32[]{:S(2)}) copy-start(bf16[2,512,1536]{2,1,0:T(8,128)(2,1)} %param.29) | copy-start | bytes 9437188
  7.2 22.5 %copy-start.70 = (u32[32]{0:T(128)S(1)}, u32[32]{0:T(128)}, u32[]{:S(2)}) copy-start(u32[32]{0:T(128)} %constant.125) | copy-start | bytes 388
  7.2 23.7 %copy-start.73 = (bf16[192]{0:T(256)(128)(2,1)S(1)}, bf16[192]{0:T(256)(128)(2,1)}, u32[]{:S(2)}) copy-start(bf16[192]{0:T(256)(128)(2,1)} %param.20) | copy-start | bytes 1156
  7.2 24.0 %copy-start.74 = (bf16[192]{0:T(256)(128)(2,1)S(1)}, bf16[192]{0:T(256)(128)(2,1)}, u32[]{:S(2)}) copy-start(bf16[192]{0:T(256)(128)(2,1)} %param.21) | copy-start | bytes 1156
  7.2 73.1 %all-gather.8.cloned.1.call-start = ((), (), s32[]{:S(2)}) async-start(), calls=%async_computation.10 | async-start | bytes 1769472 | tf_op jit(solution)/shard_map/all_gather | solution.py:133
  8.0 95.2 %all-gather.6.cloned.1.call-start = ((), (), s32[]{:S(2)}) async-start(), calls=%async_computation.9 | async-start | bytes 1769472 | tf_op jit(solution)/shard_map/all_gather | solution.py:134
  8.7 175.4 %all-gather.10.cloned.1.call-start = ((), (), s32[]{:S(2)}) async-start(), calls=%async_computation.11 | async-start | bytes 5308416 | tf_op jit(solution)/shard_map/all_gather | solution.py:132
  9.4 254.7 %all-gather.12.cloned.1.call-start = ((), (), s32[]{:S(2)}) async-start(), calls=%async_computation.12 | async-start | bytes 5308416 | tf_op jit(solution)/shard_map/all_gather | solution.py:135
  11.6 65.1 %copy-start.53 = (pred[4096]{0:T(1024)(128)(4,1)}, pred[4096]{0:T(1024)(128)(4,1)S(1)}, u32[]{:S(2)}) copy-start(pred[4096]{0:T(1024)(128)(4,1)S(1)} %and.90) | copy-start | bytes 12292
  13.3 69.5 %copy-start.9 = (s32[1,512,8]{2,1,0:T(8,128)}, s32[1,512,8]{2,1,0:T(8,128)S(1)}, u32[]{:S(2)}) copy-start(s32[1,512,8]{2,1,0:T(8,128)S(1)} %copy.86) | copy-start | bytes 49156
  13.5 63.2 %copy-start.47 = (s32[4096]{0:T(1024)}, s32[4096]{0:T(1024)S(1)}, u32[]{:S(2)}) copy-start(s32[4096]{0:T(1024)S(1)} %eq.39) | copy-start | bytes 49156
  29.6 47.0 %copy-start.63 = (s32[4096,1]{0,1:T(1,128)}, s32[4096,1]{0,1:T(1,128)S(1)}, u32[]{:S(2)}) copy-start(s32[4096,1]{0,1:T(1,128)S(1)} %compare_select_fusion.2) | copy-start | bytes 49156
  78.8 117.4 %copy-start.28 = (f32[512,32]{0,1:T(8,128)}, f32[512,32]{0,1:T(8,128)S(1)}, u32[]{:S(2)}) copy-start(f32[512,32]{0,1:T(8,128)S(1)} %get-tuple-element.56) | copy-start | bytes 196612
  86.7 110.0 %copy-start.34 = (bf16[512,8,32]{0,2,1:T(8,128)(2,1)}, bf16[512,8,32]{0,2,1:T(8,128)(2,1)S(1)}, u32[]{:S(2)}) copy-start(bf16[512,8,32]{0,2,1:T(8,128)(2,1)S(1)} %get-tuple-element.50) | copy-start | bytes 786436
  196.8 10.8 copy-start.18
  196.8 10.8 copy-start.20
  207.6 11.9 copy-start.40
  273.7 22.4 %copy-start.55 = (pred[8,400]{1,0:T(8,128)(4,1)S(1)}, pred[8,400]{1,0:T(8,128)(4,1)}, u32[]{:S(2)}) copy-start(pred[8,400]{1,0:T(8,128)(4,1)} %broadcast_in_dim.127) | copy-start | bytes 9604
  304.4 238.5 %copy-start.43 = (s32[1,512,8]{1,2,0:T(8,128)S(1)}, s32[1,512,8]{1,2,0:T(8,128)}, u32[]{:S(2)}) copy-start(s32[1,512,8]{1,2,0:T(8,128)} %param.19) | copy-start | bytes 49156
  304.4 238.8 %copy-start.65 = (pred[512]{0:T(512)(128)(4,1)S(1)}, pred[512]{0:T(512)(128)(4,1)}, u32[]{:S(2)}) copy-start(pred[512]{0:T(512)(128)(4,1)} %copy-done.64) | copy-start | bytes 1540
  304.4 334.3 %all-to-all-start = ((bf16[8,400,1536]{2,1,0:T(8,128)(2,1)}), bf16[8,400,1536]{2,1,0:T(8,128)(2,1)}, u32[]{:S(2)}, u32[]{:S(2)}) async-start(bf16[8,400,1536]{2,1,0:T(8,128)(2,1)} %broadcast_select_fusion), calls=%async_computation | async-start | bytes 19660800 | tf_op jit(solution)/shard_map/all_to_all | solution.py:194
  542.9 25.8 %copy-start.42 = (bf16[1536,16]{0,1:T(8,128)(2,1)}, bf16[1536,16]{0,1:T(8,128)(2,1)S(1)}, u32[]{:S(2)}) copy-start(bf16[1536,16]{0,1:T(8,128)(2,1)S(1)} %reshape.721) | copy-start | bytes 147460
  570.7 34.0 %copy-start.10 = (s32[1,512,8]{2,1,0:T(8,128)S(1)}, s32[1,512,8]{2,1,0:T(8,128)}, u32[]{:S(2)}) copy-start(s32[1,512,8]{2,1,0:T(8,128)} %copy-done.9) | copy-start | bytes 49156
  570.7 40.1 %copy-start.46 = (s32[4096]{0:T(1024)S(1)}, s32[4096]{0:T(1024)}, u32[]{:S(2)}) copy-start(s32[4096]{0:T(1024)} %copy-done.45) | copy-start | bytes 49156
  570.7 40.1 %copy-start.48 = (s32[4096]{0:T(1024)S(1)}, s32[4096]{0:T(1024)}, u32[]{:S(2)}) copy-start(s32[4096]{0:T(1024)} %copy-done.47) | copy-start | bytes 49156
  570.7 40.1 %copy-start.54 = (pred[4096]{0:T(1024)(128)(4,1)S(1)}, pred[4096]{0:T(1024)(128)(4,1)}, u32[]{:S(2)}) copy-start(pred[4096]{0:T(1024)(128)(4,1)} %copy-done.53) | copy-start | bytes 12292
  638.7 214.2 %all-to-all-start.2 = ((bf16[8,400,1536]{2,1,0:T(8,128)(2,1)}), bf16[8,400,1536]{2,1,0:T(8,128)(2,1)}, u32[]{:S(2)}, u32[]{:S(2)}) async-start(bf16[8,400,1536]{2,1,0:T(8,128)(2,1)} %multiply_convert_fusion), calls=%async_computation.2 | async-start | bytes 19660800 | tf_op jit(solution)/shard_map/all_to_all | solution.py:201
  644.0 10.7 copy-start.71
  887.8 218.3 %all-to-all-start.1 = ((bf16[8,400,1536]{2,1,0:T(8,128)(2,1)}), bf16[8,400,1536]{2,1,0:T(8,128)(2,1)}, u32[]{:S(2)}, u32[]{:S(2)}) async-start(bf16[8,400,1536]{2,1,0:T(8,128)(2,1)} %bitcast.304), calls=%async_computation.1 | async-start | bytes 19660800 | tf_op jit(solution)/shard_map/all_to_all | solution.py:198
  1106.1 218.3 %all-to-all-start.3 = ((bf16[8,400,1536]{2,1,0:T(8,128)(2,1)}), bf16[8,400,1536]{2,1,0:T(8,128)(2,1)}, u32[]{:S(2)}, u32[]{:S(2)}) async-start(bf16[8,400,1536]{2,1,0:T(8,128)(2,1)} %bitcast.303), calls=%async_computation.3 | async-start | bytes 19660800 | tf_op jit(solution)/shard_map/all_to_all | solution.py:207
  1111.3 409.5 %reduce-scatter.12.cloned.1.call-start = ((), (), s32[]{:S(2)}) async-start(), calls=%async_computation.15 | async-start | bytes 1769472 | tf_op jit(solution)/shard_map/reduce_scatter | solution.py:316
  1324.5 30.6 %copy-start.2 = (f32[512,1536]{1,0:T(8,128)S(1)}, f32[512,1536]{1,0:T(8,128)}, u32[]{:S(2)}) copy-start(f32[512,1536]{1,0:T(8,128)} %convert_select_fusion) | copy-start | bytes 9437188
  1324.5 30.6 %copy-start.33 = (f32[512,8]{1,0:T(8,128)S(1)}, f32[512,8]{1,0:T(8,128)}, u32[]{:S(2)}) copy-start(f32[512,8]{1,0:T(8,128)} %get-tuple-element.34) | copy-start | bytes 49156
  1355.0 25.9 %copy-start.25 = (f32[512,8]{1,0:T(8,128)S(1)}, f32[512,8]{1,0:T(8,128)}, u32[]{:S(2)}) copy-start(f32[512,8]{1,0:T(8,128)} %get-tuple-element.35) | copy-start | bytes 49156
  1355.0 26.3 %copy-start.44 = (s32[1,512,8]{1,2,0:T(8,128)S(1)}, s32[1,512,8]{1,2,0:T(8,128)}, u32[]{:S(2)}) copy-start(s32[1,512,8]{1,2,0:T(8,128)} %param.19) | copy-start | bytes 49156
  1355.1 26.3 %copy-start.50 = (f32[1536]{0:T(1024)S(1)}, f32[1536]{0:T(1024)}, u32[]{:S(2)}) copy-start(f32[1536]{0:T(1024)} %convert_element_type.241) | copy-start | bytes 18436
  1355.1 26.3 %copy-start.57 = (f32[512]{0:T(512)S(1)}, f32[512]{0:T(512)}, u32[]{:S(2)}) copy-start(f32[512]{0:T(512)} %copy-done.56) | copy-start | bytes 6148
  1406.4 21.4 %copy-start.6 = (bf16[1,512,1536]{2,1,0:T(8,128)(2,1)S(1)}, bf16[1,512,1536]{2,1,0:T(8,128)(2,1)}, u32[]{:S(2)}) copy-start(bf16[1,512,1536]{2,1,0:T(8,128)(2,1)} %param.16) | copy-start | bytes 4718596
  1431.3 132.1 %reduce-scatter.10.cloned.1.call-start = ((), (), s32[]{:S(2)}) async-start(), calls=%async_computation.14 | async-start | bytes 1769472 | tf_op jit(solution)/shard_map/reduce_scatter | solution.py:313
  1431.4 22.7 %copy-start.19 = (bf16[512,8,3,32]{0,3,2,1:T(8,128)(2,1)S(1)}, bf16[512,8,3,32]{0,3,2,1:T(8,128)(2,1)}, u32[]{:S(2)}) copy-start(bf16[512,8,3,32]{0,3,2,1:T(8,128)(2,1)} %copy-done.18) | copy-start | bytes 2359300
  1431.4 22.7 %copy-start.21 = (bf16[512,8,3,32]{0,3,2,1:T(8,128)(2,1)S(1)}, bf16[512,8,3,32]{0,3,2,1:T(8,128)(2,1)}, u32[]{:S(2)}) copy-start(bf16[512,8,3,32]{0,3,2,1:T(8,128)(2,1)} %copy-done.20) | copy-start | bytes 2359300
  1465.4 196.6 %reduce-scatter.14.cloned.1.call-start = ((), (), s32[]{:S(2)}) async-start(), calls=%async_computation.16 | async-start | bytes 5308416 | tf_op jit(solution)/shard_map/reduce_scatter | solution.py:319
  1472.9 288.3 %reduce-scatter.8.cloned.1.call-start = ((), (), s32[]{:S(2)}) async-start(), calls=%async_computation.13 | async-start | bytes 5308416 | tf_op jit(solution)/shard_map/reduce_scatter | solution.py:310
  1486.9 339.3 %reduce-scatter.16.cloned.1.call-start = ((), (), s32[]{:S(2)}) async-start(), calls=%async_computation.17 | async-start | bytes 442368
  1486.9 11.8 copy-start.75
  1498.7 9.9 copy-start.3
  1509.8 516.5 %all-reduce.10.cloned.1.call-start = ((), (), s32[]{:S(2)}) async-start(), calls=%async_computation.18 | async-start | bytes 22020096 | tf_op jit(solution)/shard_map/psum | solution.py:329
  1769.4 24.1 %copy-start.61 = (f32[512]{0:T(512)S(1)}, f32[512]{0:T(512)}, u32[]{:S(2)}) copy-start(f32[512]{0:T(512)} %copy-done.60) | copy-start | bytes 6148
  (44 other events, 161.4 us)
Sparse Core Ops, SparseCore 0:
  10.2 47.5 all-gather.7
  60.0 43.0 all-gather.5
  105.3 78.6 all-gather.9
  186.1 78.0 all-gather.11
  1431.4 64.2 reduce-scatter.11
  1499.3 63.9 reduce-scatter.9
  1567.6 94.3 reduce-scatter.13
  1666.2 94.9 reduce-scatter.7
  1765.1 61.0 reduce-scatter.15
  1829.9 196.4 all-reduce.9
where the time goes:
time: 2060 us; the launch traced here: 2050 us
  waiting for transfers between devices  1140 us (55%)
  blocking collectives  283 us (14%)
  matrix products  232 us (11%)
  local copies, waits for them, and re-layouts  224 us (11%)
  other arithmetic  138 us (7%)
  starting transfers between devices  22.1 us (1%)
    all_gather x1, blocking collectives, body(): lax.all_gather(w_router, 'fsdp', axis=0, tiled=True)  233 us
    psum x1, waiting for transfers between devices, body(): lax.psum(owned[2].astype(jnp.bfloat16), 'rep').astype(jnp.float32)  192 us
    all_to_all x1, waiting for transfers between devices, body(): lax.all_to_all(grad_send, 'fsdp', split_axis=0, concat_axis=0, tiled=True)  189 us
    all_to_all x1, waiting for transfers between devices, body(): lax.all_to_all(grad_rows.reshape(flat_shape), 'fsdp', split_axis=0, conca...  180 us
    all_to_all x1, waiting for transfers between devices, body(): lax.all_to_all(expert_out.reshape(flat_shape), 'fsdp', split_axis=0, conc...  179 us
    reduce_scatter x1, waiting for transfers between devices, body(): lax.psum_scatter(grad_query.astype(jnp.bfloat16), 'fsdp', scatter_dimensi...  99.3 us
    reduce_scatter x1, waiting for transfers between devices, body(): lax.psum_scatter(grad_out.astype(jnp.bfloat16), 'fsdp', scatter_dimension...  98.6 us
    all_gather x1, waiting for transfers between devices, body(): lax.all_gather(query_weight, 'fsdp', axis=0, tiled=True)  77.1 us
  transfers between devices with their start and end apart: 14, of which 11 were waited for; matrix products, arithmetic and copies ran while one was open for 19% of the time, Pallas kernels for 0%

commit v1 on v0

v1 whole, which is shorter than its diff:
```python
import functools
import math

import jax
import jax.numpy as jnp
from jax import lax
from jax.experimental import pallas as pl
from jax.experimental.pallas import tpu as pltpu
from jax.sharding import PartitionSpec as P

QUERY_HEADS = 24
KEY_VALUE_HEADS = 8
HEAD_SIZE = 64
BF16 = jnp.bfloat16
F32 = jnp.float32
ALL = ("fsdp", "rep")
SMALL = 128


def rms_scale(value_rows, gain_vec):
    inverse = lax.rsqrt(jnp.mean(value_rows * value_rows, axis=-1, keepdims=True) + 1e-05)
    return value_rows * inverse * gain_vec


def rotation(expert_slot_count, head_dim):
    half_dim = head_dim // 2
    frequency = jnp.exp(
        -jnp.log(10000.0) * 2.0 * jnp.arange(half_dim, dtype=jnp.float32) / head_dim
    )
    angles = jnp.arange(expert_slot_count, dtype=jnp.float32)[:, None] * frequency[None, :]
    return (jnp.cos(angles), jnp.sin(angles))


def rotary_apply(value_rows, cosine_table, sine_table):
    half_dim = value_rows.shape[-1] // 2
    extra_dims = (1,) * (value_rows.ndim - 2)
    cosine_table = cosine_table.reshape(
        cosine_table.shape[:1] + extra_dims + cosine_table.shape[1:]
    )
    sine_table = sine_table.reshape(sine_table.shape[:1] + extra_dims + sine_table.shape[1:])
    first_half = value_rows[..., :half_dim]
    second = value_rows[..., half_dim:]
    return jnp.concatenate(
        [
            first_half * cosine_table - second * sine_table,
            second * cosine_table + first_half * sine_table,
        ],
        axis=-1,
    )


def slot_table(choices_row, length, experts, capacity):
    slots = choices_row.shape[0]
    valid = (jnp.arange(slots, dtype=jnp.int32) < length)[:, None]
    chosen = jnp.any(
        choices_row[:, :, None] == jnp.arange(experts, dtype=jnp.int32)[None, None, :], axis=1
    )
    hit = (chosen & valid).astype(F32)
    rows = jnp.arange(slots, dtype=jnp.int32)
    earlier = (rows[None, :] < rows[:, None]).astype(BF16)
    position = jnp.dot(earlier, hit.astype(BF16), preferred_element_type=F32).astype(jnp.int32)
    kept = chosen & valid & (position < capacity)
    return jnp.where(kept, position, jnp.where(chosen, -1, -2))


def chosen_gates(logits, table):
    chosen = table >= -1
    masked = jnp.where(chosen, logits, -1e30)
    top = jnp.max(masked, axis=-1, keepdims=True)
    raised = jnp.where(chosen, jnp.exp(masked - top), 0.0)
    return raised / jnp.sum(raised, axis=-1, keepdims=True)


def ring_order(size):
    if size % 2:
        return list(range(size))
    return list(range(0, size, 2)) + list(range(size - 1, 0, -2))


def shift(value, order, step):
    size = len(order)
    return lax.ppermute(value, "fsdp", [(order[i], order[(i + step) % size]) for i in range(size)])


def ring_gather(value, order):
    size = len(order)
    found = {0: value}
    ahead = back = value
    for step in range(1, (size - 1) // 2 + 1):
        back = shift(back, order, 1)
        ahead = shift(ahead, order, -1)
        found[-step] = back
        found[step] = ahead
    if size % 2 == 0:
        half = value.shape[0] // 2
        top = shift(back[:half], order, 1)
        bottom = shift(ahead[half:], order, -1)
        found[size // 2] = jnp.concatenate([top, bottom], axis=0)
    return found


def add_low(left, right):
    return (left.astype(F32) + right.astype(F32)).astype(BF16)


def ring_scatter(parts, order):
    size = len(order)
    near = (size - 1) // 2
    if size % 2 == 0:
        far = parts[size // 2]
        half = far.shape[0] // 2
        top = shift(far[:half], order, 1)
        bottom = shift(far[half:], order, -1)
        ahead, back = parts[near], parts[-near]
        ahead = jnp.concatenate([add_low(ahead[:half], top), ahead[half:]], axis=0)
        back = jnp.concatenate([back[:half], add_low(back[half:], bottom)], axis=0)
    else:
        ahead, back = parts[near], parts[-near]
    for step in range(near, 0, -1):
        ahead = shift(ahead, order, 1)
        back = shift(back, order, -1)
        if step > 1:
            ahead = add_low(parts[step - 1], ahead)
            back = add_low(parts[1 - step], back)
    return ahead, back


def three_way(value):
    high = value.astype(BF16)
    rest = value - high.astype(F32)
    middle = rest.astype(BF16)
    low = (rest - middle.astype(F32)).astype(BF16)
    return high, middle, low


def dot_nn(left, right):
    return jnp.dot(left, right, preferred_element_type=F32)


def dot_nt(left, right):
    return lax.dot_general(left, right, (((1,), (1,)), ((), ())), preferred_element_type=F32)


def expert_kernel(
    first_ref,
    seq_ref,
    tok_ref,
    cot_ref,
    row_ref,
    col_ref,
    router_ref,
    gate_ref,
    up_ref,
    down_ref,
    *rest,
    padded,
):
    (
        out_ref,
        grad_ref,
        gg_ref,
        rows_ref,
        geo_ref,
        inner_ref,
        ggp_ref,
        gup_ref,
        gates_scr,
        out_acc,
        grad_acc,
    ) = rest[-11:]
    e = pl.program_id(1)
    tok = tok_ref[0]
    cot = cot_ref[0]
    slots = tok.shape[0]
    table = col_ref[0]
    lanes = lax.broadcasted_iota(jnp.int32, table.shape, 1)

    @pl.when(e == 0)
    def _():
        gates_scr[...] = chosen_gates(dot_nn(tok, router_ref[...]), table)
        out_acc[...] = jnp.zeros_like(out_acc)
        grad_acc[...] = jnp.zeros_like(grad_acc)
        gg_ref[0] = jnp.zeros_like(gg_ref[0])

    mine = lanes == first_ref[0] + e
    gate_lane = jnp.where(mine, gates_scr[...], 0.0)
    gate_col = jnp.sum(gate_lane, axis=1, keepdims=True)
    pos_col = jnp.sum(jnp.where(mine, table.astype(F32), 0.0), axis=1, keepdims=True).astype(jnp.int32)
    pos_row = row_ref[0, 0]
    pick = (lax.broadcasted_iota(jnp.int32, (padded, slots), 0) == pos_row).astype(F32).astype(BF16)
    place = (lax.broadcasted_iota(jnp.int32, (slots, padded), 1) == pos_col).astype(F32).astype(BF16)

    rows = dot_nn(pick, tok).astype(BF16)
    cot_rows = dot_nn(pick, cot)
    high, middle, low = three_way(gate_lane)
    gate_slot = dot_nn(pick, high) + dot_nn(pick, middle) + dot_nn(pick, low)
    gate_slot = jnp.sum(gate_slot, axis=1, keepdims=True)
    rows_ref[0, 0] = rows

    gate_part = dot_nn(rows, gate_ref[0])
    up_part = dot_nn(rows, up_ref[0])
    sig = 1.0 / (1.0 + jnp.exp(-gate_part))
    silu = gate_part * sig
    inner = (silu * up_part).astype(BF16)
    inner_ref[0, 0] = inner
    expert_out = dot_nn(inner, down_ref[0]).astype(BF16)
    out_acc[...] += gate_col * dot_nn(place, expert_out)

    dots = jnp.sum(cot_rows * expert_out.astype(F32), axis=1, keepdims=True)
    spread = jnp.where(lax.broadcasted_iota(jnp.int32, (padded, SMALL), 1) == e, dots, 0.0)
    high, middle, low = three_way(spread)
    gg_ref[0] += dot_nn(place, high) + dot_nn(place, middle) + dot_nn(place, low)

    geo = (gate_slot * cot_rows).astype(BF16)
    geo_ref[0, 0] = geo
    grad_inner = dot_nt(geo, down_ref[0])
    ggp = (grad_inner * up_part * sig * (1.0 + gate_part * (1.0 - sig))).astype(BF16)
    gup = (grad_inner * silu).astype(BF16)
    ggp_ref[0, 0] = ggp
    gup_ref[0, 0] = gup
    grad_rows = (dot_nt(ggp, gate_ref[0]) + dot_nt(gup, up_ref[0])).astype(BF16)
    grad_acc[...] += dot_nn(place, grad_rows)

    @pl.when(e == pl.num_programs(1) - 1)
    def _():
        out_ref[0] = out_acc[...].astype(BF16)
        grad_ref[0] = grad_acc[...].astype(BF16)


def run_experts(first, seqs, tok, cot, rows_table, cols_table, router, w_gate, w_up, w_down, padded, kept, start, total):
    count, slots, width = tok.shape
    local, _, ff = w_gate.shape
    row_block = lambda s, e, first, seq: (seq[s], first[0] + e, 0, 0)
    col_block = lambda s, e, first, seq: (seq[s], 0, 0)
    seq_block = lambda s, e, first, seq: (s, 0, 0)
    slot_block = lambda s, e, first, seq: (start + s, e, 0, 0)
    expert_block = lambda s, e, first, seq: (e, 0, 0)
    wide = jax.ShapeDtypeStruct((total, local, padded, width), BF16)
    thin = jax.ShapeDtypeStruct((total, local, padded, ff), BF16)
    whole = jax.ShapeDtypeStruct((count, slots, width), BF16)
    flops = 2 * count * local * (padded * width * (6 * ff + 4 * slots))
    moved = 4 * count * slots * width * 2 + count * local * (3 * width * ff + padded * (2 * width + 3 * ff)) * 2
    return pl.pallas_call(
        functools.partial(expert_kernel, padded=padded),
        out_shape=(
            whole,
            whole,
            jax.ShapeDtypeStruct((count, slots, SMALL), F32),
            wide,
            wide,
            thin,
            thin,
            thin,
        ),
        grid_spec=pltpu.PrefetchScalarGridSpec(
            num_scalar_prefetch=2,
            grid=(count, local),
            in_specs=[
                pl.BlockSpec((1, slots, width), seq_block),
                pl.BlockSpec((1, slots, width), seq_block),
                pl.BlockSpec((1, 1, 1, slots), row_block),
                pl.BlockSpec((1, slots, SMALL), col_block),
                pl.BlockSpec((width, SMALL), lambda s, e, first, seq: (0, 0)),
                pl.BlockSpec((1, width, ff), expert_block),
                pl.BlockSpec((1, width, ff), expert_block),
                pl.BlockSpec((1, ff, width), expert_block),
            ]
            + [pl.BlockSpec(memory_space=pl.ANY)] * len(kept),
            out_specs=[
                pl.BlockSpec((1, slots, width), seq_block),
                pl.BlockSpec((1, slots, width), seq_block),
                pl.BlockSpec((1, slots, SMALL), seq_block),
                pl.BlockSpec((1, 1, padded, width), slot_block),
                pl.BlockSpec((1, 1, padded, width), slot_block),
                pl.BlockSpec((1, 1, padded, ff), slot_block),
                pl.BlockSpec((1, 1, padded, ff), slot_block),
                pl.BlockSpec((1, 1, padded, ff), slot_block),
            ],
            scratch_shapes=[
                pltpu.VMEM((slots, SMALL), F32),
                pltpu.VMEM((slots, width), F32),
                pltpu.VMEM((slots, width), F32),
            ],
        ),
        input_output_aliases={10 + i: 3 + i for i in range(len(kept))},
        compiler_params=pltpu.CompilerParams(
            dimension_semantics=("arbitrary", "arbitrary"), vmem_limit_bytes=58 * 1024 * 1024
        ),
        cost_estimate=pl.CostEstimate(flops=flops, bytes_accessed=moved, transcendentals=count * local * padded * ff),
    )(first, seqs, tok, cot, rows_table, cols_table, router, w_gate, w_up, w_down, *kept)


def body(
    inputs,
    cotangent,
    lengths,
    choices,
    gain_attn,
    gain_moe,
    query_weight,
    key_weight,
    value_weight,
    w_out,
    w_router,
    w_gate,
    w_up,
    w_down,
):
    groups = lax.axis_size("fsdp")
    replicas = lax.axis_size("rep")
    me = lax.axis_index("fsdp")
    rep = lax.axis_index("rep")
    tokens = inputs[0].astype(F32)
    slots, width = tokens.shape
    length = lengths[0]
    choices_row = choices[0]
    top_count = choices_row.shape[1]
    local = w_gate.shape[0]
    experts = local * groups
    capacity = 25 * slots * top_count // (32 * experts)
    padded = -(-capacity // 16) * 16
    group_width = QUERY_HEADS // KEY_VALUE_HEADS
    scale_factor = 1.0 / math.sqrt(HEAD_SIZE)
    q_width = query_weight.shape[1]
    k_width = key_weight.shape[1]
    cosine_table, sine_table = rotation(slots, HEAD_SIZE)
    order = ring_order(groups)
    place_of = [order.index(j) for j in range(groups)]
    my_place = jnp.asarray(place_of, jnp.int32)[me]

    small = jnp.concatenate(
        [
            w_router,
            gain_attn[:, None],
            gain_moe[:, None],
            jnp.zeros((w_router.shape[0], SMALL - experts - 2), BF16),
        ],
        axis=1,
    )
    share = query_weight.shape[0] // replicas

    def gather_weight(shard):
        piece = lax.dynamic_slice_in_dim(shard, rep * share, share, axis=0)
        return lax.all_gather(piece, ALL, axis=0, tiled=True)

    first_set = gather_weight(
        jnp.concatenate([query_weight, key_weight, value_weight, small], axis=1)
    )
    full_qkv = first_set[:, : q_width + 2 * k_width]
    full_small = first_set[:, q_width + 2 * k_width :]
    full_out = gather_weight(w_out)
    full_gain_attn = full_small[:, experts].astype(F32)
    full_gain_moe = full_small[:, experts + 1].astype(F32)
    lane = jnp.arange(SMALL)[None, :]
    full_router = jnp.where(lane < experts, full_small, jnp.zeros_like(full_small))

    table = slot_table(choices_row, length, experts, capacity)
    row_tables = lax.all_gather(table.T, "fsdp", axis=0, tiled=False)
    col_tables = jnp.pad(
        jnp.swapaxes(row_tables, 1, 2), ((0, 0), (0, 0), (0, SMALL - experts)), constant_values=-2
    )
    row_tables = row_tables[:, :, None, :]
    cot_ring = ring_gather(lax.optimization_barrier((cotangent[0], first_set))[0], order)

    normed_float, norm_one_pull = jax.vjp(rms_scale, tokens, full_gain_attn)
    attention_normed = normed_float.astype(BF16)
    query_rows = jnp.dot(
        attention_normed, full_qkv[:, :q_width], preferred_element_type=F32
    ).reshape(slots, KEY_VALUE_HEADS, group_width, HEAD_SIZE)
    unrotated_keys = jnp.dot(
        attention_normed, full_qkv[:, q_width : q_width + k_width], preferred_element_type=F32
    ).reshape(slots, KEY_VALUE_HEADS, HEAD_SIZE)
    value_rows = (
        jnp.dot(attention_normed, full_qkv[:, q_width + k_width :], preferred_element_type=F32)
        .astype(BF16)
        .reshape(slots, KEY_VALUE_HEADS, HEAD_SIZE)
    )
    rot_queries = rotary_apply(query_rows, cosine_table, sine_table).astype(BF16)
    rot_keys = rotary_apply(unrotated_keys, cosine_table, sine_table).astype(BF16)
    rows_index = jnp.arange(slots, dtype=jnp.int32)
    allowed = (rows_index[None, :] <= rows_index[:, None]) & (rows_index[None, :] < length)

    def masked_scores():
        raw_scores = (
            jnp.einsum("qhgd,khd->hgqk", rot_queries, rot_keys, preferred_element_type=F32)
            * scale_factor
        )
        return jnp.where(allowed, raw_scores, -1e30)

    scores = masked_scores()
    log_total = jax.nn.logsumexp(scores, axis=-1, keepdims=True)
    probs_low = jnp.exp(scores - log_total).astype(BF16)
    mixed = jnp.einsum("hgqk,khd->qhgd", probs_low, value_rows, preferred_element_type=F32)
    mixed = mixed.astype(BF16).reshape(slots, QUERY_HEADS * HEAD_SIZE)
    hidden = tokens + jnp.dot(mixed, full_out, preferred_element_type=F32)
    normed_float_two, norm_two_pull = jax.vjp(rms_scale, hidden, full_gain_moe)
    normed_two = normed_float_two.astype(BF16)

    tok_ring = ring_gather(normed_two, order)
    gates = chosen_gates(
        jnp.dot(normed_two, full_router, preferred_element_type=F32)[:, :experts], table
    )
    valid_rows = (rows_index < length)[:, None]
    grad_y = jnp.where(valid_rows, cotangent[0].astype(F32), 0.0)

    near = (groups - 1) // 2
    arrivals = [(0,)] + [(-s, s) for s in range(1, near + 1)]
    if groups % 2 == 0:
        arrivals.append((groups // 2,))
    order_array = jnp.asarray(order, jnp.int32)
    first = (me * local).astype(jnp.int32).reshape(1)
    out_parts, grad_parts, gate_dots, kept, start = {}, {}, {}, (), 0
    for offsets in arrivals:
        seqs = order_array[(my_place + jnp.asarray(offsets, jnp.int32)) % groups]
        tok = jnp.stack([tok_ring[s] for s in offsets])
        cot = jnp.stack([cot_ring[s] for s in offsets])
        part_out, part_grad, dots, *kept = run_experts(
            first, seqs, tok, cot, row_tables, col_tables, full_router, w_gate, w_up, w_down,
            padded, kept, start, groups,
        )
        for j, s in enumerate(offsets):
            out_parts[s] = part_out[j]
            grad_parts[s] = part_grad[j]
            gate_dots[s % groups] = dots[j, :, :local].T
        start += len(offsets)
    rows_all, geo_all, inner_all, ggp_all, gup_all = kept

    by_offset = jnp.stack([gate_dots[s] for s in range(groups)])
    natural = by_offset[(jnp.asarray(place_of, jnp.int32) - my_place) % groups]
    grad_gates = lax.all_to_all(natural, "fsdp", split_axis=0, concat_axis=0, tiled=True)
    grad_gates = grad_gates.reshape(experts, slots).T

    left, right = ring_scatter(grad_parts, order)
    grad_normed_two = grad_parts[0].astype(F32) + left.astype(F32) + right.astype(F32)

    grad_down = jnp.einsum("necf,necd->efd", inner_all, geo_all, preferred_element_type=F32)
    grad_gate = jnp.einsum("necd,necf->edf", rows_all, ggp_all, preferred_element_type=F32)
    grad_up = jnp.einsum("necd,necf->edf", rows_all, gup_all, preferred_element_type=F32)
    expert_grads = [lax.psum(g.astype(BF16), "rep").astype(F32) for g in (grad_gate, grad_up, grad_down)]

    grad_logits = gates * (grad_gates - jnp.sum(gates * grad_gates, axis=-1, keepdims=True))
    grad_logits = grad_logits.astype(BF16)
    grad_normed_two = grad_normed_two + jnp.einsum(
        "se,de->sd", grad_logits, full_router[:, :experts], preferred_element_type=F32
    )
    grad_router = jnp.einsum("sd,se->de", normed_two, grad_logits, preferred_element_type=F32)
    grad_hidden_norm, grad_gain_moe = norm_two_pull(grad_normed_two)
    grad_hidden = grad_y + grad_hidden_norm
    grad_attn = grad_hidden.astype(BF16)
    grad_out = jnp.einsum("sa,sd->ad", mixed, grad_attn, preferred_element_type=F32)

    def reduce_weight(grad):
        owned = lax.psum_scatter(grad.astype(BF16), ALL, scatter_dimension=0, tiled=True)
        return lax.all_gather(owned, "rep", axis=0, tiled=True)

    total_out = reduce_weight(grad_out).astype(F32)
    out_left, out_right = ring_scatter(out_parts, order)
    mixture = out_parts[0].astype(F32) + out_left.astype(F32) + out_right.astype(F32)
    output = jnp.where(valid_rows, hidden + mixture, 0.0).astype(BF16)

    gradient_mixed_rows = jnp.einsum("sd,ad->sa", grad_attn, full_out, preferred_element_type=F32)
    gradient_mixed_rows = gradient_mixed_rows.astype(BF16).reshape(
        slots, KEY_VALUE_HEADS, group_width, HEAD_SIZE
    )
    scores = masked_scores()
    probs = jnp.exp(scores - log_total)
    probs_low = probs.astype(BF16)
    gradient_value_rows = jnp.einsum(
        "hgqk,qhgd->khd", probs_low, gradient_mixed_rows, preferred_element_type=F32
    )
    gradient_value_rows = gradient_value_rows.astype(BF16).reshape(slots, k_width)
    grad_probs = jnp.einsum(
        "qhgd,khd->hgqk", gradient_mixed_rows, value_rows, preferred_element_type=F32
    )
    grad_scores = probs * (grad_probs - jnp.sum(probs * grad_probs, axis=-1, keepdims=True))
    grad_scores = grad_scores.astype(BF16)
    grad_rot_queries = (
        jnp.einsum("hgqk,khd->qhgd", grad_scores, rot_keys, preferred_element_type=F32)
        * scale_factor
    )
    gradient_rotated_keys = (
        jnp.einsum("hgqk,qhgd->khd", grad_scores, rot_queries, preferred_element_type=F32)
        * scale_factor
    )
    grad_queries = (
        rotary_apply(grad_rot_queries, cosine_table, -sine_table).astype(BF16).reshape(slots, q_width)
    )
    grad_keys = (
        rotary_apply(gradient_rotated_keys, cosine_table, -sine_table)
        .astype(BF16)
        .reshape(slots, k_width)
    )
    grad_projected = jnp.concatenate([grad_queries, grad_keys, gradient_value_rows], axis=1)
    grad_qkv = jnp.einsum("sd,sa->da", attention_normed, grad_projected, preferred_element_type=F32)
    grad_normed_one = jnp.einsum("sa,da->sd", grad_projected, full_qkv, preferred_element_type=F32)
    grad_tokens_norm, grad_gain_attn = norm_one_pull(grad_normed_one)
    grad_input = (grad_hidden + grad_tokens_norm).astype(BF16)
    grad_small = jnp.concatenate(
        [
            grad_router,
            grad_gain_attn[:, None],
            grad_gain_moe[:, None],
            jnp.zeros((width, SMALL - experts - 2), F32),
        ],
        axis=1,
    )
    total_first = reduce_weight(jnp.concatenate([grad_qkv, grad_small], axis=1)).astype(F32)
    total_small = total_first[:, q_width + 2 * k_width :]
    return (
        output[None],
        grad_input[None],
        total_small[:, experts],
        total_small[:, experts + 1],
        total_first[:, :q_width],
        total_first[:, q_width : q_width + k_width],
        total_first[:, q_width + k_width : q_width + 2 * k_width],
        total_out,
        total_small[:, :experts],
        *expert_grads,
    )


def solution(mesh):
    in_specs = (
        P(("rep", "fsdp"), None, None),
        P(("rep", "fsdp"), None, None),
        P(("rep", "fsdp")),
        P(("rep", "fsdp"), None, None),
        P("fsdp"),
        P("fsdp"),
        P("fsdp", None),
        P("fsdp", None),
        P("fsdp", None),
        P("fsdp", None),
        P("fsdp", None),
        P("fsdp", None, None),
        P("fsdp", None, None),
        P("fsdp", None, None),
    )
    out_specs = (
        P(("rep", "fsdp"), None, None),
        P(("rep", "fsdp"), None, None),
        P("fsdp"),
        P("fsdp"),
        P("fsdp", None),
        P("fsdp", None),
        P("fsdp", None),
        P("fsdp", None),
        P("fsdp", None),
        P("fsdp", None, None),
        P("fsdp", None, None),
        P("fsdp", None, None),
    )
    return jax.shard_map(body, mesh=mesh, in_specs=in_specs, out_specs=out_specs, check_vma=False)
```

time: 2060 us -> 997 us (0.48)
  waiting for transfers between devices: 1140 us -> 414 us
  blocking collectives: 283 us -> 50.7 us
  local copies, waits for them, and re-layouts: 224 us -> 79.9 us
  Pallas kernels: 0 us -> 128 us
  matrix products: 232 us -> 141 us
    all_to_all x4 -> x1, waiting for transfers between devices: 548 us -> 0.01 us  [body(): lax.all_to_all(natural, 'fsdp', split_axis=0, concat_axis=0, tiled=True)]
    ppermute x0 -> x32, waiting for transfers between devices: none -> 222 us  [shift(): lax.ppermute(value, 'fsdp', [(order[i], order[(i + step) % size]) for i i...]
    psum x1, waiting for transfers between devices: 192 us -> 0.02 us  [body(): lax.psum(g.astype(BF16), 'rep').astype(F32)]
    all_gather x1 -> x3, blocking collectives: 233 us -> 50.7 us  [the longest x1 32.9 us: body(): row_tables = lax.all_gather(table.T, 'fsdp', axis=0, tiled=False)]
    gather x8 -> x5, local copies, waits for them, and re-layouts: 140 us -> 5.32 us  [the longest x4 4.13 us: body(): seqs = order_array[(my_place + jnp.asarray(offsets, jnp.int32)) % groups]]
    pallas_call x0 -> x5, Pallas kernels: none -> 128 us  [run_experts(): pl.pallas_call(functools.partial(expert_kernel, padded=padded), out_shape...]
    dot_general x24 -> x15, matrix products: 159 us -> 68.2 us  [the longest x1 11 us: body(): jnp.einsum('necd,necf->edf', rows_all, ggp_all, preferred_element_type=F32)]
    all_gather x4 -> x2, waiting for transfers between devices: 125 us -> 37 us  [gather_weight(): return lax.all_gather(piece, ALL, axis=0, tiled=True)]
  transfers between devices with their start and end apart: 14 -> 38, of which waited for: 11 -> 17; matrix products, arithmetic and copies ran while one was open for 19% -> 32% of each run, Pallas kernels for 0% -> 11%
where the time goes in v1:
time: 997 us; the launch traced here: 992 us
  waiting for transfers between devices  414 us (42%)
  matrix products  141 us (14%)
  Pallas kernels  128 us (13%)
  other arithmetic  123 us (12%)
  local copies, waits for them, and re-layouts  79.9 us (8%)
  blocking collectives  50.7 us (5%)
  starting transfers between devices  37.6 us (4%)
  between operations  18.4 us (2%)
    ppermute x32, waiting for transfers between devices, shift(): lax.ppermute(value, 'fsdp', [(order[i], order[(i + step) % size]) for i i...  222 us
    reduce_scatter x2, waiting for transfers between devices, reduce_weight(): lax.psum_scatter(grad.astype(BF16), ALL, scatter_dimension=0, tiled=True)  154 us
    pallas_call x5, Pallas kernels, run_experts(): pl.pallas_call(functools.partial(expert_kernel, padded=padded), out_shape...  128 us
    all_gather x2, waiting for transfers between devices, gather_weight(): return lax.all_gather(piece, ALL, axis=0, tiled=True)  37 us
    ppermute x32, starting transfers between devices, shift(): lax.ppermute(value, 'fsdp', [(order[i], order[(i + step) % size]) for i i...  33.1 us
    all_gather x1, blocking collectives, body(): row_tables = lax.all_gather(table.T, 'fsdp', axis=0, tiled=False)  32.9 us
    convert_element_type x1, other arithmetic, body(): grad_scores = grad_scores.astype(BF16)  22.5 us
    dot_general x1, matrix products, body(): jnp.einsum('qhgd,khd->hgqk', gradient_mixed_rows, value_rows, preferred_e...  21.3 us
  transfers between devices with their start and end apart: 38, of which 17 were waited for; matrix products, arithmetic and copies ran while one was open for 32% of the time, Pallas kernels for 11%

profile of v1, /device:TPU:0, one launch (start us, length us, event | category | flops | bytes accessed | tf_op | source)
XLA Modules:
  0.0 992.3 jit_solution(3836578671626399998)
XLA Ops:
  23.8 32.9 %all-gather = s32[128,512]{1,0:T(8,128)S(1)} all-gather(s32[16,512]{1,0:T(8,128)S(1)} %get-tuple-element.259), channel_id=2, replica_groups=mesh['rep'=4,'fsdp'=8] {'fsdp'}, dimensions={0}, use_global_device_ids=true | all-gather | bytes 294912 | tf_op jit(solution)/shard_map/all_gather | solution.py:358
  61.5 31.1 %all-gather.4.cloned.1.call-done = bf16[1536,2688]{1,0:T(8,128)(2,1)} async-done(((bf16[48,2688]{1,0:T(8,128)(2,1)}), bf16[1536,2688]{1,0:T(8,128)(2,1)}) %all-gather.4.cloned.1.call-update) | async-done | bytes 8257552 | tf_op jit(solution)/shard_map/all_gather | solution.py:344
  98.0 4.8 slice_bitcast_fusion
  102.8 6.7 copy.164
  117.5 10.5 %fusion.4 = (f32[8,3,512]{2,1,0:T(4,128)S(1)}, f32[8,512,512,3]{2,1,3,0:T(8,128)}) fusion(pred[512,512]{0,1:T(8,128)(4,1)S(1)} %fusion.55, bf16[512,8,3,32]{0,3,2,1:T(8,128)(2,1)S(1)} %get-tuple-element.221, bf16[512,8,3,32]{0,3,2,1:T(8,128)(2,1)S(1)} %get-tuple-element.220, bf16[512,8,32]{0,2,1:T(8,128)(2,1)S(1)} %get-tuple-element.247, ...), kind=kOutput, calls=%fused_computation.13 | convolution fusion | flops 828362752 | bytes 27574272 | tf_op jit(solution)/shard_map/qhgd,khd->hgqk/dot_general | solution.py:385
  128.1 11.1 %exponential_reduce_fusion = f32[8,3,512]{2,1,0:T(4,128)S(1)} fusion(f32[8,512,512,3]{2,1,3,0:T(8,128)} %get-tuple-element.256, f32[8,3,512]{2,1,0:T(4,128)S(1)} %is-finite_select_fusion, pred[512,512]{0,1:T(8,128)(4,1)S(1)} %fusion.55), kind=kLoop, calls=%fused_computation.11 | loop fusion | flops 25153536 | bytes 25526272 | tf_op jit(solution)/shard_map/reduce_sum | solution.py:391
  142.6 13.3 %convolution_convert_fusion.4 = bf16[8,64,3,512]{3,1,2,0:T(8,128)(2,1)} fusion(bf16[512,8,64,1]{0,2,3,1:T(8,128)(2,1)S(1)} %bitcast.321, f32[8,512,512,3]{2,1,3,0:T(8,128)} %get-tuple-element.256, f32[8,3,512]{2,1,0:T(4,128)S(1)} %log_add_fusion, pred[512,512]{0,1:T(8,128)(4,1)S(1)} %fusion.55), kind=kOutput, calls=%fused_computation.80 | convolution fusion | flops 831258624 | bytes 27574272 | tf_op jit(solution)/shard_map/hgqk,khd->qhgd/dot_general | solution.py:393
  155.9 5.9 all-gather.6.cloned.1.call-done
  161.8 5.3 multiply_reduce_fusion.2
  172.6 18.4 %shard_map.301 = (bf16[1,512,1536]{2,1,0:T(8,128)(2,1)}, bf16[1,512,1536]{2,1,0:T(8,128)(2,1)}, f32[1,512,128]{2,1,0:T(8,128)}, bf16[8,2,208,1536]{3,2,1,0:T(8,1...) custom-call(s32[1]{0:T(128)} %bitcast.18.first_ref, ...), custom_call_target="tpu_custom_call" | custom-call | flops 6543114240 | bytes 19562496 | tf_op jit(solution)/shard_map/pallas_call | solution.py:243
  194.7 10.1 %collective-permute-done.1 = bf16[512,1536]{1,0:T(8,128)(2,1)} collective-permute-done((bf16[512,1536]{1,0:T(8,128)(2,1)S(1)}, bf16[512,1536]{1,0:T(8,128)(2,1)}, u32[]{:S(2)}, u32[]{:S(2)}) %collective-permute-start.1) | collective-permute-done | bytes 1572896 | tf_op jit(solution)/shard_map/ppermute | solution.py:82
  214.8 30.2 %shard_map.302 = (bf16[2,512,1536]{2,1,0:T(8,128)(2,1)}, bf16[2,512,1536]{2,1,0:T(8,128)(2,1)}, f32[2,512,128]{2,1,0:T(8,128)}, bf16[8,2,208,1536]{3,2,1,0:T(8,1...) custom-call(s32[1]{0:T(128)} %bitcast.18.first_ref, ...), custom_call_target="tpu_custom_call", output_to_operand_aliasing={{3}: (10, {}), {4}: (11, {}), {5}: (12, {}), {6}: (13, {}),... | custom-call | flops 13086228480 | bytes 39124992 | tf_op jit(solution)/shard_map/pallas_call | solution.py:243
  248.7 23.5 %collective-permute-done.5 = bf16[512,1536]{1,0:T(8,128)(2,1)} collective-permute-done((bf16[512,1536]{1,0:T(8,128)(2,1)}, bf16[512,1536]{1,0:T(8,128)(2,1)}, u32[]{:S(2)}, u32[]{:S(2)}) %collective-permute-start.5) | collective-permute-done | bytes 1572896 | tf_op jit(solution)/shard_map/ppermute | solution.py:82
  282.0 30.2 %shard_map.303 = (bf16[2,512,1536]{2,1,0:T(8,128)(2,1)}, bf16[2,512,1536]{2,1,0:T(8,128)(2,1)}, f32[2,512,128]{2,1,0:T(8,128)}, bf16[8,2,208,1536]{3,2,1,0:T(8,1...) custom-call(s32[1]{0:T(128)} %bitcast.18.first_ref, ...), custom_call_target="tpu_custom_call", output_to_operand_aliasing={{3}: (10, {}), {4}: (11, {}), {5}: (12, {}), {6}: (13, {}),... | custom-call | flops 13086228480 | bytes 39124992 | tf_op jit(solution)/shard_map/pallas_call | solution.py:243
  318.0 21.6 %collective-permute-done.9 = bf16[512,1536]{1,0:T(8,128)(2,1)} collective-permute-done((bf16[512,1536]{1,0:T(8,128)(2,1)}, bf16[512,1536]{1,0:T(8,128)(2,1)}, u32[]{:S(2)}, u32[]{:S(2)}) %collective-permute-start.9) | collective-permute-done | bytes 1572896 | tf_op jit(solution)/shard_map/ppermute | solution.py:82
  353.0 30.6 %shard_map.304 = (bf16[2,512,1536]{2,1,0:T(8,128)(2,1)}, bf16[2,512,1536]{2,1,0:T(8,128)(2,1)}, f32[2,512,128]{2,1,0:T(8,128)}, bf16[8,2,208,1536]{3,2,1,0:T(8,1...) custom-call(s32[1]{0:T(128)} %bitcast.18.first_ref, ...), custom_call_target="tpu_custom_call", output_to_operand_aliasing={{3}: (10, {}), {4}: (11, {}), {5}: (12, {}), {6}: (13, {}),... | custom-call | flops 13086228480 | bytes 39124992 | tf_op jit(solution)/shard_map/pallas_call | solution.py:243
  394.3 18.6 %shard_map.305 = (bf16[1,512,1536]{2,1,0:T(8,128)(2,1)}, bf16[1,512,1536]{2,1,0:T(8,128)(2,1)}, f32[1,512,128]{2,1,0:T(8,128)}, bf16[8,2,208,1536]{3,2,1,0:T(8,1...) custom-call(s32[1]{0:T(128)} %bitcast.18.first_ref, ...), custom_call_target="tpu_custom_call", output_to_operand_aliasing={{3}: (10, {}), {4}: (11, {}), {5}: (12, {}), {6}: (13, {}),... | custom-call | flops 6543114240 | bytes 19562496 | tf_op jit(solution)/shard_map/pallas_call | solution.py:243
  422.8 4.3 all-to-all-start
  432.8 11.0 %bitcast_convert_fusion.2 = bf16[2,1536,512]{2,1,0:T(8,128)(2,1)} fusion(bf16[8,2,208,1536]{3,2,1,0:T(8,128)(2,1)} %get-tuple-element.89, bf16[8,2,208,512]{3,2,1,0:T(8,128)(2,1)} %get-tuple-element.90), kind=kOutput, calls=%fused_computation.20 | convolution fusion | flops 5236064256 | bytes 16777216 | tf_op jit(solution)/shard_map/necd,necf->edf/dot_general | solution.py:437
  443.8 18.1 %collective-permute-done.24 = bf16[256,1536]{1,0:T(8,128)(2,1)S(1)} collective-permute-done((bf16[256,1536]{1,0:T(8,128)(2,1)S(1)}, bf16[256,1536]{1,0:T(8,128)(2,1)S(1)}, u32[]{:S(2)}, u32[]{:S(2)}) %collective-permute-start.24) | collective-permute-done | bytes 786464 | tf_op jit(solution)/shard_map/ppermute | solution.py:82
  473.3 7.3 bitcast_convert_fusion.1
  480.6 22.0 %collective-permute-done.29 = bf16[512,1536]{1,0:T(8,128)(2,1)S(1)} collective-permute-done((bf16[512,1536]{1,0:T(8,128)(2,1)}, bf16[512,1536]{1,0:T(8,128)(2,1)S(1)}, u32[]{:S(2)}, u32[]{:S(2)}) %collective-permute-start.29) | collective-permute-done | bytes 1572896 | tf_op jit(solution)/shard_map/ppermute | solution.py:82
  510.4 26.0 %collective-permute-done.21 = bf16[512,1536]{1,0:T(8,128)(2,1)} collective-permute-done((bf16[512,1536]{1,0:T(8,128)(2,1)}, bf16[512,1536]{1,0:T(8,128)(2,1)}, u32[]{:S(2)}, u32[]{:S(2)}) %collective-permute-start.21) | collective-permute-done | bytes 1572896 | tf_op jit(solution)/shard_map/ppermute | solution.py:82
  538.0 4.6 fusion.31
  544.7 7.5 bitcast_convert_fusion
  552.3 19.5 %collective-permute-done.26 = bf16[512,1536]{1,0:T(8,128)(2,1)} collective-permute-done((bf16[512,1536]{1,0:T(8,128)(2,1)}, bf16[512,1536]{1,0:T(8,128)(2,1)}, u32[]{:S(2)}, u32[]{:S(2)}) %collective-permute-start.26) | collective-permute-done | bytes 1572896 | tf_op jit(solution)/shard_map/ppermute | solution.py:82
  571.7 5.5 fusion.26
  579.3 26.2 %collective-permute-done.18 = bf16[512,1536]{1,0:T(8,128)(2,1)} collective-permute-done((bf16[512,1536]{1,0:T(8,128)(2,1)}, bf16[512,1536]{1,0:T(8,128)(2,1)}, u32[]{:S(2)}, u32[]{:S(2)}) %collective-permute-start.18) | collective-permute-done | bytes 1572896 | tf_op jit(solution)/shard_map/ppermute | solution.py:82
  605.5 4.6 fusion.32
  613.2 25.9 %collective-permute-done.27 = bf16[512,1536]{1,0:T(8,128)(2,1)} collective-permute-done((bf16[512,1536]{1,0:T(8,128)(2,1)}, bf16[512,1536]{1,0:T(8,128)(2,1)}, u32[]{:S(2)}, u32[]{:S(2)}) %collective-permute-start.27) | collective-permute-done | bytes 1572896 | tf_op jit(solution)/shard_map/ppermute | solution.py:82
  639.2 4.8 multiply_reduce_fusion
  644.0 24.6 %collective-permute-done.19 = bf16[512,1536]{1,0:T(8,128)(2,1)} collective-permute-done((bf16[512,1536]{1,0:T(8,128)(2,1)}, bf16[512,1536]{1,0:T(8,128)(2,1)}, u32[]{:S(2)}, u32[]{:S(2)}) %collective-permute-start.19) | collective-permute-done | bytes 1572896 | tf_op jit(solution)/shard_map/ppermute | solution.py:82
  668.6 4.4 fusion.20
  680.1 7.2 convolution_convert_fusion.1
  687.4 21.3 %fusion = (f32[8,3,512]{2,1,0:T(4,128)S(1)}, f32[8,512,512,3]{2,1,3,0:T(8,128)}) fusion(f32[8,512,512,3]{2,1,3,0:T(8,128)} %get-tuple-element.256, f32[8,3,512]{2,1,0:T(4,128)S(1)} %copy-done.43, pred[512,512]{0,1:T(8,128)(4,1)S(1)} %copy-done.15, bf16[512,8,64,1]{0,2,3,1:T(8,128)(2,1)S(1)} %bitcast.322, bf16[512,8,3,64]{0,3,2,1:T(8,128)(2,1)S(1)} %bitcast.309), kind=kOutput, calls=%fused_computation.6 | convolution fusion | flops 836751360 | bytes 52789248 | tf_op jit(solution)/shard_map/qhgd,khd->hgqk/dot_general | solution.py:472
  708.8 22.5 %fusion.2 = bf16[8,3,512,512]{2,3,1,0:T(8,128)(2,1)} fusion(f32[8,512,512,3]{2,1,3,0:T(8,128)} %get-tuple-element.264, f32[8,512,512,3]{2,1,3,0:T(8,128)} %get-tuple-element.256, f32[8,3,512]{2,1,0:T(4,128)S(1)} %get-tuple-element.263, f32[8,3,512]{2,1,0:T(4,128)S(1)} %copy-done.43, pred[512,512]{0,1:T(8,128)(4,1)S(1)} %copy-done.15), kind=kLoop, calls=%fused_computation.8 | loop fusion | flops 37748736 | bytes 63275008 | tf_op jit(solution)/shard_map/convert_element_type | solution.py:476
  731.6 8.7 fusion.50
  740.6 7.1 multiply_bitcast_fusion
  749.6 12.2 %fusion.51 = bf16[8,64,512]{2,1,0:T(8,128)(2,1)S(1)} fusion(bf16[512,8,3,64]{0,3,2,1:T(8,128)(2,1)S(1)} %bitcast.310, f32[8,512,512,3]{2,1,3,0:T(8,128)} %get-tuple-element.256, f32[8,3,512]{2,1,0:T(4,128)S(1)} %copy-done.43, pred[512,512]{0,1:T(8,128)(4,1)S(1)} %copy-done.15), kind=kOutput, calls=%fused_computation.114 | convolution fusion | flops 830734336 | bytes 27574272 | tf_op jit(solution)/shard_map/hgqk,qhgd->khd/dot_general | solution.py:468
  761.9 8.4 fusion.15
  770.6 8.1 convolution_convert_fusion
  778.8 13.2 %concatenate.56 = bf16[1536,2688]{1,0:T(8,128)(2,1)} concatenate(bf16[1536,2560]{1,0:T(8,128)(2,1)} %convolution_convert_fusion, bf16[1536,16]{1,0:T(8,128)(2,1)S(1)} %copy.172, bf16[1536,1]{1,0:T(8,128)(2,1)S(1)} %broadcast_in_dim.159, bf16[1536,1]{1,0:T(8,128)(2,1)S(1)} %broadcast_in_dim.160, bf16[1536,110]{1,0:T(8,128)(2,1)S(1)} %broadcast_in_dim.156), dimensions={1} | concatenate | bytes 16515072 | tf_op jit(solution)/shard_map/concatenate | solution.py:507
  792.1 5.7 convert_element_type.394
  801.4 4.1 convert_element_type.398
  808.7 27.0 %reduce-scatter.5.cloned.1.call-done = bf16[48,1536]{1,0:T(8,128)(2,1)} async-done(((bf16[1536,1536]{1,0:T(8,128)(2,1)}), bf16[48,1536]{1,0:T(8,128)(2,1)}) %reduce-scatter.5.cloned.1.call-update) | async-done | bytes 147472 | tf_op jit(solution)/shard_map/reduce_scatter | solution.py:453
  835.7 7.8 all_gather.23
  844.6 127.2 %reduce-scatter.3.cloned.1.call-done = bf16[48,2688]{1,0:T(8,128)(2,1)} async-done(((bf16[1536,2688]{1,0:T(8,128)(2,1)}), bf16[48,2688]{1,0:T(8,128)(2,1)}) %reduce-scatter.3.cloned.1.call-update) | async-done | bytes 258064 | tf_op jit(solution)/shard_map/reduce_scatter | solution.py:453
  971.8 10.1 %all_gather.22 = bf16[192,2688]{1,0:T(8,128)(2,1)S(1)} all-gather(bf16[48,2688]{1,0:T(8,128)(2,1)} %reduce-scatter.3.cloned.1.call-done), channel_id=1, replica_groups=mesh['rep'=4,'fsdp'=8] {'rep'}, dimensions={0}, use_global_device_ids=true | all-gather | bytes 1290240 | tf_op jit(solution)/shard_map/all_gather | solution.py:454
  (330 shorter events, 162.5 us)
Async XLA Ops:
  7.3 85.3 %all-gather.4.cloned.1.call-start = ((), (), s32[]{:S(2)}) async-start(), calls=%async_computation.3 | async-start | bytes 8515584 | tf_op jit(solution)/shard_map/all_gather | solution.py:344
  12.7 149.1 %all-gather.6.cloned.1.call-start = ((), (), s32[]{:S(2)}) async-start(), calls=%async_computation.4 | async-start | bytes 4866048 | tf_op jit(solution)/shard_map/all_gather | solution.py:344
  17.4 43.9 %copy-start.58 = (pred[512]{0:T(512)(128)(4,1)}, pred[512]{0:T(512)(128)(4,1)S(1)}, u32[]{:S(2)}) copy-start(pred[512]{0:T(512)(128)(4,1)S(1)} %iota_compare_fusion.4) | copy-start | bytes 1540
  19.2 120.1 %copy-start.54 = (f32[512]{0:T(512)}, f32[512]{0:T(512)S(1)}, u32[]{:S(2)}) copy-start(f32[512]{0:T(512)S(1)} %fusion.81) | copy-start | bytes 6148
  61.3 55.6 %copy-start.32 = (f32[512,32]{0,1:T(8,128)}, f32[512,32]{0,1:T(8,128)S(1)}, u32[]{:S(2)}) copy-start(f32[512,32]{0,1:T(8,128)S(1)} %get-tuple-element.252) | copy-start | bytes 196612
  61.4 80.4 %copy-start.14 = (pred[512,512]{0,1:T(8,128)(4,1)}, pred[512,512]{0,1:T(8,128)(4,1)S(1)}, u32[]{:S(2)}) copy-start(pred[512,512]{0,1:T(8,128)(4,1)S(1)} %fusion.55) | copy-start | bytes 786436
  92.6 100.1 %collective-permute-start.3 = (bf16[512,1536]{1,0:T(8,128)(2,1)}, bf16[512,1536]{1,0:T(8,128)(2,1)}, u32[]{:S(2)}, u32[]{:S(2)}) collective-permute-start(bf16[512,1536]{1,0:T(8,128)(2,1)} %bitcast.319), channel_id=1, source_target_pairs={{0,1},{2,0},{4,2},{6,4},{7,6},{5,7},{3,5},{1,3},{8,9},{10,8},{12,1... | collective-permute-start | bytes 4718600 | tf_op jit(solution)/shard_map/ppermute | solution.py:82
  94.0 100.1 %collective-permute-start.2 = (bf16[512,1536]{1,0:T(8,128)(2,1)}, bf16[512,1536]{1,0:T(8,128)(2,1)}, u32[]{:S(2)}, u32[]{:S(2)}) collective-permute-start(bf16[512,1536]{1,0:T(8,128)(2,1)} %bitcast.320), channel_id=1, source_target_pairs={{0,2},{2,4},{4,6},{6,7},{7,5},{5,3},{3,1},{1,0},{8,10},{10,12},{12... | collective-permute-start | bytes 4718600 | tf_op jit(solution)/shard_map/ppermute | solution.py:82
  167.4 37.4 %collective-permute-start.1 = (bf16[512,1536]{1,0:T(8,128)(2,1)S(1)}, bf16[512,1536]{1,0:T(8,128)(2,1)}, u32[]{:S(2)}, u32[]{:S(2)}) collective-permute-start(bf16[512,1536]{1,0:T(8,128)(2,1)S(1)} %multiply_convert_fusion), channel_id=1, source_target_pairs={{0,1},{2,0},{4,2},{6,4},{7,6},{5,7},{3,5},{1,3},{8,9},{10,8},{12,1... | collective-permute-start | bytes 4718600 | tf_op jit(solution)/shard_map/ppermute | solution.py:82
  168.9 41.3 %collective-permute-start = (bf16[512,1536]{1,0:T(8,128)(2,1)S(1)}, bf16[512,1536]{1,0:T(8,128)(2,1)}, u32[]{:S(2)}, u32[]{:S(2)}) collective-permute-start(bf16[512,1536]{1,0:T(8,128)(2,1)S(1)} %multiply_convert_fusion), channel_id=1, source_target_pairs={{0,2},{2,4},{4,6},{6,7},{7,5},{5,3},{3,1},{1,0},{8,10},{10,12},{12... | collective-permute-start | bytes 4718600 | tf_op jit(solution)/shard_map/ppermute | solution.py:82
  192.7 54.0 %collective-permute-start.7 = (bf16[512,1536]{1,0:T(8,128)(2,1)}, bf16[512,1536]{1,0:T(8,128)(2,1)}, u32[]{:S(2)}, u32[]{:S(2)}) collective-permute-start(bf16[512,1536]{1,0:T(8,128)(2,1)} %collective-permute-done.3), channel_id=1, source_target_pairs={{0,1},{2,0},{4,2},{6,4},{7,6},{5,7},{3,5},{1,3},{8,9},{10,8},{12,1... | collective-permute-start | bytes 4718600 | tf_op jit(solution)/shard_map/ppermute | solution.py:82
  194.2 54.0 %collective-permute-start.6 = (bf16[512,1536]{1,0:T(8,128)(2,1)}, bf16[512,1536]{1,0:T(8,128)(2,1)}, u32[]{:S(2)}, u32[]{:S(2)}) collective-permute-start(bf16[512,1536]{1,0:T(8,128)(2,1)} %collective-permute-done.2), channel_id=1, source_target_pairs={{0,2},{2,4},{4,6},{6,7},{7,5},{5,3},{3,1},{1,0},{8,10},{10,12},{12... | collective-permute-start | bytes 4718600 | tf_op jit(solution)/shard_map/ppermute | solution.py:82
  204.8 67.4 %collective-permute-start.5 = (bf16[512,1536]{1,0:T(8,128)(2,1)}, bf16[512,1536]{1,0:T(8,128)(2,1)}, u32[]{:S(2)}, u32[]{:S(2)}) collective-permute-start(bf16[512,1536]{1,0:T(8,128)(2,1)} %collective-permute-done.1), channel_id=1, source_target_pairs={{0,1},{2,0},{4,2},{6,4},{7,6},{5,7},{3,5},{1,3},{8,9},{10,8},{12,1... | collective-permute-start | bytes 4718600 | tf_op jit(solution)/shard_map/ppermute | solution.py:82
  214.2 63.3 %collective-permute-start.4 = (bf16[512,1536]{1,0:T(8,128)(2,1)}, bf16[512,1536]{1,0:T(8,128)(2,1)}, u32[]{:S(2)}, u32[]{:S(2)}) collective-permute-start(bf16[512,1536]{1,0:T(8,128)(2,1)} %collective-permute-done), channel_id=1, source_target_pairs={{0,2},{2,4},{4,6},{6,7},{7,5},{5,3},{3,1},{1,0},{8,10},{10,12},{12... | collective-permute-start | bytes 4718600 | tf_op jit(solution)/shard_map/ppermute | solution.py:82
  246.6 67.2 %collective-permute-start.11 = (bf16[512,1536]{1,0:T(8,128)(2,1)}, bf16[512,1536]{1,0:T(8,128)(2,1)S(1)}, u32[]{:S(2)}, u32[]{:S(2)}) collective-permute-start(bf16[512,1536]{1,0:T(8,128)(2,1)} %collective-permute-done.7), channel_id=1, source_target_pairs={{0,1},{2,0},{4,2},{6,4},{7,6},{5,7},{3,5},{1,3},{8,9},{10,8},{12,1... | collective-permute-start | bytes 4718600 | tf_op jit(solution)/shard_map/ppermute | solution.py:82
  248.1 67.3 %collective-permute-start.10 = (bf16[512,1536]{1,0:T(8,128)(2,1)}, bf16[512,1536]{1,0:T(8,128)(2,1)}, u32[]{:S(2)}, u32[]{:S(2)}) collective-permute-start(bf16[512,1536]{1,0:T(8,128)(2,1)} %collective-permute-done.6), channel_id=1, source_target_pairs={{0,2},{2,4},{4,6},{6,7},{7,5},{5,3},{3,1},{1,0},{8,10},{10,12},{12... | collective-permute-start | bytes 4718600 | tf_op jit(solution)/shard_map/ppermute | solution.py:82
  272.2 67.4 %collective-permute-start.9 = (bf16[512,1536]{1,0:T(8,128)(2,1)}, bf16[512,1536]{1,0:T(8,128)(2,1)}, u32[]{:S(2)}, u32[]{:S(2)}) collective-permute-start(bf16[512,1536]{1,0:T(8,128)(2,1)} %collective-permute-done.5), channel_id=1, source_target_pairs={{0,1},{2,0},{4,2},{6,4},{7,6},{5,7},{3,5},{1,3},{8,9},{10,8},{12,1... | collective-permute-start | bytes 4718600 | tf_op jit(solution)/shard_map/ppermute | solution.py:82
  277.5 65.7 %collective-permute-start.8 = (bf16[512,1536]{1,0:T(8,128)(2,1)}, bf16[512,1536]{1,0:T(8,128)(2,1)}, u32[]{:S(2)}, u32[]{:S(2)}) collective-permute-start(bf16[512,1536]{1,0:T(8,128)(2,1)} %collective-permute-done.4), channel_id=1, source_target_pairs={{0,2},{2,4},{4,6},{6,7},{7,5},{5,3},{3,1},{1,0},{8,10},{10,12},{12... | collective-permute-start | bytes 4718600 | tf_op jit(solution)/shard_map/ppermute | solution.py:82
  313.9 75.2 %collective-permute-start.15 = (bf16[256,1536]{1,0:T(8,128)(2,1)S(1)}, bf16[256,1536]{1,0:T(8,128)(2,1)}, u32[]{:S(2)}, u32[]{:S(2)}) collective-permute-start(bf16[256,1536]{1,0:T(8,128)(2,1)S(1)} %slice.309), channel_id=1, source_target_pairs={{0,1},{2,0},{4,2},{6,4},{7,6},{5,7},{3,5},{1,3},{8,9},{10,8},{12,1... | collective-permute-start | bytes 2359304 | tf_op jit(solution)/shard_map/ppermute | solution.py:82
  317.5 71.5 %collective-permute-start.14 = (bf16[256,1536]{1,0:T(8,128)(2,1)}, bf16[256,1536]{1,0:T(8,128)(2,1)}, u32[]{:S(2)}, u32[]{:S(2)}) collective-permute-start(bf16[256,1536]{1,0:T(8,128)(2,1)} %slice.308), channel_id=1, source_target_pairs={{0,2},{2,4},{4,6},{6,7},{7,5},{5,3},{3,1},{1,0},{8,10},{10,12},{12... | collective-permute-start | bytes 2359304 | tf_op jit(solution)/shard_map/ppermute | solution.py:82
  341.7 50.0 %collective-permute-start.13 = (bf16[256,1536]{1,0:T(8,128)(2,1)}, bf16[256,1536]{1,0:T(8,128)(2,1)}, u32[]{:S(2)}, u32[]{:S(2)}) collective-permute-start(bf16[256,1536]{1,0:T(8,128)(2,1)} %slice.307), channel_id=1, source_target_pairs={{0,1},{2,0},{4,2},{6,4},{7,6},{5,7},{3,5},{1,3},{8,9},{10,8},{12,1... | collective-permute-start | bytes 2359304 | tf_op jit(solution)/shard_map/ppermute | solution.py:82
  345.2 46.4 %collective-permute-start.12 = (bf16[256,1536]{1,0:T(8,128)(2,1)}, bf16[256,1536]{1,0:T(8,128)(2,1)}, u32[]{:S(2)}, u32[]{:S(2)}) collective-permute-start(bf16[256,1536]{1,0:T(8,128)(2,1)} %slice.306), channel_id=1, source_target_pairs={{0,2},{2,4},{4,6},{6,7},{7,5},{5,3},{3,1},{1,0},{8,10},{10,12},{12... | collective-permute-start | bytes 2359304 | tf_op jit(solution)/shard_map/ppermute | solution.py:82
  422.8 129.5 %all-to-all-start = ((f32[8,2,512]{2,1,0:T(2,128)}), f32[8,2,512]{2,1,0:T(2,128)S(1)}, u32[]{:S(2)}, u32[]{:S(2)}) async-start(f32[8,2,512]{2,1,0:T(2,128)} %gather_fusion.3), calls=%async_computation | async-start | bytes 65536 | tf_op jit(solution)/shard_map/all_to_all | solution.py:430
  427.1 365.0 %all-reduce.4.cloned.1.call-start = ((), (), s32[]{:S(2)}) async-start(), calls=%async_computation.7 | async-start | bytes 18874368 | tf_op jit(solution)/shard_map/psum | solution.py:439
  427.1 41.2 %collective-permute-start.16 = (bf16[256,1536]{1,0:T(8,128)(2,1)}, bf16[256,1536]{1,0:T(8,128)(2,1)S(1)}, u32[]{:S(2)}, u32[]{:S(2)}) collective-permute-start(bf16[256,1536]{1,0:T(8,128)(2,1)} %get-tuple-element.242), channel_id=1, source_target_pairs={{0,2},{2,4},{4,6},{6,7},{7,5},{5,3},{3,1},{1,0},{8,10},{10,12},{12... | collective-permute-start | bytes 2359304 | tf_op jit(solution)/shard_map/ppermute | solution.py:82
  429.1 39.2 %collective-permute-start.20 = (bf16[256,1536]{1,0:T(8,128)(2,1)}, bf16[256,1536]{1,0:T(8,128)(2,1)S(1)}, u32[]{:S(2)}, u32[]{:S(2)}) collective-permute-start(bf16[256,1536]{1,0:T(8,128)(2,1)} %get-tuple-element.243), channel_id=1, source_target_pairs={{0,1},{2,0},{4,2},{6,4},{7,6},{5,7},{3,5},{1,3},{8,9},{10,8},{12,1... | collective-permute-start | bytes 2359304 | tf_op jit(solution)/shard_map/ppermute | solution.py:82
  430.7 31.3 %collective-permute-start.24 = (bf16[256,1536]{1,0:T(8,128)(2,1)S(1)}, bf16[256,1536]{1,0:T(8,128)(2,1)S(1)}, u32[]{:S(2)}, u32[]{:S(2)}) collective-permute-start(bf16[256,1536]{1,0:T(8,128)(2,1)S(1)} %get-tuple-element.240), channel_id=1, source_target_pairs={{0,2},{2,4},{4,6},{6,7},{7,5},{5,3},{3,1},{1,0},{8,10},{10,12},{12... | collective-permute-start | bytes 2359304 | tf_op jit(solution)/shard_map/ppermute | solution.py:82
  432.7 30.7 %collective-permute-start.28 = (bf16[256,1536]{1,0:T(8,128)(2,1)S(1)}, bf16[256,1536]{1,0:T(8,128)(2,1)S(1)}, u32[]{:S(2)}, u32[]{:S(2)}) collective-permute-start(bf16[256,1536]{1,0:T(8,128)(2,1)S(1)} %get-tuple-element.241), channel_id=1, source_target_pairs={{0,1},{2,0},{4,2},{6,4},{7,6},{5,7},{3,5},{1,3},{8,9},{10,8},{12,1... | collective-permute-start | bytes 2359304 | tf_op jit(solution)/shard_map/ppermute | solution.py:82
  465.1 37.5 %collective-permute-start.29 = (bf16[512,1536]{1,0:T(8,128)(2,1)}, bf16[512,1536]{1,0:T(8,128)(2,1)S(1)}, u32[]{:S(2)}, u32[]{:S(2)}) collective-permute-start(bf16[512,1536]{1,0:T(8,128)(2,1)} %pad_maximum_fusion.11), channel_id=1, source_target_pairs={{0,1},{2,0},{4,2},{6,4},{7,6},{5,7},{3,5},{1,3},{8,9},{10,8},{12,1... | collective-permute-start | bytes 4718600 | tf_op jit(solution)/shard_map/ppermute | solution.py:82
  466.7 37.6 %collective-permute-start.25 = (bf16[512,1536]{1,0:T(8,128)(2,1)}, bf16[512,1536]{1,0:T(8,128)(2,1)}, u32[]{:S(2)}, u32[]{:S(2)}) collective-permute-start(bf16[512,1536]{1,0:T(8,128)(2,1)} %pad_maximum_fusion.10), channel_id=1, source_target_pairs={{0,2},{2,4},{4,6},{6,7},{7,5},{5,3},{3,1},{1,0},{8,10},{10,12},{12... | collective-permute-start | bytes 4718600 | tf_op jit(solution)/shard_map/ppermute | solution.py:82
  470.0 66.4 %collective-permute-start.21 = (bf16[512,1536]{1,0:T(8,128)(2,1)}, bf16[512,1536]{1,0:T(8,128)(2,1)}, u32[]{:S(2)}, u32[]{:S(2)}) collective-permute-start(bf16[512,1536]{1,0:T(8,128)(2,1)} %pad_maximum_fusion.9), channel_id=1, source_target_pairs={{0,1},{2,0},{4,2},{6,4},{7,6},{5,7},{3,5},{1,3},{8,9},{10,8},{12,1... | collective-permute-start | bytes 4718600 | tf_op jit(solution)/shard_map/ppermute | solution.py:82
  471.9 66.1 %collective-permute-start.17 = (bf16[512,1536]{1,0:T(8,128)(2,1)}, bf16[512,1536]{1,0:T(8,128)(2,1)}, u32[]{:S(2)}, u32[]{:S(2)}) collective-permute-start(bf16[512,1536]{1,0:T(8,128)(2,1)} %pad_maximum_fusion.8), channel_id=1, source_target_pairs={{0,2},{2,4},{4,6},{6,7},{7,5},{5,3},{3,1},{1,0},{8,10},{10,12},{12... | collective-permute-start | bytes 4718600 | tf_op jit(solution)/shard_map/ppermute | solution.py:82
  473.3 31.0 %copy-start.26 = (bf16[2,512,1536]{2,1,0:T(8,128)(2,1)S(1)}, bf16[2,512,1536]{2,1,0:T(8,128)(2,1)}, u32[]{:S(2)}) copy-start(bf16[2,512,1536]{2,1,0:T(8,128)(2,1)} %get-tuple-element.81) | copy-start | bytes 9437188
  473.3 64.7 %copy-start.25 = (bf16[2,512,1536]{2,1,0:T(8,128)(2,1)S(1)}, bf16[2,512,1536]{2,1,0:T(8,128)(2,1)}, u32[]{:S(2)}) copy-start(bf16[2,512,1536]{2,1,0:T(8,128)(2,1)} %get-tuple-element.66) | copy-start | bytes 9437188
  504.3 40.3 %slice-start.3 = ((s8[10223616]{0:T(1024)(128)(4,1)}), s8[4194304]{0:T(1024)(128)(4,1)S(1)}, s32[]{:S(2)}) async-start(s8[10223616]{0:T(1024)(128)(4,1)} %bitcast.304), calls=%async_computation.11 | async-start | bytes 8388608
  504.3 40.3 %slice-start.4 = ((s8[10223616]{0:T(1024)(128)(4,1)}), s8[4194304]{0:T(1024)(128)(4,1)S(1)}, s32[]{:S(2)}) async-start(s8[10223616]{0:T(1024)(128)(4,1)} %bitcast.304), calls=%async_computation.12 | async-start | bytes 8388608
  508.4 63.3 %collective-permute-start.26 = (bf16[512,1536]{1,0:T(8,128)(2,1)}, bf16[512,1536]{1,0:T(8,128)(2,1)}, u32[]{:S(2)}, u32[]{:S(2)}) collective-permute-start(bf16[512,1536]{1,0:T(8,128)(2,1)} %get-tuple-element.226), channel_id=1, source_target_pairs={{0,2},{2,4},{4,6},{6,7},{7,5},{5,3},{3,1},{1,0},{8,10},{10,12},{12... | collective-permute-start | bytes 4718600 | tf_op jit(solution)/shard_map/ppermute | solution.py:82
  510.1 61.7 %collective-permute-start.30 = (bf16[512,1536]{1,0:T(8,128)(2,1)}, bf16[512,1536]{1,0:T(8,128)(2,1)}, u32[]{:S(2)}, u32[]{:S(2)}) collective-permute-start(bf16[512,1536]{1,0:T(8,128)(2,1)} %get-tuple-element.227), channel_id=1, source_target_pairs={{0,1},{2,0},{4,2},{6,4},{7,6},{5,7},{3,5},{1,3},{8,9},{10,8},{12,1... | collective-permute-start | bytes 4718600 | tf_op jit(solution)/shard_map/ppermute | solution.py:82
  542.6 62.8 %collective-permute-start.18 = (bf16[512,1536]{1,0:T(8,128)(2,1)}, bf16[512,1536]{1,0:T(8,128)(2,1)}, u32[]{:S(2)}, u32[]{:S(2)}) collective-permute-start(bf16[512,1536]{1,0:T(8,128)(2,1)} %get-tuple-element.234), channel_id=1, source_target_pairs={{0,2},{2,4},{4,6},{6,7},{7,5},{5,3},{3,1},{1,0},{8,10},{10,12},{12... | collective-permute-start | bytes 4718600 | tf_op jit(solution)/shard_map/ppermute | solution.py:82
  544.3 61.2 %collective-permute-start.22 = (bf16[512,1536]{1,0:T(8,128)(2,1)}, bf16[512,1536]{1,0:T(8,128)(2,1)}, u32[]{:S(2)}, u32[]{:S(2)}) collective-permute-start(bf16[512,1536]{1,0:T(8,128)(2,1)} %get-tuple-element.235), channel_id=1, source_target_pairs={{0,1},{2,0},{4,2},{6,4},{7,6},{5,7},{3,5},{1,3},{8,9},{10,8},{12,1... | collective-permute-start | bytes 4718600 | tf_op jit(solution)/shard_map/ppermute | solution.py:82
  552.2 283.5 %reduce-scatter.5.cloned.1.call-start = ((), (), s32[]{:S(2)}) async-start(), calls=%async_computation.6 | async-start | bytes 4866048 | tf_op jit(solution)/shard_map/reduce_scatter | solution.py:453
  571.7 33.7 %copy-start.24 = (bf16[2,512,1536]{2,1,0:T(8,128)(2,1)S(1)}, bf16[2,512,1536]{2,1,0:T(8,128)(2,1)}, u32[]{:S(2)}) copy-start(bf16[2,512,1536]{2,1,0:T(8,128)(2,1)} %get-tuple-element.60) | copy-start | bytes 9437188
  577.2 61.9 %collective-permute-start.27 = (bf16[512,1536]{1,0:T(8,128)(2,1)}, bf16[512,1536]{1,0:T(8,128)(2,1)}, u32[]{:S(2)}, u32[]{:S(2)}) collective-permute-start(bf16[512,1536]{1,0:T(8,128)(2,1)} %get-tuple-element.224), channel_id=1, source_target_pairs={{0,2},{2,4},{4,6},{6,7},{7,5},{5,3},{3,1},{1,0},{8,10},{10,12},{12... | collective-permute-start | bytes 4718600 | tf_op jit(solution)/shard_map/ppermute | solution.py:82
  578.9 60.3 %collective-permute-start.31 = (bf16[512,1536]{1,0:T(8,128)(2,1)}, bf16[512,1536]{1,0:T(8,128)(2,1)}, u32[]{:S(2)}, u32[]{:S(2)}) collective-permute-start(bf16[512,1536]{1,0:T(8,128)(2,1)} %get-tuple-element.225), channel_id=1, source_target_pairs={{0,1},{2,0},{4,2},{6,4},{7,6},{5,7},{3,5},{1,3},{8,9},{10,8},{12,1... | collective-permute-start | bytes 4718600 | tf_op jit(solution)/shard_map/ppermute | solution.py:82
  610.0 58.5 %collective-permute-start.19 = (bf16[512,1536]{1,0:T(8,128)(2,1)}, bf16[512,1536]{1,0:T(8,128)(2,1)}, u32[]{:S(2)}, u32[]{:S(2)}) collective-permute-start(bf16[512,1536]{1,0:T(8,128)(2,1)} %get-tuple-element.232), channel_id=1, source_target_pairs={{0,2},{2,4},{4,6},{6,7},{7,5},{5,3},{3,1},{1,0},{8,10},{10,12},{12... | collective-permute-start | bytes 4718600 | tf_op jit(solution)/shard_map/ppermute | solution.py:82
  611.6 56.9 %collective-permute-start.23 = (bf16[512,1536]{1,0:T(8,128)(2,1)}, bf16[512,1536]{1,0:T(8,128)(2,1)}, u32[]{:S(2)}, u32[]{:S(2)}) collective-permute-start(bf16[512,1536]{1,0:T(8,128)(2,1)} %get-tuple-element.233), channel_id=1, source_target_pairs={{0,1},{2,0},{4,2},{6,4},{7,6},{5,7},{3,5},{1,3},{8,9},{10,8},{12,1... | collective-permute-start | bytes 4718600 | tf_op jit(solution)/shard_map/ppermute | solution.py:82
  639.2 35.5 %slice-start.10 = ((s8[4718592]{0:T(1024)(128)(4,1)}), s8[4194304]{0:T(1024)(128)(4,1)S(1)}, s32[]{:S(2)}) async-start(s8[4718592]{0:T(1024)(128)(4,1)} %bitcast.326), calls=%async_computation.18 | async-start | bytes 8388608
  708.8 263.1 %reduce-scatter.3.cloned.1.call-start = ((), (), s32[]{:S(2)}) async-start(), calls=%async_computation.5 | async-start | bytes 8515584 | tf_op jit(solution)/shard_map/reduce_scatter | solution.py:453
  (66 other events, 697.3 us)
Sparse Core Ops, SparseCore 0:
  12.8 79.6 all-gather.3
  96.0 65.6 all-gather.5
  552.3 170.8 all-reduce.3
  728.6 107.0 reduce-scatter.4
  842.4 129.3 reduce-scatter.2

commit v2 on v1

--- a/solution.py
+++ b/solution.py
@@ -15,6 +15,7 @@
 F32 = jnp.float32
 ALL = ("fsdp", "rep")
 SMALL = 128
+LIGHT = pl.CostEstimate(flops=1000, bytes_accessed=1000, transcendentals=0)
 
 
 def rms_scale(value_rows, gain_vec):
@@ -29,24 +30,6 @@
     )
     angles = jnp.arange(expert_slot_count, dtype=jnp.float32)[:, None] * frequency[None, :]
     return (jnp.cos(angles), jnp.sin(angles))
-
-
-def rotary_apply(value_rows, cosine_table, sine_table):
-    half_dim = value_rows.shape[-1] // 2
-    extra_dims = (1,) * (value_rows.ndim - 2)
-    cosine_table = cosine_table.reshape(
-        cosine_table.shape[:1] + extra_dims + cosine_table.shape[1:]
-    )
-    sine_table = sine_table.reshape(sine_table.shape[:1] + extra_dims + sine_table.shape[1:])
-    first_half = value_rows[..., :half_dim]
-    second = value_rows[..., half_dim:]
-    return jnp.concatenate(
-        [
-            first_half * cosine_table - second * sine_table,
-            second * cosine_table + first_half * sine_table,
-        ],
-        axis=-1,
-    )
 
 
 def slot_table(choices_row, length, experts, capacity):
@@ -77,22 +60,50 @@
     return list(range(0, size, 2)) + list(range(size - 1, 0, -2))
 
 
+def tie(values, deps):
+    anywhere = pl.BlockSpec(memory_space=pl.ANY)
+    return pl.pallas_call(
+        lambda *refs: None,
+        out_shape=[jax.ShapeDtypeStruct(v.shape, v.dtype) for v in values],
+        in_specs=[anywhere] * (len(values) + len(deps)),
+        out_specs=[anywhere] * len(values),
+        input_output_aliases={i: i for i in range(len(values))},
+        cost_estimate=LIGHT,
+    )(*values, *deps)
+
+
+def swap(value, axis, bit):
+    size = lax.axis_size(axis)
+    return lax.ppermute(value, axis, [(i, i ^ bit) for i in range(size)])
+
+
 def shift(value, order, step):
     size = len(order)
     return lax.ppermute(value, "fsdp", [(order[i], order[(i + step) % size]) for i in range(size)])
 
 
-def ring_gather(value, order):
+def ring_start(value, order, steps):
+    found = {0: value}
+    for step in range(1, min(steps, (len(order) - 1) // 2) + 1):
+        found[-step] = shift(found[1 - step], order, 1)
+        found[step] = shift(found[step - 1], order, -1)
+    return found
+
+
+def ring_finish(found, order, deps):
     size = len(order)
-    found = {0: value}
-    ahead = back = value
-    for step in range(1, (size - 1) // 2 + 1):
+    found = dict(found)
+    reach = max(found)
+    back, ahead = found[-reach], found[reach]
+    if deps:
+        back, ahead = tie([back, ahead], deps)
+    for step in range(reach + 1, (size - 1) // 2 + 1):
         back = shift(back, order, 1)
         ahead = shift(ahead, order, -1)
         found[-step] = back
         found[step] = ahead
     if size % 2 == 0:
-        half = value.shape[0] // 2
+        half = back.shape[0] // 2
         top = shift(back[:half], order, 1)
         bottom = shift(ahead[half:], order, -1)
         found[size // 2] = jnp.concatenate([top, bottom], axis=0)
@@ -116,13 +127,15 @@
         back = jnp.concatenate([back[:half], add_low(back[half:], bottom)], axis=0)
     else:
         ahead, back = parts[near], parts[-near]
+    stages = [[ahead, back]]
     for step in range(near, 0, -1):
         ahead = shift(ahead, order, 1)
         back = shift(back, order, -1)
         if step > 1:
             ahead = add_low(parts[step - 1], ahead)
             back = add_low(parts[1 - step], back)
-    return ahead, back
+        stages.append([ahead, back])
+    return ahead, back, stages
 
 
 def three_way(value):
@@ -139,6 +152,292 @@
 
 def dot_nt(left, right):
     return lax.dot_general(left, right, (((1,), (1,)), ((), ())), preferred_element_type=F32)
+
+
+def dot_tn(left, right):
+    return lax.dot_general(left, right, (((0,), (0,)), ((), ())), preferred_element_type=F32)
+
+
+def tile_rotate(value, cosine, sine_left, sine_right):
+    tiles = []
+    for start in range(0, value.shape[1], SMALL):
+        tile = value[:, start : start + SMALL]
+        ahead = pltpu.roll(tile, SMALL - HEAD_SIZE // 2, axis=1)
+        behind = pltpu.roll(tile, HEAD_SIZE // 2, axis=1)
+        tiles.append(tile * cosine + ahead * sine_left + behind * sine_right)
+    return jnp.concatenate(tiles, axis=1)
+
+
+def half_variants(tile):
+    lanes = lax.broadcasted_iota(jnp.int32, tile.shape, 1)
+    wide = tile.astype(F32)
+    turned = pltpu.roll(wide, HEAD_SIZE, axis=1)
+    pick = lambda source, half: jnp.where((lanes >= HEAD_SIZE) == (half == 1), source, 0.0).astype(BF16)
+    return {(c, a): pick(wide if c == a else turned, a) for c in range(2) for a in range(2)}
+
+
+def row_blocks(slots):
+    size = min(256, slots)
+    return [(start, size, start + size) for start in range(0, slots, size)]
+
+
+def allowed_block(start, size, keys, length):
+    query = start + lax.broadcasted_iota(jnp.int32, (size, keys), 0)
+    key = lax.broadcasted_iota(jnp.int32, (size, keys), 1)
+    return (key <= query) & (key < length)
+
+
+def attention_kernel(
+    length_ref, x_ref, wq_ref, wk_ref, wv_ref, cos_ref, left_ref, right_ref, *rest
+):
+    q_ref, k_ref, v_ref, mixed_ref, lse_ref = rest[-5:]
+    x = x_ref[...]
+    slots = x.shape[0]
+    tables = (cos_ref[...], left_ref[...], right_ref[...])
+    q = tile_rotate(dot_nn(x, wq_ref[...]), *tables).astype(BF16)
+    k = tile_rotate(dot_nn(x, wk_ref[...]), *tables).astype(BF16)
+    v = dot_nn(x, wv_ref[...]).astype(BF16)
+    q_ref[...] = q
+    k_ref[...] = k
+    v_ref[...] = v
+    keys, values = half_variants(k), half_variants(v)
+    heads = q.shape[1] // HEAD_SIZE
+    group = heads // 2
+    scale = 1.0 / math.sqrt(HEAD_SIZE)
+    for start, size, seen in row_blocks(slots):
+        allowed = allowed_block(start, size, seen, length_ref[0])
+        lanes = lax.broadcasted_iota(jnp.int32, (size, SMALL), 1)
+        lse = jnp.zeros((size, SMALL), F32)
+        for tile in range(heads // 2):
+            q_tile = q[start : start + size, tile * SMALL : (tile + 1) * SMALL]
+            total = jnp.zeros((size, SMALL), F32)
+            for half in range(2):
+                head = 2 * tile + half
+                which = (head // group, half)
+                scores = dot_nt(q_tile, keys[which][:seen]) * scale
+                scores = jnp.where(allowed, scores, -1e30)
+                top = jnp.max(scores, axis=1, keepdims=True)
+                raised = jnp.exp(scores - top)
+                mass = jnp.sum(raised, axis=1, keepdims=True)
+                probs = (raised * (1.0 / mass)).astype(BF16)
+                total = total + dot_nn(probs, values[which][:seen])
+                lse = jnp.where(lanes == head, top + jnp.log(mass), lse)
+            mixed_ref[start : start + size, tile * SMALL : (tile + 1) * SMALL] = total.astype(BF16)
+        lse_ref[0, start : start + size] = lse
+
+
+def attention_back_kernel(
+    length_ref, ga_ref, wo_ref, q_ref, k_ref, v_ref, lse_ref, cos_ref, left_ref, right_ref, *rest
+):
+    gq_ref, gk_ref, gv_ref = rest[-3:]
+    slots = ga_ref.shape[0]
+    q, k, v = q_ref[...], k_ref[...], v_ref[...]
+    grad_mixed = dot_nt(ga_ref[...], wo_ref[...]).astype(BF16)
+    keys, values = half_variants(k), half_variants(v)
+    heads = q.shape[1] // HEAD_SIZE
+    group = heads // 2
+    scale = 1.0 / math.sqrt(HEAD_SIZE)
+    blocks = row_blocks(slots)
+    pairs = [(c, a) for c in range(2) for a in range(2)]
+    zero = lambda: [jnp.zeros((size, SMALL), F32) for _, size, _ in blocks]
+    gk, gv = {p: zero() for p in pairs}, {p: zero() for p in pairs}
+    turn = (cos_ref[...], -left_ref[...], -right_ref[...])
+    for start, size, seen in blocks:
+        allowed = allowed_block(start, size, seen, length_ref[0])
+        rows = slice(start, start + size)
+        for tile in range(heads // 2):
+            columns = slice(tile * SMALL, (tile + 1) * SMALL)
+            q_tile, g_tile = q[rows, columns], grad_mixed[rows, columns]
+            total = jnp.zeros((size, SMALL), F32)
+            for half in range(2):
+                head = 2 * tile + half
+                which = (head // group, half)
+                scores = dot_nt(q_tile, keys[which][:seen]) * scale
+                probs = jnp.where(allowed, jnp.exp(scores - lse_ref[0, rows, head : head + 1]), 0.0)
+                grad_probs = dot_nt(g_tile, values[which][:seen])
+                weighted = probs * grad_probs
+                grad_scores = weighted - probs * jnp.sum(weighted, axis=1, keepdims=True)
+                grad_scores = grad_scores.astype(BF16)
+                probs_low = probs.astype(BF16)
+                total = total + dot_nn(grad_scores, keys[which][:seen])
+                gv_part = dot_tn(probs_low, g_tile)
+                gk_part = dot_tn(grad_scores, q_tile)
+                for b, (key_start, key_size, _) in enumerate(blocks):
+                    if key_start < seen:
+                        piece = slice(key_start, key_start + key_size)
+                        gv[which][b] = gv[which][b] + gv_part[piece]
+                        gk[which][b] = gk[which][b] + gk_part[piece]
+            turned = tile_rotate(total * scale, *[t[rows] for t in turn])
+            gq_ref[rows, columns] = turned.astype(BF16)
+
+    for b, (start, size, _) in enumerate(blocks):
+        rows = slice(start, start + size)
+        lanes = lax.broadcasted_iota(jnp.int32, (size, SMALL), 1)
+        right = lanes >= HEAD_SIZE
+
+        def joined(parts):
+            placed = []
+            for c in range(2):
+                kept = parts[(c, c)][b]
+                moved = pltpu.roll(parts[(c, 1 - c)][b], HEAD_SIZE, axis=1)
+                placed.append(kept + moved)
+            return jnp.where(right, placed[1], placed[0])
+
+        gv_ref[rows] = joined(gv).astype(BF16)
+        gk_ref[rows] = tile_rotate(joined(gk) * scale, *[t[rows] for t in turn]).astype(BF16)
+
+
+def rotary_tables(slots):
+    cosine, sine = rotation(slots, HEAD_SIZE)
+    zero = jnp.zeros_like(sine)
+    tile = lambda left, right: jnp.concatenate([left, right] * (SMALL // HEAD_SIZE), axis=1)
+    return tile(cosine, cosine), tile(-sine, zero), tile(zero, sine)
+
+
+def head_steps(k_width):
+    return k_width // SMALL
+
+
+def attention(length, normed, weights, tables, q_width, k_width, deps):
+    slots, width = normed.shape
+    steps = head_steps(k_width)
+    q_block = q_width // steps
+    fixed = lambda j, n: (0, 0)
+    shapes = [(slots, q_width), (slots, k_width), (slots, k_width), (slots, q_width)]
+    return pl.pallas_call(
+        attention_kernel,
+        out_shape=[jax.ShapeDtypeStruct(s, BF16) for s in shapes]
+        + [jax.ShapeDtypeStruct((steps, slots, SMALL), F32)],
+        grid_spec=pltpu.PrefetchScalarGridSpec(
+            num_scalar_prefetch=1,
+            grid=(steps,),
+            in_specs=[
+                pl.BlockSpec((slots, width), fixed),
+                pl.BlockSpec((width, q_block), lambda j, n: (0, j)),
+                pl.BlockSpec((width, SMALL), lambda j, n: (0, q_width // SMALL + j)),
+                pl.BlockSpec((width, SMALL), lambda j, n: (0, (q_width + k_width) // SMALL + j)),
+                pl.BlockSpec((slots, SMALL), fixed),
+                pl.BlockSpec((slots, SMALL), fixed),
+                pl.BlockSpec((slots, SMALL), fixed),
+            ]
+            + [pl.BlockSpec(memory_space=pl.ANY)] * len(deps),
+            out_specs=[
+                pl.BlockSpec((slots, q_block), lambda j, n: (0, j)),
+                pl.BlockSpec((slots, SMALL), lambda j, n: (0, j)),
+                pl.BlockSpec((slots, SMALL), lambda j, n: (0, j)),
+                pl.BlockSpec((slots, q_block), lambda j, n: (0, j)),
+                pl.BlockSpec((1, slots, SMALL), lambda j, n: (j, 0, 0)),
+            ],
+        ),
+        compiler_params=pltpu.CompilerParams(
+            dimension_semantics=("arbitrary",), vmem_limit_bytes=48 * 1024 * 1024
+        ),
+        cost_estimate=pl.CostEstimate(flops=25 * 10**9, bytes_accessed=10**7, transcendentals=10**7),
+    )(length.reshape(1), normed, weights, weights, weights, *tables, *deps)
+
+
+def attention_back(length, grad_attn, w_out, q, k, v, lse, tables, deps):
+    slots, width = grad_attn.shape
+    q_width, k_width = q.shape[1], k.shape[1]
+    steps = head_steps(k_width)
+    q_block = q_width // steps
+    fixed = lambda j, n: (0, 0)
+    shapes = [(slots, q_width), (slots, k_width), (slots, k_width)]
+    q_spec = pl.BlockSpec((slots, q_block), lambda j, n: (0, j))
+    k_spec = pl.BlockSpec((slots, SMALL), lambda j, n: (0, j))
+    return pl.pallas_call(
+        attention_back_kernel,
+        out_shape=[jax.ShapeDtypeStruct(s, BF16) for s in shapes],
+        grid_spec=pltpu.PrefetchScalarGridSpec(
+            num_scalar_prefetch=1,
+            grid=(steps,),
+            in_specs=[
+                pl.BlockSpec((slots, width), fixed),
+                pl.BlockSpec((q_block, width), lambda j, n: (j, 0)),
+                q_spec,
+                k_spec,
+                k_spec,
+                pl.BlockSpec((1, slots, SMALL), lambda j, n: (j, 0, 0)),
+                pl.BlockSpec((slots, SMALL), fixed),
+                pl.BlockSpec((slots, SMALL), fixed),
+                pl.BlockSpec((slots, SMALL), fixed),
+            ]
+            + [pl.BlockSpec(memory_space=pl.ANY)] * len(deps),
+            out_specs=[q_spec, k_spec, k_spec],
+        ),
+        compiler_params=pltpu.CompilerParams(
+            dimension_semantics=("arbitrary",), vmem_limit_bytes=48 * 1024 * 1024
+        ),
+        cost_estimate=pl.CostEstimate(flops=3 * 10**10, bytes_accessed=10**7, transcendentals=10**7),
+    )(length.reshape(1), grad_attn, w_out, q, k, v, lse, *tables, *deps)
+
+
+def out_kernel(mixed_ref, weight_ref, input_ref, gain_ref, *rest):
+    hidden_ref, normed_ref = rest[-2:]
+    hidden = input_ref[...].astype(F32) + dot_nn(mixed_ref[...], weight_ref[...])
+    hidden_ref[...] = hidden
+    normed_ref[...] = rms_scale(hidden, gain_ref[...]).astype(BF16)
+
+
+def attention_out(mixed, weights, inputs, gain, deps, rows=128):
+    slots, width = inputs.shape
+    q_width = mixed.shape[1]
+    spec = pl.BlockSpec((rows, width), lambda i: (i, 0))
+    return pl.pallas_call(
+        out_kernel,
+        out_shape=[
+            jax.ShapeDtypeStruct((slots, width), F32),
+            jax.ShapeDtypeStruct((slots, width), BF16),
+        ],
+        grid=(slots // rows,),
+        in_specs=[
+            pl.BlockSpec((rows, q_width), lambda i: (i, 0)),
+            pl.BlockSpec((q_width, width), lambda i: (0, 0)),
+            spec,
+            pl.BlockSpec((1, width), lambda i: (0, 0)),
+        ]
+        + [pl.BlockSpec(memory_space=pl.ANY)] * len(deps),
+        out_specs=[spec, spec],
+        compiler_params=pltpu.CompilerParams(
+            dimension_semantics=("arbitrary",), vmem_limit_bytes=40 * 1024 * 1024
+        ),
+        cost_estimate=LIGHT,
+    )(mixed, weights, inputs, gain.reshape(1, width), *deps)
+
+
+def joint_grad_kernel(left_a_ref, right_a_ref, left_b_ref, right_b_ref, out_ref, *, steps):
+    first = pl.program_id(0) < steps
+
+    @pl.when(first)
+    def _():
+        out_ref[...] = dot_tn(left_a_ref[...], right_a_ref[...]).astype(BF16)
+
+    @pl.when(jnp.logical_not(first))
+    def _():
+        out_ref[...] = dot_tn(left_b_ref[...], right_b_ref[...]).astype(BF16)
+
+
+def joint_grad(left_a, right_a, left_b, right_b, columns=512):
+    slots, rows = left_a.shape
+    steps = right_a.shape[1] // columns
+    width = right_a.shape[1] + right_b.shape[1]
+    whole = pl.BlockSpec((slots, rows), lambda j: (0, 0))
+    return pl.pallas_call(
+        functools.partial(joint_grad_kernel, steps=steps),
+        out_shape=jax.ShapeDtypeStruct((rows, width), BF16),
+        grid=(width // columns,),
+        in_specs=[
+            whole,
+            pl.BlockSpec((slots, columns), lambda j: (0, jnp.minimum(j, steps - 1))),
+            whole,
+            pl.BlockSpec((slots, columns), lambda j: (0, jnp.maximum(j - steps, 0))),
+        ],
+        out_specs=pl.BlockSpec((rows, columns), lambda j: (0, j)),
+        compiler_params=pltpu.CompilerParams(
+            dimension_semantics=("arbitrary",), vmem_limit_bytes=48 * 1024 * 1024
+        ),
+        cost_estimate=LIGHT,
+    )(left_a, right_a, left_b, right_b)
 
 
 def expert_kernel(
@@ -319,11 +618,9 @@
     experts = local * groups
     capacity = 25 * slots * top_count // (32 * experts)
     padded = -(-capacity // 16) * 16
-    group_width = QUERY_HEADS // KEY_VALUE_HEADS
-    scale_factor = 1.0 / math.sqrt(HEAD_SIZE)
     q_width = query_weight.shape[1]
     k_width = key_weight.shape[1]
-    cosine_table, sine_table = rotation(slots, HEAD_SIZE)
+    tables = rotary_tables(slots)
     order = ring_order(groups)
     place_of = [order.index(j) for j in range(groups)]
     my_place = jnp.asarray(place_of, jnp.int32)[me]
@@ -355,48 +652,35 @@
     full_router = jnp.where(lane < experts, full_small, jnp.zeros_like(full_small))
 
     table = slot_table(choices_row, length, experts, capacity)
-    row_tables = lax.all_gather(table.T, "fsdp", axis=0, tiled=False)
+    row_tables = table.T[None]
+    bit = 1
+    while bit < groups:
+        other = swap(row_tables, "fsdp", bit)
+        upper = jnp.bitwise_and(me // bit, 1) == 1
+        row_tables = jnp.where(
+            upper, jnp.concatenate([other, row_tables]), jnp.concatenate([row_tables, other])
+        )
+        bit *= 2
     col_tables = jnp.pad(
         jnp.swapaxes(row_tables, 1, 2), ((0, 0), (0, 0), (0, SMALL - experts)), constant_values=-2
     )
     row_tables = row_tables[:, :, None, :]
-    cot_ring = ring_gather(lax.optimization_barrier((cotangent[0], first_set))[0], order)
+    cot_ring = ring_start(tie([cotangent[0]], [row_tables])[0], order, 2)
 
     normed_float, norm_one_pull = jax.vjp(rms_scale, tokens, full_gain_attn)
     attention_normed = normed_float.astype(BF16)
-    query_rows = jnp.dot(
-        attention_normed, full_qkv[:, :q_width], preferred_element_type=F32
-    ).reshape(slots, KEY_VALUE_HEADS, group_width, HEAD_SIZE)
-    unrotated_keys = jnp.dot(
-        attention_normed, full_qkv[:, q_width : q_width + k_width], preferred_element_type=F32
-    ).reshape(slots, KEY_VALUE_HEADS, HEAD_SIZE)
-    value_rows = (
-        jnp.dot(attention_normed, full_qkv[:, q_width + k_width :], preferred_element_type=F32)
-        .astype(BF16)
-        .reshape(slots, KEY_VALUE_HEADS, HEAD_SIZE)
-    )
-    rot_queries = rotary_apply(query_rows, cosine_table, sine_table).astype(BF16)
-    rot_keys = rotary_apply(unrotated_keys, cosine_table, sine_table).astype(BF16)
+    rot_queries, rot_keys, value_rows, mixed, log_total = attention(
+        length, attention_normed, first_set, tables, q_width, k_width, [row_tables, col_tables]
+    )
     rows_index = jnp.arange(slots, dtype=jnp.int32)
-    allowed = (rows_index[None, :] <= rows_index[:, None]) & (rows_index[None, :] < length)
-
-    def masked_scores():
-        raw_scores = (
-            jnp.einsum("qhgd,khd->hgqk", rot_queries, rot_keys, preferred_element_type=F32)
-            * scale_factor
-        )
-        return jnp.where(allowed, raw_scores, -1e30)
-
-    scores = masked_scores()
-    log_total = jax.nn.logsumexp(scores, axis=-1, keepdims=True)
-    probs_low = jnp.exp(scores - log_total).astype(BF16)
-    mixed = jnp.einsum("hgqk,khd->qhgd", probs_low, value_rows, preferred_element_type=F32)
-    mixed = mixed.astype(BF16).reshape(slots, QUERY_HEADS * HEAD_SIZE)
-    hidden = tokens + jnp.dot(mixed, full_out, preferred_element_type=F32)
-    normed_float_two, norm_two_pull = jax.vjp(rms_scale, hidden, full_gain_moe)
-    normed_two = normed_float_two.astype(BF16)
-
-    tok_ring = ring_gather(normed_two, order)
+    near_cot = [cot_ring[o] for o in (1, -1, 2, -2) if o in cot_ring]
+    cot_ring = ring_finish(cot_ring, order, [mixed])
+    hidden, normed_two = attention_out(
+        mixed, full_out, inputs[0], full_gain_moe, near_cot
+    )
+    norm_two_pull = jax.vjp(rms_scale, hidden, full_gain_moe)[1]
+
+    tok_ring = ring_finish(ring_start(normed_two, order, 1), order, [])
     gates = chosen_gates(
         jnp.dot(normed_two, full_router, preferred_element_type=F32)[:, :experts], table
     )
@@ -430,92 +714,82 @@
     grad_gates = lax.all_to_all(natural, "fsdp", split_axis=0, concat_axis=0, tiled=True)
     grad_gates = grad_gates.reshape(experts, slots).T
 
-    left, right = ring_scatter(grad_parts, order)
-    grad_normed_two = grad_parts[0].astype(F32) + left.astype(F32) + right.astype(F32)
-
     grad_down = jnp.einsum("necf,necd->efd", inner_all, geo_all, preferred_element_type=F32)
     grad_gate = jnp.einsum("necd,necf->edf", rows_all, ggp_all, preferred_element_type=F32)
     grad_up = jnp.einsum("necd,necf->edf", rows_all, gup_all, preferred_element_type=F32)
-    expert_grads = [lax.psum(g.astype(BF16), "rep").astype(F32) for g in (grad_gate, grad_up, grad_down)]
+    core_bit = jnp.bitwise_and(rep, 1)
+    expert_sums = []
+    for grad in (grad_gate, grad_up, grad_down):
+        pairs = grad.astype(BF16).reshape(local // 2, 2, *grad.shape[1:])
+        mine = lax.dynamic_index_in_dim(pairs, core_bit, 1, keepdims=False)
+        other = lax.dynamic_index_in_dim(pairs, 1 - core_bit, 1, keepdims=False)
+        expert_sums.append(add_low(mine, swap(other, "rep", 1)))
+
+    left, right, _ = ring_scatter(grad_parts, order)
+    (own_grads,) = tie([grad_parts[0]], expert_sums)
+    grad_normed_two = own_grads.astype(F32) + left.astype(F32) + right.astype(F32)
 
     grad_logits = gates * (grad_gates - jnp.sum(gates * grad_gates, axis=-1, keepdims=True))
     grad_logits = grad_logits.astype(BF16)
     grad_normed_two = grad_normed_two + jnp.einsum(
         "se,de->sd", grad_logits, full_router[:, :experts], preferred_element_type=F32
     )
-    grad_router = jnp.einsum("sd,se->de", normed_two, grad_logits, preferred_element_type=F32)
+    grad_router = jnp.einsum("sd,se->ed", normed_two, grad_logits, preferred_element_type=F32)
     grad_hidden_norm, grad_gain_moe = norm_two_pull(grad_normed_two)
     grad_hidden = grad_y + grad_hidden_norm
     grad_attn = grad_hidden.astype(BF16)
-    grad_out = jnp.einsum("sa,sd->ad", mixed, grad_attn, preferred_element_type=F32)
 
     def reduce_weight(grad):
         owned = lax.psum_scatter(grad.astype(BF16), ALL, scatter_dimension=0, tiled=True)
-        return lax.all_gather(owned, "rep", axis=0, tiled=True)
-
-    total_out = reduce_weight(grad_out).astype(F32)
-    out_left, out_right = ring_scatter(out_parts, order)
-    mixture = out_parts[0].astype(F32) + out_left.astype(F32) + out_right.astype(F32)
+        return [lax.all_gather(p, "rep", axis=0, tiled=True) for p in jnp.split(owned, 2, axis=1)]
+
+    keys = sorted(out_parts)
+    held = dict(zip(keys, tie([out_parts[o] for o in keys], [grad_attn])))
+    out_left, out_right, stages = ring_scatter(held, order)
+    mixture = held[0].astype(F32) + out_left.astype(F32) + out_right.astype(F32)
     output = jnp.where(valid_rows, hidden + mixture, 0.0).astype(BF16)
 
-    gradient_mixed_rows = jnp.einsum("sd,ad->sa", grad_attn, full_out, preferred_element_type=F32)
-    gradient_mixed_rows = gradient_mixed_rows.astype(BF16).reshape(
-        slots, KEY_VALUE_HEADS, group_width, HEAD_SIZE
-    )
-    scores = masked_scores()
-    probs = jnp.exp(scores - log_total)
-    probs_low = probs.astype(BF16)
-    gradient_value_rows = jnp.einsum(
-        "hgqk,qhgd->khd", probs_low, gradient_mixed_rows, preferred_element_type=F32
-    )
-    gradient_value_rows = gradient_value_rows.astype(BF16).reshape(slots, k_width)
-    grad_probs = jnp.einsum(
-        "qhgd,khd->hgqk", gradient_mixed_rows, value_rows, preferred_element_type=F32
-    )
-    grad_scores = probs * (grad_probs - jnp.sum(probs * grad_probs, axis=-1, keepdims=True))
-    grad_scores = grad_scores.astype(BF16)
-    grad_rot_queries = (
-        jnp.einsum("hgqk,khd->qhgd", grad_scores, rot_keys, preferred_element_type=F32)
-        * scale_factor
-    )
-    gradient_rotated_keys = (
-        jnp.einsum("hgqk,qhgd->khd", grad_scores, rot_queries, preferred_element_type=F32)
-        * scale_factor
-    )
-    grad_queries = (
-        rotary_apply(grad_rot_queries, cosine_table, -sine_table).astype(BF16).reshape(slots, q_width)
-    )
-    grad_keys = (
-        rotary_apply(gradient_rotated_keys, cosine_table, -sine_table)
-        .astype(BF16)
-        .reshape(slots, k_width)
-    )
-    grad_projected = jnp.concatenate([grad_queries, grad_keys, gradient_value_rows], axis=1)
-    grad_qkv = jnp.einsum("sd,sa->da", attention_normed, grad_projected, preferred_element_type=F32)
-    grad_normed_one = jnp.einsum("sa,da->sd", grad_projected, full_qkv, preferred_element_type=F32)
+    grad_queries, grad_keys, grad_values = attention_back(
+        length, grad_attn, full_out, rot_queries, rot_keys, value_rows, log_total, tables, []
+    )
+    projected = jnp.concatenate([grad_queries, grad_keys, grad_values], axis=1)
+    crossed = [add_low(expert_sums[0], swap(expert_sums[0], "rep", 2))]
+    (projected,) = tie([projected], [*stages[0], *crossed])
+    grad_qkv = joint_grad(attention_normed, projected, mixed, grad_attn)
+    (projected,) = tie([projected], [grad_qkv, *stages[min(1, len(stages) - 1)]])
+    grad_normed_one = jnp.einsum("sa,da->sd", projected, full_qkv, preferred_element_type=F32)
     grad_tokens_norm, grad_gain_attn = norm_one_pull(grad_normed_one)
     grad_input = (grad_hidden + grad_tokens_norm).astype(BF16)
-    grad_small = jnp.concatenate(
-        [
-            grad_router,
-            grad_gain_attn[:, None],
-            grad_gain_moe[:, None],
-            jnp.zeros((width, SMALL - experts - 2), F32),
-        ],
-        axis=1,
-    )
-    total_first = reduce_weight(jnp.concatenate([grad_qkv, grad_small], axis=1)).astype(F32)
-    total_small = total_first[:, q_width + 2 * k_width :]
+    total_first = jnp.concatenate(reduce_weight(grad_qkv), axis=1).astype(F32)
+    small_sum = jnp.concatenate([grad_router, grad_gain_attn[None], grad_gain_moe[None]], axis=0)
+    (small_sum,) = tie([small_sum.astype(BF16)], stages[min(2, len(stages) - 1)])
+    for axis, size in (("fsdp", groups), ("rep", replicas)):
+        bit = 1
+        while bit < size:
+            small_sum = add_low(small_sum, swap(small_sum, axis, bit))
+            bit *= 2
+    small_sum = small_sum.astype(F32)
+    small_sum = lax.dynamic_slice_in_dim(small_sum, me * gain_attn.shape[0], gain_attn.shape[0], axis=1)
+
+    expert_grads = []
+    for total in (*crossed, *[add_low(t, swap(t, "rep", 2)) for t in expert_sums[1:]]):
+        bit = 4
+        while bit < replicas:
+            total = add_low(total, swap(total, "rep", bit))
+            bit *= 2
+        other = swap(total, "rep", 1)
+        pair = jnp.where(core_bit == 0, jnp.stack([total, other], 1), jnp.stack([other, total], 1))
+        expert_grads.append(pair.reshape(local, *total.shape[1:]).astype(F32))
     return (
         output[None],
         grad_input[None],
-        total_small[:, experts],
-        total_small[:, experts + 1],
+        small_sum[experts],
+        small_sum[experts + 1],
         total_first[:, :q_width],
         total_first[:, q_width : q_width + k_width],
         total_first[:, q_width + k_width : q_width + 2 * k_width],
-        total_out,
-        total_small[:, :experts],
+        total_first[:, q_width + 2 * k_width :],
+        small_sum[:experts].T,
         *expert_grads,
     )
 

time: 997 us -> 882 us (0.88)
  matrix products: 141 us -> 42.7 us
  Pallas kernels: 128 us -> 200 us
  waiting for transfers between devices: 414 us -> 343 us
  blocking collectives: 50.7 us -> 17.4 us
  starting transfers between devices: 37.6 us -> 56.6 us
    reduce_scatter x2 -> x1, waiting for transfers between devices: 154 us -> 0.01 us  [reduce_weight(): lax.psum_scatter(grad.astype(BF16), ALL, scatter_dimension=0, tiled=True)]
    dot_general x15 -> x2, matrix products: 114 us -> 12.5 us  [the longest x1 10.7 us: body(): jnp.einsum('sa,da->sd', projected, full_qkv, preferred_element_type=F32)]
    ppermute x0 -> x17, waiting for transfers between devices: none -> 87.7 us  [swap(): return lax.ppermute(value, axis, [(i, i ^ bit) for i in range(size)])]
    pallas_call x0 -> x11, Pallas kernels: none -> 72.5 us  [the longest x1 29.3 us: attention_back(): pl.pallas_call(attention_back_kernel, out_shape=[jax.ShapeDtypeStruct(s,...]
    all_gather x3 -> x2, blocking collectives: 50.7 us -> 17.4 us  [reduce_weight(): lax.all_gather(p, 'rep', axis=0, tiled=True)]
    all_gather x2, waiting for transfers between devices: 37 us -> 11 us  [gather_weight(): return lax.all_gather(piece, ALL, axis=0, tiled=True)]
    ppermute x32, waiting for transfers between devices: 222 us -> 244 us  [shift(): lax.ppermute(value, 'fsdp', [(order[i], order[(i + step) % size]) for i i...]
    convert_element_type x6 -> x19, other arithmetic: 19.5 us -> 40.3 us  [add_low(): return (left.astype(F32) + right.astype(F32)).astype(BF16)]
  transfers between devices with their start and end apart: 38 -> 53, of which waited for: 17 -> 24; matrix products, arithmetic and copies ran while one was open for 32% -> 22% of each run, Pallas kernels for 11% -> 19%
where the time goes in v2:
time: 882 us; the launch traced here: 877 us
  waiting for transfers between devices  343 us (39%)
  Pallas kernels  200 us (23%)
  other arithmetic  122 us (14%)
  local copies, waits for them, and re-layouts  77 us (9%)
  starting transfers between devices  56.6 us (6%)
  matrix products  42.7 us (5%)
  between operations  18.3 us (2%)
  blocking collectives  17.4 us (2%)
    ppermute x32, waiting for transfers between devices, shift(): lax.ppermute(value, 'fsdp', [(order[i], order[(i + step) % size]) for i i...  244 us
    pallas_call x5, Pallas kernels, run_experts(): pl.pallas_call(functools.partial(expert_kernel, padded=padded), out_shape...  128 us
    ppermute x17, waiting for transfers between devices, swap(): return lax.ppermute(value, axis, [(i, i ^ bit) for i in range(size)])  87.7 us
    convert_element_type x19, other arithmetic, add_low(): return (left.astype(F32) + right.astype(F32)).astype(BF16)  40.3 us
    ppermute x32, starting transfers between devices, shift(): lax.ppermute(value, 'fsdp', [(order[i], order[(i + step) % size]) for i i...  36.2 us
    pallas_call x1, Pallas kernels, attention_back(): pl.pallas_call(attention_back_kernel, out_shape=[jax.ShapeDtypeStruct(s,...  29.3 us
    unnamed x199, local copies, waits for them, and re-layouts  25.4 us
    pallas_call x1, Pallas kernels, attention(): pl.pallas_call(attention_kernel, out_shape=[jax.ShapeDtypeStruct(s, BF16)...  24.7 us
  transfers between devices with their start and end apart: 53, of which 24 were waited for; matrix products, arithmetic and copies ran while one was open for 22% of the time, Pallas kernels for 19%

profile of v2, /device:TPU:0, one launch (start us, length us, event | category | flops | bytes accessed | tf_op | source)
XLA Modules:
  0.0 877.1 jit_solution(11687204915324437530)
XLA Ops:
  30.1 6.3 collective-permute-done.2
  50.9 43.8 %collective-permute-done.4.rest_1_ = bf16[512,1536]{1,0:T(8,128)(2,1)} collective-permute-done((bf16[512,1536]{1,0:T(8,128)(2,1)}, bf16[512,1536]{1,0:T(8,128)(2,1)}, u32[]{:S(2)}, u32[]{:S(2)}) %collective-permute-start.4) | collective-permute-done | bytes 1572896 | tf_op jit(solution)/shard_map/ppermute | solution.py:82
  97.2 6.4 collective-permute-done.3.rest_0_
  116.0 3.8 pad_maximum_fusion.5.cot_ref
  119.9 21.8 %collective-permute-done.6.rest_3_.refs_0_ = bf16[512,1536]{1,0:T(8,128)(2,1)S(1)} collective-permute-done((bf16[512,1536]{1,0:T(8,128)(2,1)}, bf16[512,1536]{1,0:T(8,128)(2,1)S(1)}, u32[]{:S(2)}, u32[]{:S(2)}) %collective-permute-start.6) | collective-permute-done | bytes 1572896 | tf_op jit(solution)/shard_map/ppermute | solution.py:82
  144.0 3.3 pad_maximum_fusion.3.cot_ref
  150.8 24.7 %shard_map.301 = (bf16[512,1536]{1,0:T(8,128)(2,1)S(1)}, bf16[512,512]{1,0:T(8,128)(2,1)S(1)}, bf16[512,512]{1,0:T(8,128)(2,1)S(1)}, bf16[512,1536]{1,0:T(8,128)(2,1)}, f32[4,512,128]{2,1,0:T(8,128)S(1)}) custom-call(s32[1]{0:T(128)} %copy.197.length_ref, bf16[512,1536]{1,0:T(8,128)(2,1)} %fusion.4.x_ref.left_a_ref, ...), custom_call_target="tpu_custom_call" | custom-call | flops 24999999488 | bytes 10000000 | tf_op jit(solution)/shard_map/pallas_call | solution.py:307
  179.2 11.0 %all-gather.5.cloned.1.call-done.weight_ref.wo_ref = bf16[1536,1536]{1,0:T(8,128)(2,1)} async-done(((bf16[48,1536]{1,0:T(8,128)(2,1)}), bf16[1536,1536]{1,0:T(8,128)(2,1)}) %all-gather.5.cloned.1.call-update) | async-done | bytes 4718608 | tf_op jit(solution)/shard_map/all_gather | solution.py:641
  194.4 6.8 shard_map.303
  209.7 18.4 %shard_map.305 = (bf16[1,512,1536]{2,1,0:T(8,128)(2,1)}, bf16[1,512,1536]{2,1,0:T(8,128)(2,1)}, f32[1,512,128]{2,1,0:T(8,128)}, bf16[8,2,208,1536]{3,2,1,0:T(8,1...) custom-call(s32[1]{0:T(128)} %bitcast.9.first_ref, ...), custom_call_target="tpu_custom_call" | custom-call | flops 6543114240 | bytes 19562496 | tf_op jit(solution)/shard_map/pallas_call | solution.py:542
  229.7 43.4 %collective-permute-done.13 = bf16[512,1536]{1,0:T(8,128)(2,1)S(1)} collective-permute-done((bf16[512,1536]{1,0:T(8,128)(2,1)}, bf16[512,1536]{1,0:T(8,128)(2,1)S(1)}, u32[]{:S(2)}, u32[]{:S(2)}) %collective-permute-start.13) | collective-permute-done | bytes 1572896 | tf_op jit(solution)/shard_map/ppermute | solution.py:82
  277.3 3.9 pad_maximum_fusion.4.tok_ref
  283.8 30.1 %shard_map.306 = (bf16[2,512,1536]{2,1,0:T(8,128)(2,1)}, bf16[2,512,1536]{2,1,0:T(8,128)(2,1)}, f32[2,512,128]{2,1,0:T(8,128)}, bf16[8,2,208,1536]{3,2,1,0:T(8,1...) custom-call(s32[1]{0:T(128)} %bitcast.9.first_ref, ...), custom_call_target="tpu_custom_call", output_to_operand_aliasing={{3}: (10, {}), {4}: (11, {}), {5}: (12, {}), {6}: (13, {}),... | custom-call | flops 13086228480 | bytes 39124992 | tf_op jit(solution)/shard_map/pallas_call | solution.py:542
  314.0 3.6 pad_maximum_fusion.1.cot_ref
  322.8 5.6 collective-permute-done.11
  328.4 3.9 pad_maximum_fusion.2.tok_ref
  334.5 30.1 %shard_map.307 = (bf16[2,512,1536]{2,1,0:T(8,128)(2,1)}, bf16[2,512,1536]{2,1,0:T(8,128)(2,1)}, f32[2,512,128]{2,1,0:T(8,128)}, bf16[8,2,208,1536]{3,2,1,0:T(8,1...) custom-call(s32[1]{0:T(128)} %bitcast.9.first_ref, ...), custom_call_target="tpu_custom_call", output_to_operand_aliasing={{3}: (10, {}), {4}: (11, {}), {5}: (12, {}), {6}: (13, {}),... | custom-call | flops 13086228480 | bytes 39124992 | tf_op jit(solution)/shard_map/pallas_call | solution.py:542
  366.4 3.8 slice_bitcast_fusion.1
  374.3 3.4 pad_maximum_fusion.tok_ref
  377.8 30.4 %shard_map.308 = (bf16[2,512,1536]{2,1,0:T(8,128)(2,1)}, bf16[2,512,1536]{2,1,0:T(8,128)(2,1)}, f32[2,512,128]{2,1,0:T(8,128)}, bf16[8,2,208,1536]{3,2,1,0:T(8,1...) custom-call(s32[1]{0:T(128)} %bitcast.9.first_ref, ...), custom_call_target="tpu_custom_call", output_to_operand_aliasing={{3}: (10, {}), {4}: (11, {}), {5}: (12, {}), {6}: (13, {}),... | custom-call | flops 13086228480 | bytes 39124992 | tf_op jit(solution)/shard_map/pallas_call | solution.py:542
  417.2 18.9 %shard_map.309 = (bf16[1,512,1536]{2,1,0:T(8,128)(2,1)}, bf16[1,512,1536]{2,1,0:T(8,128)(2,1)}, f32[1,512,128]{2,1,0:T(8,128)}, bf16[8,2,208,1536]{3,2,1,0:T(8,1...) custom-call(s32[1]{0:T(128)} %bitcast.9.first_ref, ...), custom_call_target="tpu_custom_call", output_to_operand_aliasing={{3}: (10, {}), {4}: (11, {}), {5}: (12, {}), {6}: (13, {}),... | custom-call | flops 6543114240 | bytes 19562496 | tf_op jit(solution)/shard_map/pallas_call | solution.py:542
  443.4 4.0 all-to-all-start
  451.2 9.8 %bitcast_convert_fusion.2 = bf16[2,1536,512]{2,1,0:T(8,128)(2,1)S(1)} fusion(bf16[8,2,208,1536]{3,2,1,0:T(8,128)(2,1)} %get-tuple-element.103, bf16[8,2,208,512]{3,2,1,0:T(8,128)(2,1)} %get-tuple-element.104), kind=kOutput, calls=%fused_computation.8 | convolution fusion | flops 5236064256 | bytes 16777216 | tf_op jit(solution)/shard_map/necd,necf->edf/dot_general | solution.py:718
  462.3 3.7 collective-permute-done.22
  472.2 9.5 %bitcast_convert_fusion.1 = bf16[2,1536,512]{2,1,0:T(8,128)(2,1)} fusion(bf16[8,2,208,1536]{3,2,1,0:T(8,128)(2,1)S(1)} %bitcast.179, bf16[8,2,208,512]{3,2,1,0:T(8,128)(2,1)} %get-tuple-element.105), kind=kOutput, calls=%fused_computation.7 | convolution fusion | flops 5236064256 | bytes 16777216 | tf_op jit(solution)/shard_map/necd,necf->edf/dot_general | solution.py:719
  484.5 16.7 %collective-permute-done.27 = bf16[512,1536]{1,0:T(8,128)(2,1)S(1)} collective-permute-done((bf16[512,1536]{1,0:T(8,128)(2,1)}, bf16[512,1536]{1,0:T(8,128)(2,1)S(1)}, u32[]{:S(2)}, u32[]{:S(2)}) %collective-permute-start.27) | collective-permute-done | bytes 1572896 | tf_op jit(solution)/shard_map/ppermute | solution.py:82
  504.0 4.1 fusion.16
  510.1 6.3 bitcast_convert_fusion
  524.8 3.2 add_convert_fusion.9.refs_1_
  529.3 11.4 %collective-permute-done.24 = bf16[512,1536]{1,0:T(8,128)(2,1)} collective-permute-done((bf16[512,1536]{1,0:T(8,128)(2,1)}, bf16[512,1536]{1,0:T(8,128)(2,1)}, u32[]{:S(2)}, u32[]{:S(2)}) %collective-permute-start.24) | collective-permute-done | bytes 1572896 | tf_op jit(solution)/shard_map/ppermute | solution.py:82
  540.7 4.6 fusion.17
  553.2 11.9 %collective-permute-done.38 = bf16[1,1536,512]{2,1,0:T(8,128)(2,1)} collective-permute-done((bf16[1,1536,512]{2,1,0:T(8,128)(2,1)}, bf16[1,1536,512]{2,1,0:T(8,128)(2,1)}, u32[]{:S(2)}, u32[]{:S(2)}) %collective-permute-start.38) | collective-permute-done | bytes 1572896 | tf_op jit(solution)/shard_map/ppermute | solution.py:77
  565.1 3.5 add_convert_fusion.2.refs_3_
  568.6 8.3 collective-permute-done.25
  576.9 3.2 multiply_reduce_fusion
  588.3 29.3 %shard_map.312 = (bf16[512,1536]{1,0:T(8,128)(2,1)S(1)}, bf16[512,512]{1,0:T(8,128)(2,1)S(1)}, bf16[512,512]{1,0:T(8,128)(2,1)S(1)}) custom-call(s32[1]{0:T(128)} %copy.197.length_ref, bf16[512,1536]{1,0:T(8,128)(2,1)} %get-tuple-element.178.refs_8_.ga_ref.right_b_ref, bf16[1536,1536]{1,0:T(8,128)(2,1)} %all-gather.5.cloned.1.call-done.weight_ref.wo_ref, ...), custom_call_target="tpu_custom_call" | custom-call | flops 30000001024 | bytes 10000000 | tf_op jit(solution)/shard_map/pallas_call | solution.py:348
  628.0 11.6 %shard_map.314.refs_1_ = bf16[1536,4096]{1,0:T(8,128)(2,1)} custom-call(bf16[512,1536]{1,0:T(8,128)(2,1)S(1)} %copy-done.11, bf16[512,2560]{1,0:T(8,128)(2,1)} %shard_map.313.right_a_ref.refs_0_, bf16[512,1536]{1,0:T(8,128)(2,1)S(1)} %copy-done.7, bf16[512,1536]{1,0:T(8,128)(2,1)S(1)} %copy-done.5), custom_call_target="tpu_custom_call" | custom-call | flops 1000 | bytes 1000 | tf_op jit(solution)/shard_map/pallas_call | solution.py:425
  645.7 31.7 %collective-permute-done.47 = bf16[1,512,1536]{2,1,0:T(8,128)(2,1)} collective-permute-done((bf16[1,512,1536]{2,1,0:T(8,128)(2,1)}, bf16[1,512,1536]{2,1,0:T(8,128)(2,1)}, u32[]{:S(2)}, u32[]{:S(2)}) %collective-permute-start.47) | collective-permute-done | bytes 1572896 | tf_op jit(solution)/shard_map/ppermute | solution.py:77
  677.4 3.6 add_convert_fusion
  681.0 27.7 %collective-permute-done.45 = bf16[1,1536,512]{2,1,0:T(8,128)(2,1)} collective-permute-done((bf16[1,1536,512]{2,1,0:T(8,128)(2,1)}, bf16[1,1536,512]{2,1,0:T(8,128)(2,1)}, u32[]{:S(2)}, u32[]{:S(2)}) %collective-permute-start.45) | collective-permute-done | bytes 1572896 | tf_op jit(solution)/shard_map/ppermute | solution.py:77
  718.6 10.7 %fusion.5 = (bf16[1536]{0:T(1024)(128)(2,1)S(1)}, f32[512]{0:T(512)S(1)}, f32[512,1536]{1,0:T(8,128)}) fusion(f32[512]{0:T(512)S(1)} %copy-done.77, bf16[1,512,1536]{2,1,0:T(8,128)(2,1)} %param.22, f32[1536]{0:T(1024)S(1)} %copy-done.71, bf16[512,2560]{1,0:T(8,128)(2,1)} %shard_map.315, bf16[1536,2688]{1,0:T(8,128)(2,1)} %all-gather.3.cloned.1.call-done.wq_ref.wk_ref.wv_ref), kind=kOutput, calls=%fused_computation.18 | convolution fusion | flops 4032034816 | bytes 15217664 | tf_op jit(solution)/shard_map/sa,da->sd/dot_general | solution.py:760
  729.9 38.5 %collective-permute-done.36 = bf16[512,1536]{1,0:T(8,128)(2,1)} collective-permute-done((bf16[512,1536]{1,0:T(8,128)(2,1)}, bf16[512,1536]{1,0:T(8,128)(2,1)}, u32[]{:S(2)}, u32[]{:S(2)}) %collective-permute-start.36) | collective-permute-done | bytes 1572896 | tf_op jit(solution)/shard_map/ppermute | solution.py:82
  774.4 6.0 fusion.13
  782.6 4.8 fusion.11
  790.2 5.9 fusion.12
  808.2 38.0 %collective-permute-done.37 = bf16[512,1536]{1,0:T(8,128)(2,1)S(1)} collective-permute-done((bf16[512,1536]{1,0:T(8,128)(2,1)S(1)}, bf16[512,1536]{1,0:T(8,128)(2,1)S(1)}, u32[]{:S(2)}, u32[]{:S(2)}) %collective-permute-start.37) | collective-permute-done | bytes 1572896 | tf_op jit(solution)/shard_map/ppermute | solution.py:82
  849.3 8.7 all_gather.14
  858.0 8.7 all_gather.15
  (407 shorter events, 210.1 us)
Async XLA Ops:
  7.2 140.2 %all-gather.3.cloned.1.call-start = ((), (), s32[]{:S(2)}) async-start(), calls=%async_computation.2 | async-start | bytes 8515584 | tf_op jit(solution)/shard_map/all_gather | solution.py:641
  14.6 175.7 %all-gather.5.cloned.1.call-start = ((), (), s32[]{:S(2)}) async-start(), calls=%async_computation.3 | async-start | bytes 4866048 | tf_op jit(solution)/shard_map/all_gather | solution.py:641
  25.7 10.7 %collective-permute-start.2 = (s32[4,16,512]{2,1,0:T(8,128)S(1)}, s32[4,16,512]{2,1,0:T(8,128)S(1)}, u32[]{:S(2)}, u32[]{:S(2)}) collective-permute-start(s32[4,16,512]{2,1,0:T(8,128)S(1)} %add_select_fusion), channel_id=1, source_target_pairs={{0,4},{1,5},{2,6},{3,7},{4,0},{5,1},{6,2},{7,3},{8,12},{9,13},{10,... | collective-permute-start | bytes 393224 | tf_op jit(solution)/shard_map/ppermute | solution.py:77
  37.4 57.2 %collective-permute-start.4 = (bf16[512,1536]{1,0:T(8,128)(2,1)}, bf16[512,1536]{1,0:T(8,128)(2,1)}, u32[]{:S(2)}, u32[]{:S(2)}) collective-permute-start(bf16[512,1536]{1,0:T(8,128)(2,1)} %shard_map.302), channel_id=1, source_target_pairs={{0,2},{2,4},{4,6},{6,7},{7,5},{5,3},{3,1},{1,0},{8,10},{10,12},{12... | collective-permute-start | bytes 4718600 | tf_op jit(solution)/shard_map/ppermute | solution.py:82
  39.9 63.7 %collective-permute-start.3 = (bf16[512,1536]{1,0:T(8,128)(2,1)}, bf16[512,1536]{1,0:T(8,128)(2,1)}, u32[]{:S(2)}, u32[]{:S(2)}) collective-permute-start(bf16[512,1536]{1,0:T(8,128)(2,1)} %shard_map.302), channel_id=1, source_target_pairs={{0,1},{2,0},{4,2},{6,4},{7,6},{5,7},{3,5},{1,3},{8,9},{10,8},{12,1... | collective-permute-start | bytes 4718600 | tf_op jit(solution)/shard_map/ppermute | solution.py:82
  94.7 47.0 %collective-permute-start.6 = (bf16[512,1536]{1,0:T(8,128)(2,1)}, bf16[512,1536]{1,0:T(8,128)(2,1)S(1)}, u32[]{:S(2)}, u32[]{:S(2)}) collective-permute-start(bf16[512,1536]{1,0:T(8,128)(2,1)} %collective-permute-done.4.rest_1_), channel_id=1, source_target_pairs={{0,2},{2,4},{4,6},{6,7},{7,5},{5,3},{3,1},{1,0},{8,10},{10,12},{12... | collective-permute-start | bytes 4718600 | tf_op jit(solution)/shard_map/ppermute | solution.py:82
  103.6 40.5 %collective-permute-start.5 = (bf16[512,1536]{1,0:T(8,128)(2,1)}, bf16[512,1536]{1,0:T(8,128)(2,1)}, u32[]{:S(2)}, u32[]{:S(2)}) collective-permute-start(bf16[512,1536]{1,0:T(8,128)(2,1)} %collective-permute-done.3.rest_0_), channel_id=1, source_target_pairs={{0,1},{2,0},{4,2},{6,4},{7,6},{5,7},{3,5},{1,3},{8,9},{10,8},{12,1... | collective-permute-start | bytes 4718600 | tf_op jit(solution)/shard_map/ppermute | solution.py:82
  201.3 76.1 %collective-permute-start.10 = (bf16[512,1536]{1,0:T(8,128)(2,1)}, bf16[512,1536]{1,0:T(8,128)(2,1)}, u32[]{:S(2)}, u32[]{:S(2)}) collective-permute-start(bf16[512,1536]{1,0:T(8,128)(2,1)} %get-tuple-element.74), channel_id=1, source_target_pairs={{0,1},{2,0},{4,2},{6,4},{7,6},{5,7},{3,5},{1,3},{8,9},{10,8},{12,1... | collective-permute-start | bytes 4718600 | tf_op jit(solution)/shard_map/ppermute | solution.py:82
  202.7 74.6 %collective-permute-start.7 = (bf16[512,1536]{1,0:T(8,128)(2,1)}, bf16[512,1536]{1,0:T(8,128)(2,1)}, u32[]{:S(2)}, u32[]{:S(2)}) collective-permute-start(bf16[512,1536]{1,0:T(8,128)(2,1)} %get-tuple-element.74), channel_id=1, source_target_pairs={{0,2},{2,4},{4,6},{6,7},{7,5},{5,3},{3,1},{1,0},{8,10},{10,12},{12... | collective-permute-start | bytes 4718600 | tf_op jit(solution)/shard_map/ppermute | solution.py:82
  203.3 69.8 %collective-permute-start.13 = (bf16[512,1536]{1,0:T(8,128)(2,1)}, bf16[512,1536]{1,0:T(8,128)(2,1)S(1)}, u32[]{:S(2)}, u32[]{:S(2)}) collective-permute-start(bf16[512,1536]{1,0:T(8,128)(2,1)} %get-tuple-element.75), channel_id=1, source_target_pairs={{0,2},{2,4},{4,6},{6,7},{7,5},{5,3},{3,1},{1,0},{8,10},{10,12},{12... | collective-permute-start | bytes 4718600 | tf_op jit(solution)/shard_map/ppermute | solution.py:82
  205.2 68.6 %collective-permute-start.14 = (bf16[512,1536]{1,0:T(8,128)(2,1)}, bf16[512,1536]{1,0:T(8,128)(2,1)}, u32[]{:S(2)}, u32[]{:S(2)}) collective-permute-start(bf16[512,1536]{1,0:T(8,128)(2,1)} %get-tuple-element.76), channel_id=1, source_target_pairs={{0,1},{2,0},{4,2},{6,4},{7,6},{5,7},{3,5},{1,3},{8,9},{10,8},{12,1... | collective-permute-start | bytes 4718600 | tf_op jit(solution)/shard_map/ppermute | solution.py:82
  273.2 46.9 %collective-permute-start.17 = (bf16[256,1536]{1,0:T(8,128)(2,1)S(1)}, bf16[256,1536]{1,0:T(8,128)(2,1)}, u32[]{:S(2)}, u32[]{:S(2)}) collective-permute-start(bf16[256,1536]{1,0:T(8,128)(2,1)S(1)} %slice.238), channel_id=1, source_target_pairs={{0,2},{2,4},{4,6},{6,7},{7,5},{5,3},{3,1},{1,0},{8,10},{10,12},{12... | collective-permute-start | bytes 2359304 | tf_op jit(solution)/shard_map/ppermute | solution.py:82
  275.8 44.3 %collective-permute-start.18 = (bf16[256,1536]{1,0:T(8,128)(2,1)}, bf16[256,1536]{1,0:T(8,128)(2,1)}, u32[]{:S(2)}, u32[]{:S(2)}) collective-permute-start(bf16[256,1536]{1,0:T(8,128)(2,1)} %slice.239), channel_id=1, source_target_pairs={{0,1},{2,0},{4,2},{6,4},{7,6},{5,7},{3,5},{1,3},{8,9},{10,8},{12,1... | collective-permute-start | bytes 2359304 | tf_op jit(solution)/shard_map/ppermute | solution.py:82
  281.2 47.2 %collective-permute-start.11 = (bf16[512,1536]{1,0:T(8,128)(2,1)}, bf16[512,1536]{1,0:T(8,128)(2,1)}, u32[]{:S(2)}, u32[]{:S(2)}) collective-permute-start(bf16[512,1536]{1,0:T(8,128)(2,1)} %collective-permute-done.10), channel_id=1, source_target_pairs={{0,1},{2,0},{4,2},{6,4},{7,6},{5,7},{3,5},{1,3},{8,9},{10,8},{12,1... | collective-permute-start | bytes 4718600 | tf_op jit(solution)/shard_map/ppermute | solution.py:82
  282.9 45.5 %collective-permute-start.8 = (bf16[512,1536]{1,0:T(8,128)(2,1)}, bf16[512,1536]{1,0:T(8,128)(2,1)}, u32[]{:S(2)}, u32[]{:S(2)}) collective-permute-start(bf16[512,1536]{1,0:T(8,128)(2,1)} %collective-permute-done.7), channel_id=1, source_target_pairs={{0,2},{2,4},{4,6},{6,7},{7,5},{5,3},{3,1},{1,0},{8,10},{10,12},{12... | collective-permute-start | bytes 4718600 | tf_op jit(solution)/shard_map/ppermute | solution.py:82
  332.3 37.8 %collective-permute-start.12 = (bf16[512,1536]{1,0:T(8,128)(2,1)}, bf16[512,1536]{1,0:T(8,128)(2,1)S(1)}, u32[]{:S(2)}, u32[]{:S(2)}) collective-permute-start(bf16[512,1536]{1,0:T(8,128)(2,1)} %collective-permute-done.11), channel_id=1, source_target_pairs={{0,1},{2,0},{4,2},{6,4},{7,6},{5,7},{3,5},{1,3},{8,9},{10,8},{12,1... | collective-permute-start | bytes 4718600 | tf_op jit(solution)/shard_map/ppermute | solution.py:82
  333.8 37.9 %collective-permute-start.9 = (bf16[512,1536]{1,0:T(8,128)(2,1)}, bf16[512,1536]{1,0:T(8,128)(2,1)}, u32[]{:S(2)}, u32[]{:S(2)}) collective-permute-start(bf16[512,1536]{1,0:T(8,128)(2,1)} %collective-permute-done.8), channel_id=1, source_target_pairs={{0,2},{2,4},{4,6},{6,7},{7,5},{5,3},{3,1},{1,0},{8,10},{10,12},{12... | collective-permute-start | bytes 4718600 | tf_op jit(solution)/shard_map/ppermute | solution.py:82
  370.2 44.4 %collective-permute-start.16 = (bf16[256,1536]{1,0:T(8,128)(2,1)S(1)}, bf16[256,1536]{1,0:T(8,128)(2,1)}, u32[]{:S(2)}, u32[]{:S(2)}) collective-permute-start(bf16[256,1536]{1,0:T(8,128)(2,1)S(1)} %slice.237), channel_id=1, source_target_pairs={{0,1},{2,0},{4,2},{6,4},{7,6},{5,7},{3,5},{1,3},{8,9},{10,8},{12,1... | collective-permute-start | bytes 2359304 | tf_op jit(solution)/shard_map/ppermute | solution.py:82
  373.8 40.8 %collective-permute-start.15 = (bf16[256,1536]{1,0:T(8,128)(2,1)}, bf16[256,1536]{1,0:T(8,128)(2,1)}, u32[]{:S(2)}, u32[]{:S(2)}) collective-permute-start(bf16[256,1536]{1,0:T(8,128)(2,1)} %slice.236), channel_id=1, source_target_pairs={{0,2},{2,4},{4,6},{6,7},{7,5},{5,3},{3,1},{1,0},{8,10},{10,12},{12... | collective-permute-start | bytes 2359304 | tf_op jit(solution)/shard_map/ppermute | solution.py:82
  443.4 75.9 %all-to-all-start = ((f32[8,2,512]{2,1,0:T(2,128)}), f32[8,2,512]{2,1,0:T(2,128)}, u32[]{:S(2)}, u32[]{:S(2)}) async-start(f32[8,2,512]{2,1,0:T(2,128)} %gather_fusion.3), calls=%async_computation | async-start | bytes 65536 | tf_op jit(solution)/shard_map/all_to_all | solution.py:714
  447.4 400.8 %reduce-scatter.2.cloned.1.call-start = ((), (), s32[]{:S(2)}) async-start(), calls=%async_computation.4 | async-start | bytes 12976128 | tf_op jit(solution)/shard_map/reduce_scatter | solution.py:743
  449.1 16.8 %collective-permute-start.22 = (bf16[256,1536]{1,0:T(8,128)(2,1)S(1)}, bf16[256,1536]{1,0:T(8,128)(2,1)S(1)}, u32[]{:S(2)}, u32[]{:S(2)}) collective-permute-start(bf16[256,1536]{1,0:T(8,128)(2,1)S(1)} %get-tuple-element.199), channel_id=1, source_target_pairs={{0,2},{2,4},{4,6},{6,7},{7,5},{5,3},{3,1},{1,0},{8,10},{10,12},{12... | collective-permute-start | bytes 2359304 | tf_op jit(solution)/shard_map/ppermute | solution.py:82
  451.1 16.1 %collective-permute-start.26 = (bf16[256,1536]{1,0:T(8,128)(2,1)S(1)}, bf16[256,1536]{1,0:T(8,128)(2,1)S(1)}, u32[]{:S(2)}, u32[]{:S(2)}) collective-permute-start(bf16[256,1536]{1,0:T(8,128)(2,1)S(1)} %get-tuple-element.200), channel_id=1, source_target_pairs={{0,1},{2,0},{4,2},{6,4},{7,6},{5,7},{3,5},{1,3},{8,9},{10,8},{12,1... | collective-permute-start | bytes 2359304 | tf_op jit(solution)/shard_map/ppermute | solution.py:82
  462.3 62.6 %collective-permute-start.19 = (bf16[1,1536,512]{2,1,0:T(8,128)(2,1)}, bf16[1,1536,512]{2,1,0:T(8,128)(2,1)}, u32[]{:S(2)}, u32[]{:S(2)}) collective-permute-start(bf16[1,1536,512]{2,1,0:T(8,128)(2,1)} %constant_dynamic-slice_fusion.2), channel_id=1, source_target_pairs={{0,8},{8,0},{16,24},{24,16},{1,9},{9,1},{17,25},{25,17},{2,10},{10... | collective-permute-start | bytes 4718600 | tf_op jit(solution)/shard_map/ppermute | solution.py:77
  468.9 32.3 %collective-permute-start.27 = (bf16[512,1536]{1,0:T(8,128)(2,1)}, bf16[512,1536]{1,0:T(8,128)(2,1)S(1)}, u32[]{:S(2)}, u32[]{:S(2)}) collective-permute-start(bf16[512,1536]{1,0:T(8,128)(2,1)} %pad_maximum_fusion.8), channel_id=1, source_target_pairs={{0,1},{2,0},{4,2},{6,4},{7,6},{5,7},{3,5},{1,3},{8,9},{10,8},{12,1... | collective-permute-start | bytes 4718600 | tf_op jit(solution)/shard_map/ppermute | solution.py:82
  470.5 33.5 %collective-permute-start.23 = (bf16[512,1536]{1,0:T(8,128)(2,1)}, bf16[512,1536]{1,0:T(8,128)(2,1)}, u32[]{:S(2)}, u32[]{:S(2)}) collective-permute-start(bf16[512,1536]{1,0:T(8,128)(2,1)} %pad_maximum_fusion.7), channel_id=1, source_target_pairs={{0,2},{2,4},{4,6},{6,7},{7,5},{5,3},{3,1},{1,0},{8,10},{10,12},{12... | collective-permute-start | bytes 4718600 | tf_op jit(solution)/shard_map/ppermute | solution.py:82
  484.5 62.8 %collective-permute-start.20 = (bf16[1,1536,512]{2,1,0:T(8,128)(2,1)}, bf16[1,1536,512]{2,1,0:T(8,128)(2,1)}, u32[]{:S(2)}, u32[]{:S(2)}) collective-permute-start(bf16[1,1536,512]{2,1,0:T(8,128)(2,1)} %constant_dynamic-slice_fusion.1), channel_id=1, source_target_pairs={{0,8},{8,0},{16,24},{24,16},{1,9},{9,1},{17,25},{25,17},{2,10},{10... | collective-permute-start | bytes 4718600 | tf_op jit(solution)/shard_map/ppermute | solution.py:77
  508.1 32.6 %collective-permute-start.24 = (bf16[512,1536]{1,0:T(8,128)(2,1)}, bf16[512,1536]{1,0:T(8,128)(2,1)}, u32[]{:S(2)}, u32[]{:S(2)}) collective-permute-start(bf16[512,1536]{1,0:T(8,128)(2,1)} %get-tuple-element.183), channel_id=1, source_target_pairs={{0,2},{2,4},{4,6},{6,7},{7,5},{5,3},{3,1},{1,0},{8,10},{10,12},{12... | collective-permute-start | bytes 4718600 | tf_op jit(solution)/shard_map/ppermute | solution.py:82
  508.4 32.3 %collective-permute-start.28 = (bf16[512,1536]{1,0:T(8,128)(2,1)}, bf16[512,1536]{1,0:T(8,128)(2,1)}, u32[]{:S(2)}, u32[]{:S(2)}) collective-permute-start(bf16[512,1536]{1,0:T(8,128)(2,1)} %get-tuple-element.184), channel_id=1, source_target_pairs={{0,1},{2,0},{4,2},{6,4},{7,6},{5,7},{3,5},{1,3},{8,9},{10,8},{12,1... | collective-permute-start | bytes 4718600 | tf_op jit(solution)/shard_map/ppermute | solution.py:82
  519.3 31.0 %collective-permute-start.21 = (bf16[1,512,1536]{2,1,0:T(8,128)(2,1)}, bf16[1,512,1536]{2,1,0:T(8,128)(2,1)}, u32[]{:S(2)}, u32[]{:S(2)}) collective-permute-start(bf16[1,512,1536]{2,1,0:T(8,128)(2,1)} %constant_dynamic-slice_fusion), channel_id=1, source_target_pairs={{0,8},{8,0},{16,24},{24,16},{1,9},{9,1},{17,25},{25,17},{2,10},{10... | collective-permute-start | bytes 4718600 | tf_op jit(solution)/shard_map/ppermute | solution.py:77
  528.0 37.1 %collective-permute-start.38 = (bf16[1,1536,512]{2,1,0:T(8,128)(2,1)}, bf16[1,1536,512]{2,1,0:T(8,128)(2,1)}, u32[]{:S(2)}, u32[]{:S(2)}) collective-permute-start(bf16[1,1536,512]{2,1,0:T(8,128)(2,1)} %add_convert_fusion.9.refs_1_), channel_id=1, source_target_pairs={{0,16},{8,24},{16,0},{24,8},{1,17},{9,25},{17,1},{25,9},{2,18},{10... | collective-permute-start | bytes 4718600 | tf_op jit(solution)/shard_map/ppermute | solution.py:77
  545.2 31.7 %collective-permute-start.25 = (bf16[512,1536]{1,0:T(8,128)(2,1)}, bf16[512,1536]{1,0:T(8,128)(2,1)}, u32[]{:S(2)}, u32[]{:S(2)}) collective-permute-start(bf16[512,1536]{1,0:T(8,128)(2,1)} %get-tuple-element.181), channel_id=1, source_target_pairs={{0,2},{2,4},{4,6},{6,7},{7,5},{5,3},{3,1},{1,0},{8,10},{10,12},{12... | collective-permute-start | bytes 4718600 | tf_op jit(solution)/shard_map/ppermute | solution.py:82
  545.8 31.1 %collective-permute-start.29 = (bf16[512,1536]{1,0:T(8,128)(2,1)}, bf16[512,1536]{1,0:T(8,128)(2,1)}, u32[]{:S(2)}, u32[]{:S(2)}) collective-permute-start(bf16[512,1536]{1,0:T(8,128)(2,1)} %get-tuple-element.182), channel_id=1, source_target_pairs={{0,1},{2,0},{4,2},{6,4},{7,6},{5,7},{3,5},{1,3},{8,9},{10,8},{12,1... | collective-permute-start | bytes 4718600 | tf_op jit(solution)/shard_map/ppermute | solution.py:82
  586.2 33.1 %collective-permute-start.30 = (bf16[256,1536]{1,0:T(8,128)(2,1)S(1)}, bf16[256,1536]{1,0:T(8,128)(2,1)}, u32[]{:S(2)}, u32[]{:S(2)}) collective-permute-start(bf16[256,1536]{1,0:T(8,128)(2,1)S(1)} %get-tuple-element.197), channel_id=1, source_target_pairs={{0,2},{2,4},{4,6},{6,7},{7,5},{5,3},{3,1},{1,0},{8,10},{10,12},{12... | collective-permute-start | bytes 2359304 | tf_op jit(solution)/shard_map/ppermute | solution.py:82
  587.6 34.7 %collective-permute-start.34 = (bf16[256,1536]{1,0:T(8,128)(2,1)S(1)}, bf16[256,1536]{1,0:T(8,128)(2,1)S(1)}, u32[]{:S(2)}, u32[]{:S(2)}) collective-permute-start(bf16[256,1536]{1,0:T(8,128)(2,1)S(1)} %get-tuple-element.198), channel_id=1, source_target_pairs={{0,1},{2,0},{4,2},{6,4},{7,6},{5,7},{3,5},{1,3},{8,9},{10,8},{12,1... | collective-permute-start | bytes 2359304 | tf_op jit(solution)/shard_map/ppermute | solution.py:82
  639.6 37.7 %collective-permute-start.47 = (bf16[1,512,1536]{2,1,0:T(8,128)(2,1)}, bf16[1,512,1536]{2,1,0:T(8,128)(2,1)}, u32[]{:S(2)}, u32[]{:S(2)}) collective-permute-start(bf16[1,512,1536]{2,1,0:T(8,128)(2,1)} %add_convert_fusion.7.refs_3_), channel_id=1, source_target_pairs={{0,16},{8,24},{16,0},{24,8},{1,17},{9,25},{17,1},{25,9},{2,18},{10... | collective-permute-start | bytes 4718600 | tf_op jit(solution)/shard_map/ppermute | solution.py:77
  640.6 68.1 %collective-permute-start.45 = (bf16[1,1536,512]{2,1,0:T(8,128)(2,1)}, bf16[1,1536,512]{2,1,0:T(8,128)(2,1)}, u32[]{:S(2)}, u32[]{:S(2)}) collective-permute-start(bf16[1,1536,512]{2,1,0:T(8,128)(2,1)} %add_convert_fusion.8.refs_2_), channel_id=1, source_target_pairs={{0,16},{8,24},{16,0},{24,8},{1,17},{9,25},{17,1},{25,9},{2,18},{10... | collective-permute-start | bytes 4718600 | tf_op jit(solution)/shard_map/ppermute | solution.py:77
  641.7 70.0 %collective-permute-start.35 = (bf16[512,1536]{1,0:T(8,128)(2,1)}, bf16[512,1536]{1,0:T(8,128)(2,1)}, u32[]{:S(2)}, u32[]{:S(2)}) collective-permute-start(bf16[512,1536]{1,0:T(8,128)(2,1)} %pad_maximum_fusion.10.refs_2_), channel_id=1, source_target_pairs={{0,1},{2,0},{4,2},{6,4},{7,6},{5,7},{3,5},{1,3},{8,9},{10,8},{12,1... | collective-permute-start | bytes 4718600 | tf_op jit(solution)/shard_map/ppermute | solution.py:82
  645.3 137.3 %collective-permute-start.44 = (bf16[1,1536,512]{2,1,0:T(8,128)(2,1)}, bf16[1,1536,512]{2,1,0:T(8,128)(2,1)}, u32[]{:S(2)}, u32[]{:S(2)}) collective-permute-start(bf16[1,1536,512]{2,1,0:T(8,128)(2,1)} %add_convert_fusion.2.refs_3_), channel_id=1, source_target_pairs={{0,8},{8,0},{16,24},{24,16},{1,9},{9,1},{17,25},{25,17},{2,10},{10... | collective-permute-start | bytes 4718600 | tf_op jit(solution)/shard_map/ppermute | solution.py:77
  645.3 70.9 %collective-permute-start.31 = (bf16[512,1536]{1,0:T(8,128)(2,1)}, bf16[512,1536]{1,0:T(8,128)(2,1)S(1)}, u32[]{:S(2)}, u32[]{:S(2)}) collective-permute-start(bf16[512,1536]{1,0:T(8,128)(2,1)} %pad_maximum_fusion.9.refs_1_), channel_id=1, source_target_pairs={{0,2},{2,4},{4,6},{6,7},{7,5},{5,3},{3,1},{1,0},{8,10},{10,12},{12... | collective-permute-start | bytes 4718600 | tf_op jit(solution)/shard_map/ppermute | solution.py:82
  681.0 93.5 %collective-permute-start.48 = (bf16[1,512,1536]{2,1,0:T(8,128)(2,1)}, bf16[1,512,1536]{2,1,0:T(8,128)(2,1)}, u32[]{:S(2)}, u32[]{:S(2)}) collective-permute-start(bf16[1,512,1536]{2,1,0:T(8,128)(2,1)} %add_convert_fusion), channel_id=1, source_target_pairs={{0,8},{8,0},{16,24},{24,16},{1,9},{9,1},{17,25},{25,17},{2,10},{10... | collective-permute-start | bytes 4718600 | tf_op jit(solution)/shard_map/ppermute | solution.py:77
  714.8 53.6 %collective-permute-start.36 = (bf16[512,1536]{1,0:T(8,128)(2,1)}, bf16[512,1536]{1,0:T(8,128)(2,1)}, u32[]{:S(2)}, u32[]{:S(2)}) collective-permute-start(bf16[512,1536]{1,0:T(8,128)(2,1)} %add_convert_fusion.4.refs_3_), channel_id=1, source_target_pairs={{0,1},{2,0},{4,2},{6,4},{7,6},{5,7},{3,5},{1,3},{8,9},{10,8},{12,1... | collective-permute-start | bytes 4718600 | tf_op jit(solution)/shard_map/ppermute | solution.py:82
  717.7 53.6 %collective-permute-start.32 = (bf16[512,1536]{1,0:T(8,128)(2,1)}, bf16[512,1536]{1,0:T(8,128)(2,1)}, u32[]{:S(2)}, u32[]{:S(2)}) collective-permute-start(bf16[512,1536]{1,0:T(8,128)(2,1)} %add_convert_fusion.6.refs_2_), channel_id=1, source_target_pairs={{0,2},{2,4},{4,6},{6,7},{7,5},{5,3},{3,1},{1,0},{8,10},{10,12},{12... | collective-permute-start | bytes 4718600 | tf_op jit(solution)/shard_map/ppermute | solution.py:82
  774.3 15.9 %collective-permute-start.46 = (bf16[1,1536,512]{2,1,0:T(8,128)(2,1)}, bf16[1,1536,512]{2,1,0:T(8,128)(2,1)}, u32[]{:S(2)}, u32[]{:S(2)}) collective-permute-start(bf16[1,1536,512]{2,1,0:T(8,128)(2,1)} %add_convert_fusion.1), channel_id=1, source_target_pairs={{0,8},{8,0},{16,24},{24,16},{1,9},{9,1},{17,25},{25,17},{2,10},{10... | collective-permute-start | bytes 4718600 | tf_op jit(solution)/shard_map/ppermute | solution.py:77
  780.4 8.8 %collective-permute-start.40 = (bf16[18,1536]{1,0:T(8,128)(2,1)S(1)}, bf16[18,1536]{1,0:T(8,128)(2,1)S(1)}, u32[]{:S(2)}, u32[]{:S(2)}) collective-permute-start(bf16[18,1536]{1,0:T(8,128)(2,1)S(1)} %add_convert_fusion.15), channel_id=1, source_target_pairs={{0,2},{1,3},{2,0},{3,1},{4,6},{5,7},{6,4},{7,5},{8,10},{9,11},{10,... | collective-permute-start | bytes 165896 | tf_op jit(solution)/shard_map/ppermute | solution.py:77
  789.3 9.9 %collective-permute-start.41 = (bf16[18,1536]{1,0:T(8,128)(2,1)S(1)}, bf16[18,1536]{1,0:T(8,128)(2,1)S(1)}, u32[]{:S(2)}, u32[]{:S(2)}) collective-permute-start(bf16[18,1536]{1,0:T(8,128)(2,1)S(1)} %add_convert_fusion.14), channel_id=1, source_target_pairs={{0,4},{1,5},{2,6},{3,7},{4,0},{5,1},{6,2},{7,3},{8,12},{9,13},{10,... | collective-permute-start | bytes 165896 | tf_op jit(solution)/shard_map/ppermute | solution.py:77
  799.4 46.7 %collective-permute-start.37 = (bf16[512,1536]{1,0:T(8,128)(2,1)S(1)}, bf16[512,1536]{1,0:T(8,128)(2,1)S(1)}, u32[]{:S(2)}, u32[]{:S(2)}) collective-permute-start(bf16[512,1536]{1,0:T(8,128)(2,1)S(1)} %copy-done.41), channel_id=1, source_target_pairs={{0,1},{2,0},{4,2},{6,4},{7,6},{5,7},{3,5},{1,3},{8,9},{10,8},{12,1... | collective-permute-start | bytes 4718600 | tf_op jit(solution)/shard_map/ppermute | solution.py:82
  802.4 43.7 %collective-permute-start.33 = (bf16[512,1536]{1,0:T(8,128)(2,1)S(1)}, bf16[512,1536]{1,0:T(8,128)(2,1)S(1)}, u32[]{:S(2)}, u32[]{:S(2)}) collective-permute-start(bf16[512,1536]{1,0:T(8,128)(2,1)S(1)} %copy-done.42), channel_id=1, source_target_pairs={{0,2},{2,4},{4,6},{6,7},{7,5},{5,3},{3,1},{1,0},{8,10},{10,12},{12... | collective-permute-start | bytes 4718600 | tf_op jit(solution)/shard_map/ppermute | solution.py:82
  (100 other events, 2457.9 us)
Sparse Core Ops, SparseCore 0:
  14.7 103.2 all-gather.2
  121.4 68.7 all-gather.4
  639.8 190.0 reduce-scatter.1

commit v3 on v2

--- a/solution.py
+++ b/solution.py
@@ -771,8 +771,9 @@
     small_sum = small_sum.astype(F32)
     small_sum = lax.dynamic_slice_in_dim(small_sum, me * gain_attn.shape[0], gain_attn.shape[0], axis=1)
 
+    later_sums = tie(expert_sums[1:], stages[min(2, len(stages) - 1)])
     expert_grads = []
-    for total in (*crossed, *[add_low(t, swap(t, "rep", 2)) for t in expert_sums[1:]]):
+    for total in (*crossed, *[add_low(t, swap(t, "rep", 2)) for t in later_sums]):
         bit = 4
         while bit < replicas:
             total = add_low(total, swap(total, "rep", bit))

time: 882 us -> 857 us (0.972)
  waiting for transfers between devices: 343 us -> 323 us
    ppermute x32, waiting for transfers between devices: 244 us -> 229 us  [shift(): lax.ppermute(value, 'fsdp', [(order[i], order[(i + step) % size]) for i i...]
    unnamed x199 -> x183, local copies, waits for them, and re-layouts: 25.4 us -> 28.3 us
  transfers between devices with their start and end apart: 53 -> 53, of which waited for: 24 -> 23; matrix products, arithmetic and copies ran while one was open for 22% -> 22% of each run, Pallas kernels for 19% -> 19%
where the time goes in v3:
time: 857 us; the launch traced here: 852 us
  waiting for transfers between devices  323 us (38%)
  Pallas kernels  200 us (23%)
  other arithmetic  114 us (13%)
  local copies, waits for them, and re-layouts  78 us (9%)
  starting transfers between devices  57.7 us (7%)
  matrix products  43.1 us (5%)
  between operations  18.3 us (2%)
  blocking collectives  17.2 us (2%)
    ppermute x32, waiting for transfers between devices, shift(): lax.ppermute(value, 'fsdp', [(order[i], order[(i + step) % size]) for i i...  229 us
    pallas_call x5, Pallas kernels, run_experts(): pl.pallas_call(functools.partial(expert_kernel, padded=padded), out_shape...  128 us
    ppermute x17, waiting for transfers between devices, swap(): return lax.ppermute(value, axis, [(i, i ^ bit) for i in range(size)])  79.3 us
    ppermute x32, starting transfers between devices, shift(): lax.ppermute(value, 'fsdp', [(order[i], order[(i + step) % size]) for i i...  35.1 us
    convert_element_type x19, other arithmetic, add_low(): return (left.astype(F32) + right.astype(F32)).astype(BF16)  34.4 us
    pallas_call x1, Pallas kernels, attention_back(): pl.pallas_call(attention_back_kernel, out_shape=[jax.ShapeDtypeStruct(s,...  29.3 us
    unnamed x183, local copies, waits for them, and re-layouts  28.3 us
    pallas_call x1, Pallas kernels, attention(): pl.pallas_call(attention_kernel, out_shape=[jax.ShapeDtypeStruct(s, BF16)...  24.7 us
  transfers between devices with their start and end apart: 53, of which 23 were waited for; matrix products, arithmetic and copies ran while one was open for 22% of the time, Pallas kernels for 19%

profile of v3, /device:TPU:0, one launch (start us, length us, event | category | flops | bytes accessed | tf_op | source)
XLA Modules:
  0.0 852.0 jit_solution(12781987561361958503)
XLA Ops:
  29.6 4.8 collective-permute-done.2
  49.0 43.7 %collective-permute-done.4.rest_1_ = bf16[512,1536]{1,0:T(8,128)(2,1)} collective-permute-done((bf16[512,1536]{1,0:T(8,128)(2,1)}, bf16[512,1536]{1,0:T(8,128)(2,1)}, u32[]{:S(2)}, u32[]{:S(2)}) %collective-permute-start.4) | collective-permute-done | bytes 1572896 | tf_op jit(solution)/shard_map/ppermute | solution.py:82
  95.2 6.4 collective-permute-done.3.rest_0_
  114.2 3.8 pad_maximum_fusion.5.cot_ref
  118.0 21.7 %collective-permute-done.6.rest_3_.refs_0_ = bf16[512,1536]{1,0:T(8,128)(2,1)S(1)} collective-permute-done((bf16[512,1536]{1,0:T(8,128)(2,1)}, bf16[512,1536]{1,0:T(8,128)(2,1)S(1)}, u32[]{:S(2)}, u32[]{:S(2)}) %collective-permute-start.6) | collective-permute-done | bytes 1572896 | tf_op jit(solution)/shard_map/ppermute | solution.py:82
  142.1 3.3 pad_maximum_fusion.3.cot_ref
  148.8 24.7 %shard_map.301 = (bf16[512,1536]{1,0:T(8,128)(2,1)S(1)}, bf16[512,512]{1,0:T(8,128)(2,1)S(1)}, bf16[512,512]{1,0:T(8,128)(2,1)S(1)}, bf16[512,1536]{1,0:T(8,128)(2,1)}, f32[4,512,128]{2,1,0:T(8,128)S(1)}) custom-call(s32[1]{0:T(128)} %copy.201.length_ref, bf16[512,1536]{1,0:T(8,128)(2,1)} %fusion.4.x_ref.left_a_ref, ...), custom_call_target="tpu_custom_call" | custom-call | flops 24999999488 | bytes 10000000 | tf_op jit(solution)/shard_map/pallas_call | solution.py:307
  177.2 11.0 %all-gather.5.cloned.1.call-done.weight_ref.wo_ref = bf16[1536,1536]{1,0:T(8,128)(2,1)} async-done(((bf16[48,1536]{1,0:T(8,128)(2,1)}), bf16[1536,1536]{1,0:T(8,128)(2,1)}) %all-gather.5.cloned.1.call-update) | async-done | bytes 4718608 | tf_op jit(solution)/shard_map/all_gather | solution.py:641
  192.5 6.9 shard_map.303
  207.9 18.4 %shard_map.305 = (bf16[1,512,1536]{2,1,0:T(8,128)(2,1)}, bf16[1,512,1536]{2,1,0:T(8,128)(2,1)}, f32[1,512,128]{2,1,0:T(8,128)}, bf16[8,2,208,1536]{3,2,1,0:T(8,1...) custom-call(s32[1]{0:T(128)} %bitcast.9.first_ref, ...), custom_call_target="tpu_custom_call" | custom-call | flops 6543114240 | bytes 19562496 | tf_op jit(solution)/shard_map/pallas_call | solution.py:542
  228.1 43.1 %collective-permute-done.13 = bf16[512,1536]{1,0:T(8,128)(2,1)S(1)} collective-permute-done((bf16[512,1536]{1,0:T(8,128)(2,1)}, bf16[512,1536]{1,0:T(8,128)(2,1)S(1)}, u32[]{:S(2)}, u32[]{:S(2)}) %collective-permute-start.13) | collective-permute-done | bytes 1572896 | tf_op jit(solution)/shard_map/ppermute | solution.py:82
  275.4 3.9 pad_maximum_fusion.4.tok_ref
  281.4 30.1 %shard_map.306 = (bf16[2,512,1536]{2,1,0:T(8,128)(2,1)}, bf16[2,512,1536]{2,1,0:T(8,128)(2,1)}, f32[2,512,128]{2,1,0:T(8,128)}, bf16[8,2,208,1536]{3,2,1,0:T(8,1...) custom-call(s32[1]{0:T(128)} %bitcast.9.first_ref, ...), custom_call_target="tpu_custom_call", output_to_operand_aliasing={{3}: (10, {}), {4}: (11, {}), {5}: (12, {}), {6}: (13, {}),... | custom-call | flops 13086228480 | bytes 39124992 | tf_op jit(solution)/shard_map/pallas_call | solution.py:542
  311.6 3.5 pad_maximum_fusion.1.cot_ref
  320.3 6.2 collective-permute-done.11
  326.6 3.9 pad_maximum_fusion.2.tok_ref
  332.7 30.1 %shard_map.307 = (bf16[2,512,1536]{2,1,0:T(8,128)(2,1)}, bf16[2,512,1536]{2,1,0:T(8,128)(2,1)}, f32[2,512,128]{2,1,0:T(8,128)}, bf16[8,2,208,1536]{3,2,1,0:T(8,1...) custom-call(s32[1]{0:T(128)} %bitcast.9.first_ref, ...), custom_call_target="tpu_custom_call", output_to_operand_aliasing={{3}: (10, {}), {4}: (11, {}), {5}: (12, {}), {6}: (13, {}),... | custom-call | flops 13086228480 | bytes 39124992 | tf_op jit(solution)/shard_map/pallas_call | solution.py:542
  364.5 3.8 slice_bitcast_fusion.1
  372.5 3.4 pad_maximum_fusion.tok_ref
  375.9 30.4 %shard_map.308 = (bf16[2,512,1536]{2,1,0:T(8,128)(2,1)}, bf16[2,512,1536]{2,1,0:T(8,128)(2,1)}, f32[2,512,128]{2,1,0:T(8,128)}, bf16[8,2,208,1536]{3,2,1,0:T(8,1...) custom-call(s32[1]{0:T(128)} %bitcast.9.first_ref, ...), custom_call_target="tpu_custom_call", output_to_operand_aliasing={{3}: (10, {}), {4}: (11, {}), {5}: (12, {}), {6}: (13, {}),... | custom-call | flops 13086228480 | bytes 39124992 | tf_op jit(solution)/shard_map/pallas_call | solution.py:542
  415.4 18.8 %shard_map.309 = (bf16[1,512,1536]{2,1,0:T(8,128)(2,1)}, bf16[1,512,1536]{2,1,0:T(8,128)(2,1)}, f32[1,512,128]{2,1,0:T(8,128)}, bf16[8,2,208,1536]{3,2,1,0:T(8,1...) custom-call(s32[1]{0:T(128)} %bitcast.9.first_ref, ...), custom_call_target="tpu_custom_call", output_to_operand_aliasing={{3}: (10, {}), {4}: (11, {}), {5}: (12, {}), {6}: (13, {}),... | custom-call | flops 6543114240 | bytes 19562496 | tf_op jit(solution)/shard_map/pallas_call | solution.py:542
  441.6 4.0 all-to-all-start
  449.4 9.8 %bitcast_convert_fusion.2 = bf16[2,1536,512]{2,1,0:T(8,128)(2,1)S(1)} fusion(bf16[8,2,208,1536]{3,2,1,0:T(8,128)(2,1)} %get-tuple-element.105, bf16[8,2,208,512]{3,2,1,0:T(8,128)(2,1)} %get-tuple-element.106), kind=kOutput, calls=%fused_computation.8 | convolution fusion | flops 5236064256 | bytes 16777216 | tf_op jit(solution)/shard_map/necd,necf->edf/dot_general | solution.py:718
  460.5 3.7 collective-permute-done.22
  470.5 9.4 %bitcast_convert_fusion.1 = bf16[2,1536,512]{2,1,0:T(8,128)(2,1)} fusion(bf16[8,2,208,1536]{3,2,1,0:T(8,128)(2,1)S(1)} %bitcast.179, bf16[8,2,208,512]{3,2,1,0:T(8,128)(2,1)} %get-tuple-element.107), kind=kOutput, calls=%fused_computation.7 | convolution fusion | flops 5236064256 | bytes 16777216 | tf_op jit(solution)/shard_map/necd,necf->edf/dot_general | solution.py:719
  482.7 16.8 %collective-permute-done.27 = bf16[512,1536]{1,0:T(8,128)(2,1)S(1)} collective-permute-done((bf16[512,1536]{1,0:T(8,128)(2,1)}, bf16[512,1536]{1,0:T(8,128)(2,1)S(1)}, u32[]{:S(2)}, u32[]{:S(2)}) %collective-permute-start.27) | collective-permute-done | bytes 1572896 | tf_op jit(solution)/shard_map/ppermute | solution.py:82
  502.2 4.1 fusion.16
  508.3 6.3 bitcast_convert_fusion
  527.5 11.3 %collective-permute-done.24 = bf16[512,1536]{1,0:T(8,128)(2,1)} collective-permute-done((bf16[512,1536]{1,0:T(8,128)(2,1)}, bf16[512,1536]{1,0:T(8,128)(2,1)}, u32[]{:S(2)}, u32[]{:S(2)}) %collective-permute-start.24) | collective-permute-done | bytes 1572896 | tf_op jit(solution)/shard_map/ppermute | solution.py:82
  538.7 4.6 fusion.17
  551.4 11.9 %collective-permute-done.38 = bf16[1,1536,512]{2,1,0:T(8,128)(2,1)} collective-permute-done((bf16[1,1536,512]{2,1,0:T(8,128)(2,1)}, bf16[1,1536,512]{2,1,0:T(8,128)(2,1)}, u32[]{:S(2)}, u32[]{:S(2)}) %collective-permute-start.38) | collective-permute-done | bytes 1572896 | tf_op jit(solution)/shard_map/ppermute | solution.py:77
  563.4 3.5 add_convert_fusion.2.refs_3_
  566.8 8.1 collective-permute-done.25
  575.0 3.2 multiply_reduce_fusion
  586.4 29.3 %shard_map.312 = (bf16[512,1536]{1,0:T(8,128)(2,1)S(1)}, bf16[512,512]{1,0:T(8,128)(2,1)S(1)}, bf16[512,512]{1,0:T(8,128)(2,1)S(1)}) custom-call(s32[1]{0:T(128)} %copy.201.length_ref, bf16[512,1536]{1,0:T(8,128)(2,1)} %get-tuple-element.182.refs_8_.ga_ref.right_b_ref, bf16[1536,1536]{1,0:T(8,128)(2,1)} %all-gather.5.cloned.1.call-done.weight_ref.wo_ref, ...), custom_call_target="tpu_custom_call" | custom-call | flops 30000001024 | bytes 10000000 | tf_op jit(solution)/shard_map/pallas_call | solution.py:348
  624.9 11.7 %shard_map.314.refs_1_ = bf16[1536,4096]{1,0:T(8,128)(2,1)} custom-call(bf16[512,1536]{1,0:T(8,128)(2,1)S(1)} %copy-done.10, bf16[512,2560]{1,0:T(8,128)(2,1)} %shard_map.313.right_a_ref.refs_0_, bf16[512,1536]{1,0:T(8,128)(2,1)S(1)} %copy-done.6, bf16[512,1536]{1,0:T(8,128)(2,1)S(1)} %copy-done.4), custom_call_target="tpu_custom_call" | custom-call | flops 1000 | bytes 1000 | tf_op jit(solution)/shard_map/pallas_call | solution.py:425
  640.5 27.8 %collective-permute-done.35 = bf16[512,1536]{1,0:T(8,128)(2,1)S(1)} collective-permute-done((bf16[512,1536]{1,0:T(8,128)(2,1)}, bf16[512,1536]{1,0:T(8,128)(2,1)S(1)}, u32[]{:S(2)}, u32[]{:S(2)}) %collective-permute-start.35) | collective-permute-done | bytes 1572896 | tf_op jit(solution)/shard_map/ppermute | solution.py:82
  675.3 11.2 %fusion.5 = (bf16[1536]{0:T(1024)(128)(2,1)S(1)}, f32[512]{0:T(512)S(1)}, f32[512,1536]{1,0:T(8,128)}) fusion(f32[512]{0:T(512)S(1)} %copy-done.70, bf16[1,512,1536]{2,1,0:T(8,128)(2,1)} %param.22, f32[1536]{0:T(1024)S(1)} %copy-done.64, bf16[512,2560]{1,0:T(8,128)(2,1)} %shard_map.315, bf16[1536,2688]{1,0:T(8,128)(2,1)} %all-gather.3.cloned.1.call-done.wq_ref.wk_ref.wv_ref), kind=kOutput, calls=%fused_computation.18 | convolution fusion | flops 4032034816 | bytes 15217664 | tf_op jit(solution)/shard_map/sa,da->sd/dot_general | solution.py:760
  687.1 34.2 %collective-permute-done.36 = bf16[512,1536]{1,0:T(8,128)(2,1)} collective-permute-done((bf16[512,1536]{1,0:T(8,128)(2,1)}, bf16[512,1536]{1,0:T(8,128)(2,1)}, u32[]{:S(2)}, u32[]{:S(2)}) %collective-permute-start.36) | collective-permute-done | bytes 1572896 | tf_op jit(solution)/shard_map/ppermute | solution.py:82
  729.5 3.6 collective-permute-done.39
  734.1 4.3 collective-permute-done.40
  738.5 3.2 collective-permute-start.41
  741.7 5.9 fusion.11
  751.1 5.5 fusion.19
  758.6 50.5 %collective-permute-done.43 = bf16[18,1536]{1,0:T(8,128)(2,1)S(1)} collective-permute-done((bf16[18,1536]{1,0:T(8,128)(2,1)S(1)}, bf16[18,1536]{1,0:T(8,128)(2,1)S(1)}, u32[]{:S(2)}, u32[]{:S(2)}) %collective-permute-start.43) | collective-permute-done | bytes 55328 | tf_op jit(solution)/shard_map/ppermute | solution.py:77
  820.0 3.4 reduce-scatter.2.cloned.1.call-done
  824.4 8.5 all_gather.14
  832.9 8.7 %all_gather.15 = bf16[192,2048]{1,0:T(8,128)(2,1)S(1)} all-gather(bf16[48,2048]{1,0:T(8,128)(2,1)S(1)} %get-tuple-element.206), channel_id=1, replica_groups=mesh['rep'=4,'fsdp'=8] {'rep'}, dimensions={0}, use_global_device_ids=true | all-gather | bytes 983040 | tf_op jit(solution)/shard_map/all_gather | solution.py:744
  (392 shorter events, 207.3 us)
Async XLA Ops:
  7.2 138.2 %all-gather.3.cloned.1.call-start = ((), (), s32[]{:S(2)}) async-start(), calls=%async_computation.2 | async-start | bytes 8515584 | tf_op jit(solution)/shard_map/all_gather | solution.py:641
  12.6 175.7 %all-gather.5.cloned.1.call-start = ((), (), s32[]{:S(2)}) async-start(), calls=%async_computation.3 | async-start | bytes 4866048 | tf_op jit(solution)/shard_map/all_gather | solution.py:641
  23.7 10.7 %collective-permute-start.2 = (s32[4,16,512]{2,1,0:T(8,128)S(1)}, s32[4,16,512]{2,1,0:T(8,128)S(1)}, u32[]{:S(2)}, u32[]{:S(2)}) collective-permute-start(s32[4,16,512]{2,1,0:T(8,128)S(1)} %add_select_fusion), channel_id=1, source_target_pairs={{0,4},{1,5},{2,6},{3,7},{4,0},{5,1},{6,2},{7,3},{8,12},{9,13},{10,... | collective-permute-start | bytes 393224 | tf_op jit(solution)/shard_map/ppermute | solution.py:77
  35.5 57.2 %collective-permute-start.4 = (bf16[512,1536]{1,0:T(8,128)(2,1)}, bf16[512,1536]{1,0:T(8,128)(2,1)}, u32[]{:S(2)}, u32[]{:S(2)}) collective-permute-start(bf16[512,1536]{1,0:T(8,128)(2,1)} %shard_map.302), channel_id=1, source_target_pairs={{0,2},{2,4},{4,6},{6,7},{7,5},{5,3},{3,1},{1,0},{8,10},{10,12},{12... | collective-permute-start | bytes 4718600 | tf_op jit(solution)/shard_map/ppermute | solution.py:82
  37.9 63.7 %collective-permute-start.3 = (bf16[512,1536]{1,0:T(8,128)(2,1)}, bf16[512,1536]{1,0:T(8,128)(2,1)}, u32[]{:S(2)}, u32[]{:S(2)}) collective-permute-start(bf16[512,1536]{1,0:T(8,128)(2,1)} %shard_map.302), channel_id=1, source_target_pairs={{0,1},{2,0},{4,2},{6,4},{7,6},{5,7},{3,5},{1,3},{8,9},{10,8},{12,1... | collective-permute-start | bytes 4718600 | tf_op jit(solution)/shard_map/ppermute | solution.py:82
  92.7 47.0 %collective-permute-start.6 = (bf16[512,1536]{1,0:T(8,128)(2,1)}, bf16[512,1536]{1,0:T(8,128)(2,1)S(1)}, u32[]{:S(2)}, u32[]{:S(2)}) collective-permute-start(bf16[512,1536]{1,0:T(8,128)(2,1)} %collective-permute-done.4.rest_1_), channel_id=1, source_target_pairs={{0,2},{2,4},{4,6},{6,7},{7,5},{5,3},{3,1},{1,0},{8,10},{10,12},{12... | collective-permute-start | bytes 4718600 | tf_op jit(solution)/shard_map/ppermute | solution.py:82
  101.6 40.5 %collective-permute-start.5 = (bf16[512,1536]{1,0:T(8,128)(2,1)}, bf16[512,1536]{1,0:T(8,128)(2,1)}, u32[]{:S(2)}, u32[]{:S(2)}) collective-permute-start(bf16[512,1536]{1,0:T(8,128)(2,1)} %collective-permute-done.3.rest_0_), channel_id=1, source_target_pairs={{0,1},{2,0},{4,2},{6,4},{7,6},{5,7},{3,5},{1,3},{8,9},{10,8},{12,1... | collective-permute-start | bytes 4718600 | tf_op jit(solution)/shard_map/ppermute | solution.py:82
  199.3 76.1 %collective-permute-start.10 = (bf16[512,1536]{1,0:T(8,128)(2,1)}, bf16[512,1536]{1,0:T(8,128)(2,1)}, u32[]{:S(2)}, u32[]{:S(2)}) collective-permute-start(bf16[512,1536]{1,0:T(8,128)(2,1)} %get-tuple-element.76), channel_id=1, source_target_pairs={{0,1},{2,0},{4,2},{6,4},{7,6},{5,7},{3,5},{1,3},{8,9},{10,8},{12,1... | collective-permute-start | bytes 4718600 | tf_op jit(solution)/shard_map/ppermute | solution.py:82
  200.8 74.6 %collective-permute-start.7 = (bf16[512,1536]{1,0:T(8,128)(2,1)}, bf16[512,1536]{1,0:T(8,128)(2,1)}, u32[]{:S(2)}, u32[]{:S(2)}) collective-permute-start(bf16[512,1536]{1,0:T(8,128)(2,1)} %get-tuple-element.76), channel_id=1, source_target_pairs={{0,2},{2,4},{4,6},{6,7},{7,5},{5,3},{3,1},{1,0},{8,10},{10,12},{12... | collective-permute-start | bytes 4718600 | tf_op jit(solution)/shard_map/ppermute | solution.py:82
  201.3 69.8 %collective-permute-start.13 = (bf16[512,1536]{1,0:T(8,128)(2,1)}, bf16[512,1536]{1,0:T(8,128)(2,1)S(1)}, u32[]{:S(2)}, u32[]{:S(2)}) collective-permute-start(bf16[512,1536]{1,0:T(8,128)(2,1)} %get-tuple-element.77), channel_id=1, source_target_pairs={{0,2},{2,4},{4,6},{6,7},{7,5},{5,3},{3,1},{1,0},{8,10},{10,12},{12... | collective-permute-start | bytes 4718600 | tf_op jit(solution)/shard_map/ppermute | solution.py:82
  203.3 68.6 %collective-permute-start.14 = (bf16[512,1536]{1,0:T(8,128)(2,1)}, bf16[512,1536]{1,0:T(8,128)(2,1)}, u32[]{:S(2)}, u32[]{:S(2)}) collective-permute-start(bf16[512,1536]{1,0:T(8,128)(2,1)} %get-tuple-element.78), channel_id=1, source_target_pairs={{0,1},{2,0},{4,2},{6,4},{7,6},{5,7},{3,5},{1,3},{8,9},{10,8},{12,1... | collective-permute-start | bytes 4718600 | tf_op jit(solution)/shard_map/ppermute | solution.py:82
  271.2 46.5 %collective-permute-start.17 = (bf16[256,1536]{1,0:T(8,128)(2,1)S(1)}, bf16[256,1536]{1,0:T(8,128)(2,1)}, u32[]{:S(2)}, u32[]{:S(2)}) collective-permute-start(bf16[256,1536]{1,0:T(8,128)(2,1)S(1)} %slice.238), channel_id=1, source_target_pairs={{0,2},{2,4},{4,6},{6,7},{7,5},{5,3},{3,1},{1,0},{8,10},{10,12},{12... | collective-permute-start | bytes 2359304 | tf_op jit(solution)/shard_map/ppermute | solution.py:82
  273.9 43.8 %collective-permute-start.18 = (bf16[256,1536]{1,0:T(8,128)(2,1)}, bf16[256,1536]{1,0:T(8,128)(2,1)}, u32[]{:S(2)}, u32[]{:S(2)}) collective-permute-start(bf16[256,1536]{1,0:T(8,128)(2,1)} %slice.239), channel_id=1, source_target_pairs={{0,1},{2,0},{4,2},{6,4},{7,6},{5,7},{3,5},{1,3},{8,9},{10,8},{12,1... | collective-permute-start | bytes 2359304 | tf_op jit(solution)/shard_map/ppermute | solution.py:82
  279.2 47.3 %collective-permute-start.11 = (bf16[512,1536]{1,0:T(8,128)(2,1)}, bf16[512,1536]{1,0:T(8,128)(2,1)}, u32[]{:S(2)}, u32[]{:S(2)}) collective-permute-start(bf16[512,1536]{1,0:T(8,128)(2,1)} %collective-permute-done.10), channel_id=1, source_target_pairs={{0,1},{2,0},{4,2},{6,4},{7,6},{5,7},{3,5},{1,3},{8,9},{10,8},{12,1... | collective-permute-start | bytes 4718600 | tf_op jit(solution)/shard_map/ppermute | solution.py:82
  281.0 45.6 %collective-permute-start.8 = (bf16[512,1536]{1,0:T(8,128)(2,1)}, bf16[512,1536]{1,0:T(8,128)(2,1)}, u32[]{:S(2)}, u32[]{:S(2)}) collective-permute-start(bf16[512,1536]{1,0:T(8,128)(2,1)} %collective-permute-done.7), channel_id=1, source_target_pairs={{0,2},{2,4},{4,6},{6,7},{7,5},{5,3},{3,1},{1,0},{8,10},{10,12},{12... | collective-permute-start | bytes 4718600 | tf_op jit(solution)/shard_map/ppermute | solution.py:82
  330.5 37.8 %collective-permute-start.12 = (bf16[512,1536]{1,0:T(8,128)(2,1)}, bf16[512,1536]{1,0:T(8,128)(2,1)S(1)}, u32[]{:S(2)}, u32[]{:S(2)}) collective-permute-start(bf16[512,1536]{1,0:T(8,128)(2,1)} %collective-permute-done.11), channel_id=1, source_target_pairs={{0,1},{2,0},{4,2},{6,4},{7,6},{5,7},{3,5},{1,3},{8,9},{10,8},{12,1... | collective-permute-start | bytes 4718600 | tf_op jit(solution)/shard_map/ppermute | solution.py:82
  331.8 37.9 %collective-permute-start.9 = (bf16[512,1536]{1,0:T(8,128)(2,1)}, bf16[512,1536]{1,0:T(8,128)(2,1)}, u32[]{:S(2)}, u32[]{:S(2)}) collective-permute-start(bf16[512,1536]{1,0:T(8,128)(2,1)} %collective-permute-done.8), channel_id=1, source_target_pairs={{0,2},{2,4},{4,6},{6,7},{7,5},{5,3},{3,1},{1,0},{8,10},{10,12},{12... | collective-permute-start | bytes 4718600 | tf_op jit(solution)/shard_map/ppermute | solution.py:82
  368.3 44.4 %collective-permute-start.16 = (bf16[256,1536]{1,0:T(8,128)(2,1)S(1)}, bf16[256,1536]{1,0:T(8,128)(2,1)}, u32[]{:S(2)}, u32[]{:S(2)}) collective-permute-start(bf16[256,1536]{1,0:T(8,128)(2,1)S(1)} %slice.237), channel_id=1, source_target_pairs={{0,1},{2,0},{4,2},{6,4},{7,6},{5,7},{3,5},{1,3},{8,9},{10,8},{12,1... | collective-permute-start | bytes 2359304 | tf_op jit(solution)/shard_map/ppermute | solution.py:82
  371.8 40.9 %collective-permute-start.15 = (bf16[256,1536]{1,0:T(8,128)(2,1)}, bf16[256,1536]{1,0:T(8,128)(2,1)}, u32[]{:S(2)}, u32[]{:S(2)}) collective-permute-start(bf16[256,1536]{1,0:T(8,128)(2,1)} %slice.236), channel_id=1, source_target_pairs={{0,2},{2,4},{4,6},{6,7},{7,5},{5,3},{3,1},{1,0},{8,10},{10,12},{12... | collective-permute-start | bytes 2359304 | tf_op jit(solution)/shard_map/ppermute | solution.py:82
  441.6 76.0 %all-to-all-start = ((f32[8,2,512]{2,1,0:T(2,128)}), f32[8,2,512]{2,1,0:T(2,128)}, u32[]{:S(2)}, u32[]{:S(2)}) async-start(f32[8,2,512]{2,1,0:T(2,128)} %gather_fusion.3), calls=%async_computation | async-start | bytes 65536 | tf_op jit(solution)/shard_map/all_to_all | solution.py:714
  445.6 377.8 %reduce-scatter.2.cloned.1.call-start = ((), (), s32[]{:S(2)}) async-start(), calls=%async_computation.4 | async-start | bytes 12976128 | tf_op jit(solution)/shard_map/reduce_scatter | solution.py:743
  447.3 16.9 %collective-permute-start.22 = (bf16[256,1536]{1,0:T(8,128)(2,1)S(1)}, bf16[256,1536]{1,0:T(8,128)(2,1)S(1)}, u32[]{:S(2)}, u32[]{:S(2)}) collective-permute-start(bf16[256,1536]{1,0:T(8,128)(2,1)S(1)} %get-tuple-element.203), channel_id=1, source_target_pairs={{0,2},{2,4},{4,6},{6,7},{7,5},{5,3},{3,1},{1,0},{8,10},{10,12},{12... | collective-permute-start | bytes 2359304 | tf_op jit(solution)/shard_map/ppermute | solution.py:82
  449.2 16.2 %collective-permute-start.26 = (bf16[256,1536]{1,0:T(8,128)(2,1)S(1)}, bf16[256,1536]{1,0:T(8,128)(2,1)S(1)}, u32[]{:S(2)}, u32[]{:S(2)}) collective-permute-start(bf16[256,1536]{1,0:T(8,128)(2,1)S(1)} %get-tuple-element.204), channel_id=1, source_target_pairs={{0,1},{2,0},{4,2},{6,4},{7,6},{5,7},{3,5},{1,3},{8,9},{10,8},{12,1... | collective-permute-start | bytes 2359304 | tf_op jit(solution)/shard_map/ppermute | solution.py:82
  460.4 62.6 %collective-permute-start.19 = (bf16[1,1536,512]{2,1,0:T(8,128)(2,1)}, bf16[1,1536,512]{2,1,0:T(8,128)(2,1)}, u32[]{:S(2)}, u32[]{:S(2)}) collective-permute-start(bf16[1,1536,512]{2,1,0:T(8,128)(2,1)} %constant_dynamic-slice_fusion.2), channel_id=1, source_target_pairs={{0,8},{8,0},{16,24},{24,16},{1,9},{9,1},{17,25},{25,17},{2,10},{10... | collective-permute-start | bytes 4718600 | tf_op jit(solution)/shard_map/ppermute | solution.py:77
  467.1 32.4 %collective-permute-start.27 = (bf16[512,1536]{1,0:T(8,128)(2,1)}, bf16[512,1536]{1,0:T(8,128)(2,1)S(1)}, u32[]{:S(2)}, u32[]{:S(2)}) collective-permute-start(bf16[512,1536]{1,0:T(8,128)(2,1)} %pad_maximum_fusion.8), channel_id=1, source_target_pairs={{0,1},{2,0},{4,2},{6,4},{7,6},{5,7},{3,5},{1,3},{8,9},{10,8},{12,1... | collective-permute-start | bytes 4718600 | tf_op jit(solution)/shard_map/ppermute | solution.py:82
  468.8 33.4 %collective-permute-start.23 = (bf16[512,1536]{1,0:T(8,128)(2,1)}, bf16[512,1536]{1,0:T(8,128)(2,1)}, u32[]{:S(2)}, u32[]{:S(2)}) collective-permute-start(bf16[512,1536]{1,0:T(8,128)(2,1)} %pad_maximum_fusion.7), channel_id=1, source_target_pairs={{0,2},{2,4},{4,6},{6,7},{7,5},{5,3},{3,1},{1,0},{8,10},{10,12},{12... | collective-permute-start | bytes 4718600 | tf_op jit(solution)/shard_map/ppermute | solution.py:82
  482.7 62.7 %collective-permute-start.20 = (bf16[1,1536,512]{2,1,0:T(8,128)(2,1)}, bf16[1,1536,512]{2,1,0:T(8,128)(2,1)}, u32[]{:S(2)}, u32[]{:S(2)}) collective-permute-start(bf16[1,1536,512]{2,1,0:T(8,128)(2,1)} %constant_dynamic-slice_fusion.1), channel_id=1, source_target_pairs={{0,8},{8,0},{16,24},{24,16},{1,9},{9,1},{17,25},{25,17},{2,10},{10... | collective-permute-start | bytes 4718600 | tf_op jit(solution)/shard_map/ppermute | solution.py:77
  506.3 32.5 %collective-permute-start.24 = (bf16[512,1536]{1,0:T(8,128)(2,1)}, bf16[512,1536]{1,0:T(8,128)(2,1)}, u32[]{:S(2)}, u32[]{:S(2)}) collective-permute-start(bf16[512,1536]{1,0:T(8,128)(2,1)} %get-tuple-element.187), channel_id=1, source_target_pairs={{0,2},{2,4},{4,6},{6,7},{7,5},{5,3},{3,1},{1,0},{8,10},{10,12},{12... | collective-permute-start | bytes 4718600 | tf_op jit(solution)/shard_map/ppermute | solution.py:82
  506.7 32.0 %collective-permute-start.28 = (bf16[512,1536]{1,0:T(8,128)(2,1)}, bf16[512,1536]{1,0:T(8,128)(2,1)}, u32[]{:S(2)}, u32[]{:S(2)}) collective-permute-start(bf16[512,1536]{1,0:T(8,128)(2,1)} %get-tuple-element.188), channel_id=1, source_target_pairs={{0,1},{2,0},{4,2},{6,4},{7,6},{5,7},{3,5},{1,3},{8,9},{10,8},{12,1... | collective-permute-start | bytes 4718600 | tf_op jit(solution)/shard_map/ppermute | solution.py:82
  517.6 30.9 %collective-permute-start.21 = (bf16[1,512,1536]{2,1,0:T(8,128)(2,1)}, bf16[1,512,1536]{2,1,0:T(8,128)(2,1)}, u32[]{:S(2)}, u32[]{:S(2)}) collective-permute-start(bf16[1,512,1536]{2,1,0:T(8,128)(2,1)} %constant_dynamic-slice_fusion), channel_id=1, source_target_pairs={{0,8},{8,0},{16,24},{24,16},{1,9},{9,1},{17,25},{25,17},{2,10},{10... | collective-permute-start | bytes 4718600 | tf_op jit(solution)/shard_map/ppermute | solution.py:77
  526.2 37.1 %collective-permute-start.38 = (bf16[1,1536,512]{2,1,0:T(8,128)(2,1)}, bf16[1,1536,512]{2,1,0:T(8,128)(2,1)}, u32[]{:S(2)}, u32[]{:S(2)}) collective-permute-start(bf16[1,1536,512]{2,1,0:T(8,128)(2,1)} %add_convert_fusion.9.refs_1_), channel_id=1, source_target_pairs={{0,16},{8,24},{16,0},{24,8},{1,17},{9,25},{17,1},{25,9},{2,18},{10... | collective-permute-start | bytes 4718600 | tf_op jit(solution)/shard_map/ppermute | solution.py:77
  543.4 31.5 %collective-permute-start.25 = (bf16[512,1536]{1,0:T(8,128)(2,1)}, bf16[512,1536]{1,0:T(8,128)(2,1)}, u32[]{:S(2)}, u32[]{:S(2)}) collective-permute-start(bf16[512,1536]{1,0:T(8,128)(2,1)} %get-tuple-element.185), channel_id=1, source_target_pairs={{0,2},{2,4},{4,6},{6,7},{7,5},{5,3},{3,1},{1,0},{8,10},{10,12},{12... | collective-permute-start | bytes 4718600 | tf_op jit(solution)/shard_map/ppermute | solution.py:82
  544.1 30.8 %collective-permute-start.29 = (bf16[512,1536]{1,0:T(8,128)(2,1)}, bf16[512,1536]{1,0:T(8,128)(2,1)}, u32[]{:S(2)}, u32[]{:S(2)}) collective-permute-start(bf16[512,1536]{1,0:T(8,128)(2,1)} %get-tuple-element.186), channel_id=1, source_target_pairs={{0,1},{2,0},{4,2},{6,4},{7,6},{5,7},{3,5},{1,3},{8,9},{10,8},{12,1... | collective-permute-start | bytes 4718600 | tf_op jit(solution)/shard_map/ppermute | solution.py:82
  584.3 33.1 %collective-permute-start.30 = (bf16[256,1536]{1,0:T(8,128)(2,1)S(1)}, bf16[256,1536]{1,0:T(8,128)(2,1)S(1)}, u32[]{:S(2)}, u32[]{:S(2)}) collective-permute-start(bf16[256,1536]{1,0:T(8,128)(2,1)S(1)} %get-tuple-element.201), channel_id=1, source_target_pairs={{0,2},{2,4},{4,6},{6,7},{7,5},{5,3},{3,1},{1,0},{8,10},{10,12},{12... | collective-permute-start | bytes 2359304 | tf_op jit(solution)/shard_map/ppermute | solution.py:82
  585.7 33.5 %collective-permute-start.34 = (bf16[256,1536]{1,0:T(8,128)(2,1)S(1)}, bf16[256,1536]{1,0:T(8,128)(2,1)S(1)}, u32[]{:S(2)}, u32[]{:S(2)}) collective-permute-start(bf16[256,1536]{1,0:T(8,128)(2,1)S(1)} %get-tuple-element.202), channel_id=1, source_target_pairs={{0,1},{2,0},{4,2},{6,4},{7,6},{5,7},{3,5},{1,3},{8,9},{10,8},{12,1... | collective-permute-start | bytes 2359304 | tf_op jit(solution)/shard_map/ppermute | solution.py:82
  636.7 31.6 %collective-permute-start.35 = (bf16[512,1536]{1,0:T(8,128)(2,1)}, bf16[512,1536]{1,0:T(8,128)(2,1)S(1)}, u32[]{:S(2)}, u32[]{:S(2)}) collective-permute-start(bf16[512,1536]{1,0:T(8,128)(2,1)} %pad_maximum_fusion.10.refs_2_), channel_id=1, source_target_pairs={{0,1},{2,0},{4,2},{6,4},{7,6},{5,7},{3,5},{1,3},{8,9},{10,8},{12,1... | collective-permute-start | bytes 4718600 | tf_op jit(solution)/shard_map/ppermute | solution.py:82
  638.4 34.6 %collective-permute-start.31 = (bf16[512,1536]{1,0:T(8,128)(2,1)}, bf16[512,1536]{1,0:T(8,128)(2,1)S(1)}, u32[]{:S(2)}, u32[]{:S(2)}) collective-permute-start(bf16[512,1536]{1,0:T(8,128)(2,1)} %pad_maximum_fusion.9.refs_1_), channel_id=1, source_target_pairs={{0,2},{2,4},{4,6},{6,7},{7,5},{5,3},{3,1},{1,0},{8,10},{10,12},{12... | collective-permute-start | bytes 4718600 | tf_op jit(solution)/shard_map/ppermute | solution.py:82
  640.5 101.2 %collective-permute-start.44 = (bf16[1,1536,512]{2,1,0:T(8,128)(2,1)}, bf16[1,1536,512]{2,1,0:T(8,128)(2,1)}, u32[]{:S(2)}, u32[]{:S(2)}) collective-permute-start(bf16[1,1536,512]{2,1,0:T(8,128)(2,1)} %add_convert_fusion.2.refs_3_), channel_id=1, source_target_pairs={{0,8},{8,0},{16,24},{24,16},{1,9},{9,1},{17,25},{25,17},{2,10},{10... | collective-permute-start | bytes 4718600 | tf_op jit(solution)/shard_map/ppermute | solution.py:77
  671.3 50.0 %collective-permute-start.36 = (bf16[512,1536]{1,0:T(8,128)(2,1)}, bf16[512,1536]{1,0:T(8,128)(2,1)}, u32[]{:S(2)}, u32[]{:S(2)}) collective-permute-start(bf16[512,1536]{1,0:T(8,128)(2,1)} %add_convert_fusion.4.refs_3_), channel_id=1, source_target_pairs={{0,1},{2,0},{4,2},{6,4},{7,6},{5,7},{3,5},{1,3},{8,9},{10,8},{12,1... | collective-permute-start | bytes 4718600 | tf_op jit(solution)/shard_map/ppermute | solution.py:82
  674.6 49.7 %collective-permute-start.32 = (bf16[512,1536]{1,0:T(8,128)(2,1)}, bf16[512,1536]{1,0:T(8,128)(2,1)}, u32[]{:S(2)}, u32[]{:S(2)}) collective-permute-start(bf16[512,1536]{1,0:T(8,128)(2,1)} %add_convert_fusion.6.refs_2_), channel_id=1, source_target_pairs={{0,2},{2,4},{4,6},{6,7},{7,5},{5,3},{3,1},{1,0},{8,10},{10,12},{12... | collective-permute-start | bytes 4718600 | tf_op jit(solution)/shard_map/ppermute | solution.py:82
  727.3 5.8 collective-permute-start.39
  738.5 9.1 %collective-permute-start.41 = (bf16[18,1536]{1,0:T(8,128)(2,1)S(1)}, bf16[18,1536]{1,0:T(8,128)(2,1)S(1)}, u32[]{:S(2)}, u32[]{:S(2)}) collective-permute-start(bf16[18,1536]{1,0:T(8,128)(2,1)S(1)} %add_convert_fusion.14), channel_id=1, source_target_pairs={{0,4},{1,5},{2,6},{3,7},{4,0},{5,1},{6,2},{7,3},{8,12},{9,13},{10,... | collective-permute-start | bytes 165896 | tf_op jit(solution)/shard_map/ppermute | solution.py:77
  747.6 61.6 %collective-permute-start.47 = (bf16[1,512,1536]{2,1,0:T(8,128)(2,1)}, bf16[1,512,1536]{2,1,0:T(8,128)(2,1)S(1)}, u32[]{:S(2)}, u32[]{:S(2)}) collective-permute-start(bf16[1,512,1536]{2,1,0:T(8,128)(2,1)} %get-tuple-element.135), channel_id=1, source_target_pairs={{0,16},{8,24},{16,0},{24,8},{1,17},{9,25},{17,1},{25,9},{2,18},{10... | collective-permute-start | bytes 4718600 | tf_op jit(solution)/shard_map/ppermute | solution.py:77
  748.3 61.4 %collective-permute-start.45 = (bf16[1,1536,512]{2,1,0:T(8,128)(2,1)}, bf16[1,1536,512]{2,1,0:T(8,128)(2,1)S(1)}, u32[]{:S(2)}, u32[]{:S(2)}) collective-permute-start(bf16[1,1536,512]{2,1,0:T(8,128)(2,1)} %get-tuple-element.134), channel_id=1, source_target_pairs={{0,16},{8,24},{16,0},{24,8},{1,17},{9,25},{17,1},{25,9},{2,18},{10... | collective-permute-start | bytes 4718600 | tf_op jit(solution)/shard_map/ppermute | solution.py:77
  749.8 59.3 %collective-permute-start.43 = (bf16[18,1536]{1,0:T(8,128)(2,1)S(1)}, bf16[18,1536]{1,0:T(8,128)(2,1)S(1)}, u32[]{:S(2)}, u32[]{:S(2)}) collective-permute-start(bf16[18,1536]{1,0:T(8,128)(2,1)S(1)} %add_convert_fusion.12), channel_id=1, source_target_pairs={{0,16},{8,24},{16,0},{24,8},{1,17},{9,25},{17,1},{25,9},{2,18},{10... | collective-permute-start | bytes 165896 | tf_op jit(solution)/shard_map/ppermute | solution.py:77
  756.6 55.3 %collective-permute-start.37 = (bf16[512,1536]{1,0:T(8,128)(2,1)S(1)}, bf16[512,1536]{1,0:T(8,128)(2,1)S(1)}, u32[]{:S(2)}, u32[]{:S(2)}) collective-permute-start(bf16[512,1536]{1,0:T(8,128)(2,1)S(1)} %copy-done.35), channel_id=1, source_target_pairs={{0,1},{2,0},{4,2},{6,4},{7,6},{5,7},{3,5},{1,3},{8,9},{10,8},{12,1... | collective-permute-start | bytes 4718600 | tf_op jit(solution)/shard_map/ppermute | solution.py:82
  756.8 55.1 %collective-permute-start.33 = (bf16[512,1536]{1,0:T(8,128)(2,1)S(1)}, bf16[512,1536]{1,0:T(8,128)(2,1)S(1)}, u32[]{:S(2)}, u32[]{:S(2)}) collective-permute-start(bf16[512,1536]{1,0:T(8,128)(2,1)S(1)} %copy-done.36), channel_id=1, source_target_pairs={{0,2},{2,4},{4,6},{6,7},{7,5},{5,3},{3,1},{1,0},{8,10},{10,12},{12... | collective-permute-start | bytes 4718600 | tf_op jit(solution)/shard_map/ppermute | solution.py:82
  810.2 6.8 collective-permute-start.46
  (92 other events, 2244.4 us)
Sparse Core Ops, SparseCore 0:
  12.7 103.1 all-gather.2
  119.4 68.7 all-gather.4
  636.8 186.5 reduce-scatter.1

commit v4 on v3

--- a/solution.py
+++ b/solution.py
@@ -122,11 +122,13 @@
         half = far.shape[0] // 2
         top = shift(far[:half], order, 1)
         bottom = shift(far[half:], order, -1)
+        first = [top, bottom]
         ahead, back = parts[near], parts[-near]
         ahead = jnp.concatenate([add_low(ahead[:half], top), ahead[half:]], axis=0)
         back = jnp.concatenate([back[:half], add_low(back[half:], bottom)], axis=0)
     else:
         ahead, back = parts[near], parts[-near]
+        first = []
     stages = [[ahead, back]]
     for step in range(near, 0, -1):
         ahead = shift(ahead, order, 1)
@@ -135,7 +137,7 @@
             ahead = add_low(parts[step - 1], ahead)
             back = add_low(parts[1 - step], back)
         stages.append([ahead, back])
-    return ahead, back, stages
+    return ahead, back, stages, first
 
 
 def three_way(value):
@@ -725,7 +727,7 @@
         other = lax.dynamic_index_in_dim(pairs, 1 - core_bit, 1, keepdims=False)
         expert_sums.append(add_low(mine, swap(other, "rep", 1)))
 
-    left, right, _ = ring_scatter(grad_parts, order)
+    left, right, *_ = ring_scatter(grad_parts, order)
     (own_grads,) = tie([grad_parts[0]], expert_sums)
     grad_normed_two = own_grads.astype(F32) + left.astype(F32) + right.astype(F32)
 
@@ -745,7 +747,7 @@
 
     keys = sorted(out_parts)
     held = dict(zip(keys, tie([out_parts[o] for o in keys], [grad_attn])))
-    out_left, out_right, stages = ring_scatter(held, order)
+    out_left, out_right, stages, first_hop = ring_scatter(held, order)
     mixture = held[0].astype(F32) + out_left.astype(F32) + out_right.astype(F32)
     output = jnp.where(valid_rows, hidden + mixture, 0.0).astype(BF16)
 
@@ -754,13 +756,18 @@
     )
     projected = jnp.concatenate([grad_queries, grad_keys, grad_values], axis=1)
     crossed = [add_low(expert_sums[0], swap(expert_sums[0], "rep", 2))]
-    (projected,) = tie([projected], [*stages[0], *crossed])
+    (projected,) = tie([projected], [*first_hop, *crossed])
     grad_qkv = joint_grad(attention_normed, projected, mixed, grad_attn)
     (projected,) = tie([projected], [grad_qkv, *stages[min(1, len(stages) - 1)]])
     grad_normed_one = jnp.einsum("sa,da->sd", projected, full_qkv, preferred_element_type=F32)
     grad_tokens_norm, grad_gain_attn = norm_one_pull(grad_normed_one)
     grad_input = (grad_hidden + grad_tokens_norm).astype(BF16)
-    total_first = jnp.concatenate(reduce_weight(grad_qkv), axis=1).astype(F32)
+    total_low, total_high = reduce_weight(grad_qkv)
+    middle = total_low.shape[1]
+    starts = (0, q_width, q_width + k_width, q_width + 2 * k_width)
+    sides = [(total_low, a) if a < middle else (total_high, a - middle) for a in starts]
+    sizes = (q_width, k_width, k_width, width)
+    totals = [side[:, a : a + n].astype(F32) for (side, a), n in zip(sides, sizes)]
     small_sum = jnp.concatenate([grad_router, grad_gain_attn[None], grad_gain_moe[None]], axis=0)
     (small_sum,) = tie([small_sum.astype(BF16)], stages[min(2, len(stages) - 1)])
     for axis, size in (("fsdp", groups), ("rep", replicas)):
@@ -786,10 +793,7 @@
         grad_input[None],
         small_sum[experts],
         small_sum[experts + 1],
-        total_first[:, :q_width],
-        total_first[:, q_width : q_width + k_width],
-        total_first[:, q_width + k_width : q_width + 2 * k_width],
-        total_first[:, q_width + 2 * k_width :],
+        *totals,
         small_sum[:experts].T,
         *expert_grads,
     )

time: 857 us -> 869 us (1.014)
  waiting for transfers between devices: 323 us -> 337 us
    ppermute x32, waiting for transfers between devices: 229 us -> 243 us  [shift(): lax.ppermute(value, 'fsdp', [(order[i], order[(i + step) % size]) for i i...]
    unnamed x183 -> x189, local copies, waits for them, and re-layouts: 28.3 us -> 25.2 us
where the time goes in v4:
time: 869 us; the launch traced here: 864 us
  waiting for transfers between devices  337 us (39%)
  Pallas kernels  201 us (23%)
  other arithmetic  115 us (13%)
  local copies, waits for them, and re-layouts  77.1 us (9%)
  starting transfers between devices  55.9 us (6%)
  matrix products  43.4 us (5%)
  between operations  18.3 us (2%)
  blocking collectives  17.2 us (2%)
    ppermute x32, waiting for transfers between devices, shift(): lax.ppermute(value, 'fsdp', [(order[i], order[(i + step) % size]) for i i...  243 us
    pallas_call x5, Pallas kernels, run_experts(): pl.pallas_call(functools.partial(expert_kernel, padded=padded), out_shape...  128 us
    ppermute x17, waiting for transfers between devices, swap(): return lax.ppermute(value, axis, [(i, i ^ bit) for i in range(size)])  82.9 us
    convert_element_type x19, other arithmetic, add_low(): return (left.astype(F32) + right.astype(F32)).astype(BF16)  35.3 us
    ppermute x32, starting transfers between devices, shift(): lax.ppermute(value, 'fsdp', [(order[i], order[(i + step) % size]) for i i...  35.1 us
    pallas_call x1, Pallas kernels, attention_back(): pl.pallas_call(attention_back_kernel, out_shape=[jax.ShapeDtypeStruct(s,...  29.3 us
    unnamed x189, local copies, waits for them, and re-layouts  25.2 us
    pallas_call x1, Pallas kernels, attention(): pl.pallas_call(attention_kernel, out_shape=[jax.ShapeDtypeStruct(s, BF16)...  24.7 us
  transfers between devices with their start and end apart: 53, of which 23 were waited for; matrix products, arithmetic and copies ran while one was open for 22% of the time, Pallas kernels for 19%

profile of v4, /device:TPU:0, one launch (start us, length us, event | category | flops | bytes accessed | tf_op | source)
XLA Modules:
  0.0 864.3 jit_solution(17002476447846963052)
XLA Ops:
  30.1 6.3 collective-permute-done.2
  50.9 43.8 %collective-permute-done.4.rest_1_ = bf16[512,1536]{1,0:T(8,128)(2,1)} collective-permute-done((bf16[512,1536]{1,0:T(8,128)(2,1)}, bf16[512,1536]{1,0:T(8,128)(2,1)}, u32[]{:S(2)}, u32[]{:S(2)}) %collective-permute-start.4) | collective-permute-done | bytes 1572896 | tf_op jit(solution)/shard_map/ppermute | solution.py:82
  97.2 6.4 collective-permute-done.3.rest_0_
  116.0 3.8 pad_maximum_fusion.5.cot_ref
  119.8 21.9 %collective-permute-done.6.rest_3_.refs_0_ = bf16[512,1536]{1,0:T(8,128)(2,1)S(1)} collective-permute-done((bf16[512,1536]{1,0:T(8,128)(2,1)}, bf16[512,1536]{1,0:T(8,128)(2,1)S(1)}, u32[]{:S(2)}, u32[]{:S(2)}) %collective-permute-start.6) | collective-permute-done | bytes 1572896 | tf_op jit(solution)/shard_map/ppermute | solution.py:82
  144.0 3.3 pad_maximum_fusion.3.cot_ref
  150.9 24.7 %shard_map.301 = (bf16[512,1536]{1,0:T(8,128)(2,1)S(1)}, bf16[512,512]{1,0:T(8,128)(2,1)S(1)}, bf16[512,512]{1,0:T(8,128)(2,1)S(1)}, bf16[512,1536]{1,0:T(8,128)(2,1)}, f32[4,512,128]{2,1,0:T(8,128)S(1)}) custom-call(s32[1]{0:T(128)} %copy.201.length_ref, bf16[512,1536]{1,0:T(8,128)(2,1)} %fusion.4.x_ref.left_a_ref, ...), custom_call_target="tpu_custom_call" | custom-call | flops 24999999488 | bytes 10000000 | tf_op jit(solution)/shard_map/pallas_call | solution.py:309
  179.3 11.0 %all-gather.5.cloned.1.call-done.weight_ref.wo_ref = bf16[1536,1536]{1,0:T(8,128)(2,1)} async-done(((bf16[48,1536]{1,0:T(8,128)(2,1)}), bf16[1536,1536]{1,0:T(8,128)(2,1)}) %all-gather.5.cloned.1.call-update) | async-done | bytes 4718608 | tf_op jit(solution)/shard_map/all_gather | solution.py:643
  194.5 6.8 shard_map.303
  209.9 18.4 %shard_map.305 = (bf16[1,512,1536]{2,1,0:T(8,128)(2,1)}, bf16[1,512,1536]{2,1,0:T(8,128)(2,1)}, f32[1,512,128]{2,1,0:T(8,128)}, bf16[8,2,208,1536]{3,2,1,0:T(8,1...) custom-call(s32[1]{0:T(128)} %bitcast.9.first_ref, ...), custom_call_target="tpu_custom_call" | custom-call | flops 6543114240 | bytes 19562496 | tf_op jit(solution)/shard_map/pallas_call | solution.py:544
  230.1 43.1 %collective-permute-done.13 = bf16[512,1536]{1,0:T(8,128)(2,1)S(1)} collective-permute-done((bf16[512,1536]{1,0:T(8,128)(2,1)}, bf16[512,1536]{1,0:T(8,128)(2,1)S(1)}, u32[]{:S(2)}, u32[]{:S(2)}) %collective-permute-start.13) | collective-permute-done | bytes 1572896 | tf_op jit(solution)/shard_map/ppermute | solution.py:82
  277.4 3.9 pad_maximum_fusion.4.tok_ref
  283.4 30.1 %shard_map.306 = (bf16[2,512,1536]{2,1,0:T(8,128)(2,1)}, bf16[2,512,1536]{2,1,0:T(8,128)(2,1)}, f32[2,512,128]{2,1,0:T(8,128)}, bf16[8,2,208,1536]{3,2,1,0:T(8,1...) custom-call(s32[1]{0:T(128)} %bitcast.9.first_ref, ...), custom_call_target="tpu_custom_call", output_to_operand_aliasing={{3}: (10, {}), {4}: (11, {}), {5}: (12, {}), {6}: (13, {}),... | custom-call | flops 13086228480 | bytes 39124992 | tf_op jit(solution)/shard_map/pallas_call | solution.py:544
  313.6 3.6 pad_maximum_fusion.1.cot_ref
  322.4 6.1 collective-permute-done.11
  328.5 3.9 pad_maximum_fusion.2.tok_ref
  334.6 30.1 %shard_map.307 = (bf16[2,512,1536]{2,1,0:T(8,128)(2,1)}, bf16[2,512,1536]{2,1,0:T(8,128)(2,1)}, f32[2,512,128]{2,1,0:T(8,128)}, bf16[8,2,208,1536]{3,2,1,0:T(8,1...) custom-call(s32[1]{0:T(128)} %bitcast.9.first_ref, ...), custom_call_target="tpu_custom_call", output_to_operand_aliasing={{3}: (10, {}), {4}: (11, {}), {5}: (12, {}), {6}: (13, {}),... | custom-call | flops 13086228480 | bytes 39124992 | tf_op jit(solution)/shard_map/pallas_call | solution.py:544
  366.4 3.8 slice_bitcast_fusion.1
  374.4 3.4 pad_maximum_fusion.tok_ref
  377.8 30.4 %shard_map.308 = (bf16[2,512,1536]{2,1,0:T(8,128)(2,1)}, bf16[2,512,1536]{2,1,0:T(8,128)(2,1)}, f32[2,512,128]{2,1,0:T(8,128)}, bf16[8,2,208,1536]{3,2,1,0:T(8,1...) custom-call(s32[1]{0:T(128)} %bitcast.9.first_ref, ...), custom_call_target="tpu_custom_call", output_to_operand_aliasing={{3}: (10, {}), {4}: (11, {}), {5}: (12, {}), {6}: (13, {}),... | custom-call | flops 13086228480 | bytes 39124992 | tf_op jit(solution)/shard_map/pallas_call | solution.py:544
  417.3 18.9 %shard_map.309 = (bf16[1,512,1536]{2,1,0:T(8,128)(2,1)}, bf16[1,512,1536]{2,1,0:T(8,128)(2,1)}, f32[1,512,128]{2,1,0:T(8,128)}, bf16[8,2,208,1536]{3,2,1,0:T(8,1...) custom-call(s32[1]{0:T(128)} %bitcast.9.first_ref, ...), custom_call_target="tpu_custom_call", output_to_operand_aliasing={{3}: (10, {}), {4}: (11, {}), {5}: (12, {}), {6}: (13, {}),... | custom-call | flops 6543114240 | bytes 19562496 | tf_op jit(solution)/shard_map/pallas_call | solution.py:544
  443.6 4.0 all-to-all-start
  451.4 9.8 %bitcast_convert_fusion.2 = bf16[2,1536,512]{2,1,0:T(8,128)(2,1)S(1)} fusion(bf16[8,2,208,1536]{3,2,1,0:T(8,128)(2,1)} %get-tuple-element.105, bf16[8,2,208,512]{3,2,1,0:T(8,128)(2,1)} %get-tuple-element.106), kind=kOutput, calls=%fused_computation.8 | convolution fusion | flops 5236064256 | bytes 16777216 | tf_op jit(solution)/shard_map/necd,necf->edf/dot_general | solution.py:720
  462.5 3.6 collective-permute-done.22
  472.4 9.4 %bitcast_convert_fusion.1 = bf16[2,1536,512]{2,1,0:T(8,128)(2,1)} fusion(bf16[8,2,208,1536]{3,2,1,0:T(8,128)(2,1)S(1)} %bitcast.179, bf16[8,2,208,512]{3,2,1,0:T(8,128)(2,1)} %get-tuple-element.107), kind=kOutput, calls=%fused_computation.7 | convolution fusion | flops 5236064256 | bytes 16777216 | tf_op jit(solution)/shard_map/necd,necf->edf/dot_general | solution.py:721
  484.6 16.8 %collective-permute-done.27 = bf16[512,1536]{1,0:T(8,128)(2,1)S(1)} collective-permute-done((bf16[512,1536]{1,0:T(8,128)(2,1)}, bf16[512,1536]{1,0:T(8,128)(2,1)S(1)}, u32[]{:S(2)}, u32[]{:S(2)}) %collective-permute-start.27) | collective-permute-done | bytes 1572896 | tf_op jit(solution)/shard_map/ppermute | solution.py:82
  504.2 4.1 fusion.16
  510.3 6.3 bitcast_convert_fusion
  525.1 3.1 add_convert_fusion.9.refs_1_
  529.5 11.4 %collective-permute-done.24 = bf16[512,1536]{1,0:T(8,128)(2,1)} collective-permute-done((bf16[512,1536]{1,0:T(8,128)(2,1)}, bf16[512,1536]{1,0:T(8,128)(2,1)}, u32[]{:S(2)}, u32[]{:S(2)}) %collective-permute-start.24) | collective-permute-done | bytes 1572896 | tf_op jit(solution)/shard_map/ppermute | solution.py:82
  540.9 4.6 fusion.17
  553.6 11.8 %collective-permute-done.38 = bf16[1,1536,512]{2,1,0:T(8,128)(2,1)} collective-permute-done((bf16[1,1536,512]{2,1,0:T(8,128)(2,1)}, bf16[1,1536,512]{2,1,0:T(8,128)(2,1)}, u32[]{:S(2)}, u32[]{:S(2)}) %collective-permute-start.38) | collective-permute-done | bytes 1572896 | tf_op jit(solution)/shard_map/ppermute | solution.py:77
  565.4 3.5 add_convert_fusion.2.refs_3_
  568.8 8.4 collective-permute-done.25
  577.2 3.2 multiply_reduce_fusion
  580.5 3.2 fusion.46
  587.4 29.3 %shard_map.312 = (bf16[512,1536]{1,0:T(8,128)(2,1)S(1)}, bf16[512,512]{1,0:T(8,128)(2,1)S(1)}, bf16[512,512]{1,0:T(8,128)(2,1)S(1)}) custom-call(s32[1]{0:T(128)} %copy.201.length_ref, bf16[512,1536]{1,0:T(8,128)(2,1)} %get-tuple-element.182.refs_8_.ga_ref.right_b_ref, bf16[1536,1536]{1,0:T(8,128)(2,1)} %all-gather.5.cloned.1.call-done.weight_ref.wo_ref, ...), custom_call_target="tpu_custom_call" | custom-call | flops 30000001024 | bytes 10000000 | tf_op jit(solution)/shard_map/pallas_call | solution.py:350
  622.6 11.7 %shard_map.314.refs_1_ = bf16[1536,4096]{1,0:T(8,128)(2,1)} custom-call(bf16[512,1536]{1,0:T(8,128)(2,1)S(1)} %copy-done.10, bf16[512,2560]{1,0:T(8,128)(2,1)} %shard_map.313.right_a_ref.refs_0_, bf16[512,1536]{1,0:T(8,128)(2,1)S(1)} %copy-done.6, bf16[512,1536]{1,0:T(8,128)(2,1)S(1)} %copy-done.4), custom_call_target="tpu_custom_call" | custom-call | flops 1000 | bytes 1000 | tf_op jit(solution)/shard_map/pallas_call | solution.py:427
  644.1 27.2 %collective-permute-done.35 = bf16[512,1536]{1,0:T(8,128)(2,1)S(1)} collective-permute-done((bf16[512,1536]{1,0:T(8,128)(2,1)S(1)}, bf16[512,1536]{1,0:T(8,128)(2,1)S(1)}, u32[]{:S(2)}, u32[]{:S(2)}) %collective-permute-start.35) | collective-permute-done | bytes 1572896 | tf_op jit(solution)/shard_map/ppermute | solution.py:82
  676.8 11.2 %fusion.5 = (bf16[1536]{0:T(1024)(128)(2,1)S(1)}, f32[512]{0:T(512)S(1)}, f32[512,1536]{1,0:T(8,128)}) fusion(f32[512]{0:T(512)S(1)} %copy-done.72, bf16[1,512,1536]{2,1,0:T(8,128)(2,1)} %param.22, f32[1536]{0:T(1024)S(1)} %copy-done.66, bf16[512,2560]{1,0:T(8,128)(2,1)} %shard_map.315, bf16[1536,2688]{1,0:T(8,128)(2,1)} %all-gather.3.cloned.1.call-done.wq_ref.wk_ref.wv_ref), kind=kOutput, calls=%fused_computation.18 | convolution fusion | flops 4032034816 | bytes 15217664 | tf_op jit(solution)/shard_map/sa,da->sd/dot_general | solution.py:762
  688.6 48.1 %collective-permute-done.36 = bf16[512,1536]{1,0:T(8,128)(2,1)} collective-permute-done((bf16[512,1536]{1,0:T(8,128)(2,1)}, bf16[512,1536]{1,0:T(8,128)(2,1)}, u32[]{:S(2)}, u32[]{:S(2)}) %collective-permute-start.36) | collective-permute-done | bytes 1572896 | tf_op jit(solution)/shard_map/ppermute | solution.py:82
  744.4 3.2 collective-permute-done.39
  748.8 4.0 collective-permute-done.40
  754.3 5.8 fusion.11
  763.6 5.4 fusion.19
  771.1 53.4 %collective-permute-done.43 = bf16[18,1536]{1,0:T(8,128)(2,1)S(1)} collective-permute-done((bf16[18,1536]{1,0:T(8,128)(2,1)S(1)}, bf16[18,1536]{1,0:T(8,128)(2,1)S(1)}, u32[]{:S(2)}, u32[]{:S(2)}) %collective-permute-start.43) | collective-permute-done | bytes 55328 | tf_op jit(solution)/shard_map/ppermute | solution.py:77
  836.4 8.5 all_gather.15
  846.9 8.7 %all_gather.14 = bf16[192,2048]{1,0:T(8,128)(2,1)S(1)} all-gather(bf16[48,2048]{1,0:T(8,128)(2,1)S(1)} %get-tuple-element.204), channel_id=1, replica_groups=mesh['rep'=4,'fsdp'=8] {'rep'}, dimensions={0}, use_global_device_ids=true | all-gather | bytes 983040 | tf_op jit(solution)/shard_map/all_gather | solution.py:746
  (398 shorter events, 202.6 us)
Async XLA Ops:
  7.2 140.2 %all-gather.3.cloned.1.call-start = ((), (), s32[]{:S(2)}) async-start(), calls=%async_computation.2 | async-start | bytes 8515584 | tf_op jit(solution)/shard_map/all_gather | solution.py:643
  14.6 175.7 %all-gather.5.cloned.1.call-start = ((), (), s32[]{:S(2)}) async-start(), calls=%async_computation.3 | async-start | bytes 4866048 | tf_op jit(solution)/shard_map/all_gather | solution.py:643
  16.3 4.9 collective-permute-start
  25.7 10.7 %collective-permute-start.2 = (s32[4,16,512]{2,1,0:T(8,128)S(1)}, s32[4,16,512]{2,1,0:T(8,128)S(1)}, u32[]{:S(2)}, u32[]{:S(2)}) collective-permute-start(s32[4,16,512]{2,1,0:T(8,128)S(1)} %add_select_fusion), channel_id=1, source_target_pairs={{0,4},{1,5},{2,6},{3,7},{4,0},{5,1},{6,2},{7,3},{8,12},{9,13},{10,... | collective-permute-start | bytes 393224 | tf_op jit(solution)/shard_map/ppermute | solution.py:77
  37.4 57.2 %collective-permute-start.4 = (bf16[512,1536]{1,0:T(8,128)(2,1)}, bf16[512,1536]{1,0:T(8,128)(2,1)}, u32[]{:S(2)}, u32[]{:S(2)}) collective-permute-start(bf16[512,1536]{1,0:T(8,128)(2,1)} %shard_map.302), channel_id=1, source_target_pairs={{0,2},{2,4},{4,6},{6,7},{7,5},{5,3},{3,1},{1,0},{8,10},{10,12},{12... | collective-permute-start | bytes 4718600 | tf_op jit(solution)/shard_map/ppermute | solution.py:82
  39.9 63.7 %collective-permute-start.3 = (bf16[512,1536]{1,0:T(8,128)(2,1)}, bf16[512,1536]{1,0:T(8,128)(2,1)}, u32[]{:S(2)}, u32[]{:S(2)}) collective-permute-start(bf16[512,1536]{1,0:T(8,128)(2,1)} %shard_map.302), channel_id=1, source_target_pairs={{0,1},{2,0},{4,2},{6,4},{7,6},{5,7},{3,5},{1,3},{8,9},{10,8},{12,1... | collective-permute-start | bytes 4718600 | tf_op jit(solution)/shard_map/ppermute | solution.py:82
  94.7 47.0 %collective-permute-start.6 = (bf16[512,1536]{1,0:T(8,128)(2,1)}, bf16[512,1536]{1,0:T(8,128)(2,1)S(1)}, u32[]{:S(2)}, u32[]{:S(2)}) collective-permute-start(bf16[512,1536]{1,0:T(8,128)(2,1)} %collective-permute-done.4.rest_1_), channel_id=1, source_target_pairs={{0,2},{2,4},{4,6},{6,7},{7,5},{5,3},{3,1},{1,0},{8,10},{10,12},{12... | collective-permute-start | bytes 4718600 | tf_op jit(solution)/shard_map/ppermute | solution.py:82
  103.6 40.5 %collective-permute-start.5 = (bf16[512,1536]{1,0:T(8,128)(2,1)}, bf16[512,1536]{1,0:T(8,128)(2,1)}, u32[]{:S(2)}, u32[]{:S(2)}) collective-permute-start(bf16[512,1536]{1,0:T(8,128)(2,1)} %collective-permute-done.3.rest_0_), channel_id=1, source_target_pairs={{0,1},{2,0},{4,2},{6,4},{7,6},{5,7},{3,5},{1,3},{8,9},{10,8},{12,1... | collective-permute-start | bytes 4718600 | tf_op jit(solution)/shard_map/ppermute | solution.py:82
  201.3 76.0 %collective-permute-start.10 = (bf16[512,1536]{1,0:T(8,128)(2,1)}, bf16[512,1536]{1,0:T(8,128)(2,1)}, u32[]{:S(2)}, u32[]{:S(2)}) collective-permute-start(bf16[512,1536]{1,0:T(8,128)(2,1)} %get-tuple-element.76), channel_id=1, source_target_pairs={{0,1},{2,0},{4,2},{6,4},{7,6},{5,7},{3,5},{1,3},{8,9},{10,8},{12,1... | collective-permute-start | bytes 4718600 | tf_op jit(solution)/shard_map/ppermute | solution.py:82
  202.8 74.6 %collective-permute-start.7 = (bf16[512,1536]{1,0:T(8,128)(2,1)}, bf16[512,1536]{1,0:T(8,128)(2,1)}, u32[]{:S(2)}, u32[]{:S(2)}) collective-permute-start(bf16[512,1536]{1,0:T(8,128)(2,1)} %get-tuple-element.76), channel_id=1, source_target_pairs={{0,2},{2,4},{4,6},{6,7},{7,5},{5,3},{3,1},{1,0},{8,10},{10,12},{12... | collective-permute-start | bytes 4718600 | tf_op jit(solution)/shard_map/ppermute | solution.py:82
  203.3 69.8 %collective-permute-start.13 = (bf16[512,1536]{1,0:T(8,128)(2,1)}, bf16[512,1536]{1,0:T(8,128)(2,1)S(1)}, u32[]{:S(2)}, u32[]{:S(2)}) collective-permute-start(bf16[512,1536]{1,0:T(8,128)(2,1)} %get-tuple-element.77), channel_id=1, source_target_pairs={{0,2},{2,4},{4,6},{6,7},{7,5},{5,3},{3,1},{1,0},{8,10},{10,12},{12... | collective-permute-start | bytes 4718600 | tf_op jit(solution)/shard_map/ppermute | solution.py:82
  205.2 68.6 %collective-permute-start.14 = (bf16[512,1536]{1,0:T(8,128)(2,1)}, bf16[512,1536]{1,0:T(8,128)(2,1)}, u32[]{:S(2)}, u32[]{:S(2)}) collective-permute-start(bf16[512,1536]{1,0:T(8,128)(2,1)} %get-tuple-element.78), channel_id=1, source_target_pairs={{0,1},{2,0},{4,2},{6,4},{7,6},{5,7},{3,5},{1,3},{8,9},{10,8},{12,1... | collective-permute-start | bytes 4718600 | tf_op jit(solution)/shard_map/ppermute | solution.py:82
  273.2 46.5 %collective-permute-start.17 = (bf16[256,1536]{1,0:T(8,128)(2,1)S(1)}, bf16[256,1536]{1,0:T(8,128)(2,1)}, u32[]{:S(2)}, u32[]{:S(2)}) collective-permute-start(bf16[256,1536]{1,0:T(8,128)(2,1)S(1)} %slice.238), channel_id=1, source_target_pairs={{0,2},{2,4},{4,6},{6,7},{7,5},{5,3},{3,1},{1,0},{8,10},{10,12},{12... | collective-permute-start | bytes 2359304 | tf_op jit(solution)/shard_map/ppermute | solution.py:82
  275.9 43.9 %collective-permute-start.18 = (bf16[256,1536]{1,0:T(8,128)(2,1)}, bf16[256,1536]{1,0:T(8,128)(2,1)}, u32[]{:S(2)}, u32[]{:S(2)}) collective-permute-start(bf16[256,1536]{1,0:T(8,128)(2,1)} %slice.239), channel_id=1, source_target_pairs={{0,1},{2,0},{4,2},{6,4},{7,6},{5,7},{3,5},{1,3},{8,9},{10,8},{12,1... | collective-permute-start | bytes 2359304 | tf_op jit(solution)/shard_map/ppermute | solution.py:82
  281.2 47.2 %collective-permute-start.11 = (bf16[512,1536]{1,0:T(8,128)(2,1)}, bf16[512,1536]{1,0:T(8,128)(2,1)}, u32[]{:S(2)}, u32[]{:S(2)}) collective-permute-start(bf16[512,1536]{1,0:T(8,128)(2,1)} %collective-permute-done.10), channel_id=1, source_target_pairs={{0,1},{2,0},{4,2},{6,4},{7,6},{5,7},{3,5},{1,3},{8,9},{10,8},{12,1... | collective-permute-start | bytes 4718600 | tf_op jit(solution)/shard_map/ppermute | solution.py:82
  282.9 45.5 %collective-permute-start.8 = (bf16[512,1536]{1,0:T(8,128)(2,1)}, bf16[512,1536]{1,0:T(8,128)(2,1)}, u32[]{:S(2)}, u32[]{:S(2)}) collective-permute-start(bf16[512,1536]{1,0:T(8,128)(2,1)} %collective-permute-done.7), channel_id=1, source_target_pairs={{0,2},{2,4},{4,6},{6,7},{7,5},{5,3},{3,1},{1,0},{8,10},{10,12},{12... | collective-permute-start | bytes 4718600 | tf_op jit(solution)/shard_map/ppermute | solution.py:82
  332.4 37.8 %collective-permute-start.12 = (bf16[512,1536]{1,0:T(8,128)(2,1)}, bf16[512,1536]{1,0:T(8,128)(2,1)S(1)}, u32[]{:S(2)}, u32[]{:S(2)}) collective-permute-start(bf16[512,1536]{1,0:T(8,128)(2,1)} %collective-permute-done.11), channel_id=1, source_target_pairs={{0,1},{2,0},{4,2},{6,4},{7,6},{5,7},{3,5},{1,3},{8,9},{10,8},{12,1... | collective-permute-start | bytes 4718600 | tf_op jit(solution)/shard_map/ppermute | solution.py:82
  333.8 37.9 %collective-permute-start.9 = (bf16[512,1536]{1,0:T(8,128)(2,1)}, bf16[512,1536]{1,0:T(8,128)(2,1)}, u32[]{:S(2)}, u32[]{:S(2)}) collective-permute-start(bf16[512,1536]{1,0:T(8,128)(2,1)} %collective-permute-done.8), channel_id=1, source_target_pairs={{0,2},{2,4},{4,6},{6,7},{7,5},{5,3},{3,1},{1,0},{8,10},{10,12},{12... | collective-permute-start | bytes 4718600 | tf_op jit(solution)/shard_map/ppermute | solution.py:82
  370.2 44.4 %collective-permute-start.16 = (bf16[256,1536]{1,0:T(8,128)(2,1)S(1)}, bf16[256,1536]{1,0:T(8,128)(2,1)}, u32[]{:S(2)}, u32[]{:S(2)}) collective-permute-start(bf16[256,1536]{1,0:T(8,128)(2,1)S(1)} %slice.237), channel_id=1, source_target_pairs={{0,1},{2,0},{4,2},{6,4},{7,6},{5,7},{3,5},{1,3},{8,9},{10,8},{12,1... | collective-permute-start | bytes 2359304 | tf_op jit(solution)/shard_map/ppermute | solution.py:82
  373.8 40.9 %collective-permute-start.15 = (bf16[256,1536]{1,0:T(8,128)(2,1)}, bf16[256,1536]{1,0:T(8,128)(2,1)}, u32[]{:S(2)}, u32[]{:S(2)}) collective-permute-start(bf16[256,1536]{1,0:T(8,128)(2,1)} %slice.236), channel_id=1, source_target_pairs={{0,2},{2,4},{4,6},{6,7},{7,5},{5,3},{3,1},{1,0},{8,10},{10,12},{12... | collective-permute-start | bytes 2359304 | tf_op jit(solution)/shard_map/ppermute | solution.py:82
  443.6 76.0 %all-to-all-start = ((f32[8,2,512]{2,1,0:T(2,128)}), f32[8,2,512]{2,1,0:T(2,128)}, u32[]{:S(2)}, u32[]{:S(2)}) async-start(f32[8,2,512]{2,1,0:T(2,128)} %gather_fusion.3), calls=%async_computation | async-start | bytes 65536 | tf_op jit(solution)/shard_map/all_to_all | solution.py:716
  447.6 387.8 %reduce-scatter.2.cloned.1.call-start = ((), (), s32[]{:S(2)}) async-start(), calls=%async_computation.4 | async-start | bytes 12976128 | tf_op jit(solution)/shard_map/reduce_scatter | solution.py:745
  449.3 16.8 %collective-permute-start.22 = (bf16[256,1536]{1,0:T(8,128)(2,1)S(1)}, bf16[256,1536]{1,0:T(8,128)(2,1)S(1)}, u32[]{:S(2)}, u32[]{:S(2)}) collective-permute-start(bf16[256,1536]{1,0:T(8,128)(2,1)S(1)} %get-tuple-element.201), channel_id=1, source_target_pairs={{0,2},{2,4},{4,6},{6,7},{7,5},{5,3},{3,1},{1,0},{8,10},{10,12},{12... | collective-permute-start | bytes 2359304 | tf_op jit(solution)/shard_map/ppermute | solution.py:82
  451.3 16.1 %collective-permute-start.26 = (bf16[256,1536]{1,0:T(8,128)(2,1)S(1)}, bf16[256,1536]{1,0:T(8,128)(2,1)S(1)}, u32[]{:S(2)}, u32[]{:S(2)}) collective-permute-start(bf16[256,1536]{1,0:T(8,128)(2,1)S(1)} %get-tuple-element.202), channel_id=1, source_target_pairs={{0,1},{2,0},{4,2},{6,4},{7,6},{5,7},{3,5},{1,3},{8,9},{10,8},{12,1... | collective-permute-start | bytes 2359304 | tf_op jit(solution)/shard_map/ppermute | solution.py:82
  462.5 62.6 %collective-permute-start.19 = (bf16[1,1536,512]{2,1,0:T(8,128)(2,1)}, bf16[1,1536,512]{2,1,0:T(8,128)(2,1)}, u32[]{:S(2)}, u32[]{:S(2)}) collective-permute-start(bf16[1,1536,512]{2,1,0:T(8,128)(2,1)} %constant_dynamic-slice_fusion.2), channel_id=1, source_target_pairs={{0,8},{8,0},{16,24},{24,16},{1,9},{9,1},{17,25},{25,17},{2,10},{10... | collective-permute-start | bytes 4718600 | tf_op jit(solution)/shard_map/ppermute | solution.py:77
  469.0 32.3 %collective-permute-start.27 = (bf16[512,1536]{1,0:T(8,128)(2,1)}, bf16[512,1536]{1,0:T(8,128)(2,1)S(1)}, u32[]{:S(2)}, u32[]{:S(2)}) collective-permute-start(bf16[512,1536]{1,0:T(8,128)(2,1)} %pad_maximum_fusion.8), channel_id=1, source_target_pairs={{0,1},{2,0},{4,2},{6,4},{7,6},{5,7},{3,5},{1,3},{8,9},{10,8},{12,1... | collective-permute-start | bytes 4718600 | tf_op jit(solution)/shard_map/ppermute | solution.py:82
  470.7 33.5 %collective-permute-start.23 = (bf16[512,1536]{1,0:T(8,128)(2,1)}, bf16[512,1536]{1,0:T(8,128)(2,1)}, u32[]{:S(2)}, u32[]{:S(2)}) collective-permute-start(bf16[512,1536]{1,0:T(8,128)(2,1)} %pad_maximum_fusion.7), channel_id=1, source_target_pairs={{0,2},{2,4},{4,6},{6,7},{7,5},{5,3},{3,1},{1,0},{8,10},{10,12},{12... | collective-permute-start | bytes 4718600 | tf_op jit(solution)/shard_map/ppermute | solution.py:82
  484.6 62.9 %collective-permute-start.20 = (bf16[1,1536,512]{2,1,0:T(8,128)(2,1)}, bf16[1,1536,512]{2,1,0:T(8,128)(2,1)}, u32[]{:S(2)}, u32[]{:S(2)}) collective-permute-start(bf16[1,1536,512]{2,1,0:T(8,128)(2,1)} %constant_dynamic-slice_fusion.1), channel_id=1, source_target_pairs={{0,8},{8,0},{16,24},{24,16},{1,9},{9,1},{17,25},{25,17},{2,10},{10... | collective-permute-start | bytes 4718600 | tf_op jit(solution)/shard_map/ppermute | solution.py:77
  508.3 32.6 %collective-permute-start.24 = (bf16[512,1536]{1,0:T(8,128)(2,1)}, bf16[512,1536]{1,0:T(8,128)(2,1)}, u32[]{:S(2)}, u32[]{:S(2)}) collective-permute-start(bf16[512,1536]{1,0:T(8,128)(2,1)} %get-tuple-element.187), channel_id=1, source_target_pairs={{0,2},{2,4},{4,6},{6,7},{7,5},{5,3},{3,1},{1,0},{8,10},{10,12},{12... | collective-permute-start | bytes 4718600 | tf_op jit(solution)/shard_map/ppermute | solution.py:82
  508.6 32.3 %collective-permute-start.28 = (bf16[512,1536]{1,0:T(8,128)(2,1)}, bf16[512,1536]{1,0:T(8,128)(2,1)}, u32[]{:S(2)}, u32[]{:S(2)}) collective-permute-start(bf16[512,1536]{1,0:T(8,128)(2,1)} %get-tuple-element.188), channel_id=1, source_target_pairs={{0,1},{2,0},{4,2},{6,4},{7,6},{5,7},{3,5},{1,3},{8,9},{10,8},{12,1... | collective-permute-start | bytes 4718600 | tf_op jit(solution)/shard_map/ppermute | solution.py:82
  519.6 31.0 %collective-permute-start.21 = (bf16[1,512,1536]{2,1,0:T(8,128)(2,1)}, bf16[1,512,1536]{2,1,0:T(8,128)(2,1)}, u32[]{:S(2)}, u32[]{:S(2)}) collective-permute-start(bf16[1,512,1536]{2,1,0:T(8,128)(2,1)} %constant_dynamic-slice_fusion), channel_id=1, source_target_pairs={{0,8},{8,0},{16,24},{24,16},{1,9},{9,1},{17,25},{25,17},{2,10},{10... | collective-permute-start | bytes 4718600 | tf_op jit(solution)/shard_map/ppermute | solution.py:77
  528.2 37.1 %collective-permute-start.38 = (bf16[1,1536,512]{2,1,0:T(8,128)(2,1)}, bf16[1,1536,512]{2,1,0:T(8,128)(2,1)}, u32[]{:S(2)}, u32[]{:S(2)}) collective-permute-start(bf16[1,1536,512]{2,1,0:T(8,128)(2,1)} %add_convert_fusion.9.refs_1_), channel_id=1, source_target_pairs={{0,16},{8,24},{16,0},{24,8},{1,17},{9,25},{17,1},{25,9},{2,18},{10... | collective-permute-start | bytes 4718600 | tf_op jit(solution)/shard_map/ppermute | solution.py:77
  545.5 31.7 %collective-permute-start.25 = (bf16[512,1536]{1,0:T(8,128)(2,1)}, bf16[512,1536]{1,0:T(8,128)(2,1)}, u32[]{:S(2)}, u32[]{:S(2)}) collective-permute-start(bf16[512,1536]{1,0:T(8,128)(2,1)} %get-tuple-element.185), channel_id=1, source_target_pairs={{0,2},{2,4},{4,6},{6,7},{7,5},{5,3},{3,1},{1,0},{8,10},{10,12},{12... | collective-permute-start | bytes 4718600 | tf_op jit(solution)/shard_map/ppermute | solution.py:82
  546.1 31.1 %collective-permute-start.29 = (bf16[512,1536]{1,0:T(8,128)(2,1)}, bf16[512,1536]{1,0:T(8,128)(2,1)}, u32[]{:S(2)}, u32[]{:S(2)}) collective-permute-start(bf16[512,1536]{1,0:T(8,128)(2,1)} %get-tuple-element.186), channel_id=1, source_target_pairs={{0,1},{2,0},{4,2},{6,4},{7,6},{5,7},{3,5},{1,3},{8,9},{10,8},{12,1... | collective-permute-start | bytes 4718600 | tf_op jit(solution)/shard_map/ppermute | solution.py:82
  585.3 33.1 %collective-permute-start.30 = (bf16[256,1536]{1,0:T(8,128)(2,1)S(1)}, bf16[256,1536]{1,0:T(8,128)(2,1)}, u32[]{:S(2)}, u32[]{:S(2)}) collective-permute-start(bf16[256,1536]{1,0:T(8,128)(2,1)S(1)} %get-tuple-element.199), channel_id=1, source_target_pairs={{0,2},{2,4},{4,6},{6,7},{7,5},{5,3},{3,1},{1,0},{8,10},{10,12},{12... | collective-permute-start | bytes 2359304 | tf_op jit(solution)/shard_map/ppermute | solution.py:82
  586.8 31.6 %collective-permute-start.34 = (bf16[256,1536]{1,0:T(8,128)(2,1)S(1)}, bf16[256,1536]{1,0:T(8,128)(2,1)}, u32[]{:S(2)}, u32[]{:S(2)}) collective-permute-start(bf16[256,1536]{1,0:T(8,128)(2,1)S(1)} %get-tuple-element.200), channel_id=1, source_target_pairs={{0,1},{2,0},{4,2},{6,4},{7,6},{5,7},{3,5},{1,3},{8,9},{10,8},{12,1... | collective-permute-start | bytes 2359304 | tf_op jit(solution)/shard_map/ppermute | solution.py:82
  638.4 32.9 %collective-permute-start.35 = (bf16[512,1536]{1,0:T(8,128)(2,1)S(1)}, bf16[512,1536]{1,0:T(8,128)(2,1)S(1)}, u32[]{:S(2)}, u32[]{:S(2)}) collective-permute-start(bf16[512,1536]{1,0:T(8,128)(2,1)S(1)} %pad_maximum_fusion.10), channel_id=1, source_target_pairs={{0,1},{2,0},{4,2},{6,4},{7,6},{5,7},{3,5},{1,3},{8,9},{10,8},{12,1... | collective-permute-start | bytes 4718600 | tf_op jit(solution)/shard_map/ppermute | solution.py:82
  641.7 32.9 %collective-permute-start.31 = (bf16[512,1536]{1,0:T(8,128)(2,1)S(1)}, bf16[512,1536]{1,0:T(8,128)(2,1)S(1)}, u32[]{:S(2)}, u32[]{:S(2)}) collective-permute-start(bf16[512,1536]{1,0:T(8,128)(2,1)S(1)} %pad_maximum_fusion.9), channel_id=1, source_target_pairs={{0,2},{2,4},{4,6},{6,7},{7,5},{5,3},{3,1},{1,0},{8,10},{10,12},{12... | collective-permute-start | bytes 4718600 | tf_op jit(solution)/shard_map/ppermute | solution.py:82
  644.1 110.3 %collective-permute-start.44 = (bf16[1,1536,512]{2,1,0:T(8,128)(2,1)}, bf16[1,1536,512]{2,1,0:T(8,128)(2,1)}, u32[]{:S(2)}, u32[]{:S(2)}) collective-permute-start(bf16[1,1536,512]{2,1,0:T(8,128)(2,1)} %add_convert_fusion.2.refs_3_), channel_id=1, source_target_pairs={{0,8},{8,0},{16,24},{24,16},{1,9},{9,1},{17,25},{25,17},{2,10},{10... | collective-permute-start | bytes 4718600 | tf_op jit(solution)/shard_map/ppermute | solution.py:77
  672.8 63.9 %collective-permute-start.36 = (bf16[512,1536]{1,0:T(8,128)(2,1)}, bf16[512,1536]{1,0:T(8,128)(2,1)}, u32[]{:S(2)}, u32[]{:S(2)}) collective-permute-start(bf16[512,1536]{1,0:T(8,128)(2,1)} %add_convert_fusion.4.refs_3_), channel_id=1, source_target_pairs={{0,1},{2,0},{4,2},{6,4},{7,6},{5,7},{3,5},{1,3},{8,9},{10,8},{12,1... | collective-permute-start | bytes 4718600 | tf_op jit(solution)/shard_map/ppermute | solution.py:82
  676.1 63.8 %collective-permute-start.32 = (bf16[512,1536]{1,0:T(8,128)(2,1)}, bf16[512,1536]{1,0:T(8,128)(2,1)}, u32[]{:S(2)}, u32[]{:S(2)}) collective-permute-start(bf16[512,1536]{1,0:T(8,128)(2,1)} %add_convert_fusion.6.refs_2_), channel_id=1, source_target_pairs={{0,2},{2,4},{4,6},{6,7},{7,5},{5,3},{3,1},{1,0},{8,10},{10,12},{12... | collective-permute-start | bytes 4718600 | tf_op jit(solution)/shard_map/ppermute | solution.py:82
  752.9 8.2 collective-permute-start.41
  760.2 64.4 %collective-permute-start.47 = (bf16[1,512,1536]{2,1,0:T(8,128)(2,1)}, bf16[1,512,1536]{2,1,0:T(8,128)(2,1)S(1)}, u32[]{:S(2)}, u32[]{:S(2)}) collective-permute-start(bf16[1,512,1536]{2,1,0:T(8,128)(2,1)} %get-tuple-element.135), channel_id=1, source_target_pairs={{0,16},{8,24},{16,0},{24,8},{1,17},{9,25},{17,1},{25,9},{2,18},{10... | collective-permute-start | bytes 4718600 | tf_op jit(solution)/shard_map/ppermute | solution.py:77
  761.2 63.9 %collective-permute-start.45 = (bf16[1,1536,512]{2,1,0:T(8,128)(2,1)}, bf16[1,1536,512]{2,1,0:T(8,128)(2,1)S(1)}, u32[]{:S(2)}, u32[]{:S(2)}) collective-permute-start(bf16[1,1536,512]{2,1,0:T(8,128)(2,1)} %get-tuple-element.134), channel_id=1, source_target_pairs={{0,16},{8,24},{16,0},{24,8},{1,17},{9,25},{17,1},{25,9},{2,18},{10... | collective-permute-start | bytes 4718600 | tf_op jit(solution)/shard_map/ppermute | solution.py:77
  762.5 62.0 %collective-permute-start.43 = (bf16[18,1536]{1,0:T(8,128)(2,1)S(1)}, bf16[18,1536]{1,0:T(8,128)(2,1)S(1)}, u32[]{:S(2)}, u32[]{:S(2)}) collective-permute-start(bf16[18,1536]{1,0:T(8,128)(2,1)S(1)} %add_convert_fusion.12), channel_id=1, source_target_pairs={{0,16},{8,24},{16,0},{24,8},{1,17},{9,25},{17,1},{25,9},{2,18},{10... | collective-permute-start | bytes 165896 | tf_op jit(solution)/shard_map/ppermute | solution.py:77
  769.1 58.2 %collective-permute-start.37 = (bf16[512,1536]{1,0:T(8,128)(2,1)S(1)}, bf16[512,1536]{1,0:T(8,128)(2,1)S(1)}, u32[]{:S(2)}, u32[]{:S(2)}) collective-permute-start(bf16[512,1536]{1,0:T(8,128)(2,1)S(1)} %copy-done.36), channel_id=1, source_target_pairs={{0,1},{2,0},{4,2},{6,4},{7,6},{5,7},{3,5},{1,3},{8,9},{10,8},{12,1... | collective-permute-start | bytes 4718600 | tf_op jit(solution)/shard_map/ppermute | solution.py:82
  770.7 56.6 %collective-permute-start.33 = (bf16[512,1536]{1,0:T(8,128)(2,1)S(1)}, bf16[512,1536]{1,0:T(8,128)(2,1)S(1)}, u32[]{:S(2)}, u32[]{:S(2)}) collective-permute-start(bf16[512,1536]{1,0:T(8,128)(2,1)S(1)} %copy-done.37), channel_id=1, source_target_pairs={{0,2},{2,4},{4,6},{6,7},{7,5},{5,3},{3,1},{1,0},{8,10},{10,12},{12... | collective-permute-start | bytes 4718600 | tf_op jit(solution)/shard_map/ppermute | solution.py:82
  825.5 6.8 collective-permute-start.46
  (95 other events, 2443.5 us)
Sparse Core Ops, SparseCore 0:
  14.7 103.2 all-gather.2
  121.4 68.7 all-gather.4
  634.4 191.1 reduce-scatter.1
